TPU v7x, 32 devices: a whole 2x2x4 slice. The times are simulated.
32 devices in a mesh: rep: 8 (over z, y), grp: 4 (over x, core).
Axes of the slice: x: 2, y: 2, z: 4, core: 2. Of those that a mesh axis runs over, the one named last changes fastest.
Arguments:
- tokens: bfloat16 [8, 2048, 768], P('rep', 'grp'), may hold values from -6 to 6
- prev_logits: float32 [8, 2048, 12], P('rep', 'grp'), may hold values from -6 to 6
- routes: int32 [8, 2048, 2], P('rep', 'grp'), may hold values from 0 to 11, all different within a row; in each aligned block of 512 rows (0 to 511, 512 to 1023, ..., all dimensions but the last counted through in order) at most 128 rows name the same one
- branch_points: int32 [8, 2], P('rep'), may hold values from 1 to 1024, as said below
- cotangent: bfloat16 [8, 2048, 768], P('rep', 'grp'), may hold values from -6 to 6
- attn_gain: bfloat16 [768], replicated, may hold values from 0.5 to 1.5
- qkv_weight: bfloat16 [768, 2304], P('grp'), may hold values from -0.21875 to 0.21875
- out_weight: bfloat16 [768, 768], P('grp'), may hold values from -0.875 to 0.875
- ffn_gain: bfloat16 [768], replicated, may hold values from 0.5 to 1.5
- router_weight: bfloat16 [768, 12], replicated, may hold values from -0.109375 to 0.109375
- resid_weight: bfloat16 [12, 12], replicated, may hold values from -0.875 to 0.875
- const_weight: bfloat16 [2, 768, 2], replicated, may hold values from -0.21875 to 0.21875
- const_vector: bfloat16 [2, 768], replicated, may hold values from -6 to 6
- gate_weight: bfloat16 [768, 16384], P(None, 'grp'), may hold values from -0.21875 to 0.21875
- up_weight: bfloat16 [768, 16384], P(None, 'grp'), may hold values from -0.21875 to 0.21875
- down_weight: bfloat16 [16384, 768], P('grp'), may hold values from -0.375 to 0.375
Outputs:
- layer_output: float32 [8, 2048, 768], P('rep', 'grp')
- input_grad: float32 [8, 2048, 768], P('rep', 'grp')
- prev_grad: float32 [8, 2048, 12], P('rep', 'grp')
- gains_grad: float32 [2, 768], replicated
- qkv_grad: float32 [768, 2304], P('grp')
- projection_grad: float32 [768, 768], P('grp')
- router_grad: float32 [768, 12], replicated
- resid_grad: float32 [12, 12], replicated
- const_grad: float32 [2, 768, 2], replicated
- vector_grad: float32 [2, 768], replicated
- gate_grad: float32 [768, 16384], P(None, 'grp')
- up_grad: float32 [768, 16384], P(None, 'grp')
- down_grad: float32 [16384, 768], P('grp')
Inputs may be any that keep to these rules, and one draw needn't show every extreme that they name: `routes`: each row names 2 different ids: 0 to 7 are feed-forward experts, 8 the zero expert, 9 the copy expert, 10 and 11 the constant experts. Among the rows of one device no id is named by more than 128 rows. `branch_points`: each group has one continuation that follows the whole prompt.
All inputs are finite; a program needn't handle non-finite values.
Results may differ from a plain program's by a relative error of at most 0.023.
Values may be sent and summed in bfloat16 or wider, within the bound.
No kernel may reach another device: no remote copies, remote signals or barrier semaphores. Data moves between devices by JAX's collectives and lax.ppermute only.
A program may use at most 256 MiB of HBM per device.

v0:
```python
from functools import partial
import math

import jax
import jax.numpy as jnp
import numpy as np
from jax import lax
from jax.sharding import PartitionSpec as P

D = 768
HEADS = 12
HEAD_DIM = 64
EXPERTS = 8
TOP = 2
P_DEV = 256
TOK_DEV = 512
CAP = 128


NORM_EPS = 1e-06
MASKED = -1e30
HIGHEST = lax.Precision.HIGHEST


def from_partner(value, axis, distance):
    mask = 2**distance
    pairs = [(source, source ^ mask) for source in range(lax.axis_size(axis))]
    return lax.ppermute(value, axis, pairs)


def rms_norm(values, gain):
    return values * lax.rsqrt(jnp.mean(values * values, axis=-1, keepdims=True) + NORM_EPS) * gain


def softmax_rows(logits):
    shifted = logits - jnp.max(logits, axis=-1, keepdims=True)
    weights = jnp.exp(shifted)
    return weights / jnp.sum(weights, axis=-1, keepdims=True)


def split_heads(matrix):
    return matrix.reshape(matrix.shape[0], HEADS, HEAD_DIM)


def score_block(query_heads, key_heads, allowed):
    scores = jnp.einsum(
        "qhd,khd->hqk", query_heads, key_heads, preferred_element_type=jnp.float32
    ) * (1.0 / math.sqrt(HEAD_DIM))
    return jnp.where(allowed[None], scores, MASKED)


def forward_block(running, query_heads, key_heads, value_heads, allowed):
    run_max, run_sum, run_acc = running
    scores = score_block(query_heads, key_heads, allowed)
    new_max = jnp.maximum(run_max, jnp.max(scores, axis=2))
    weights = jnp.where(allowed[None], jnp.exp(scores - new_max[:, :, None]), 0.0)
    rescale = jnp.exp(run_max - new_max)
    new_sum = run_sum * rescale + jnp.sum(weights, axis=2)
    mixed_part = jnp.einsum(
        "hqk,khd->qhd",
        weights.astype(jnp.bfloat16),
        value_heads,
        preferred_element_type=jnp.float32,
    )
    new_acc = run_acc * jnp.transpose(rescale)[:, :, None] + mixed_part
    return (new_max, new_sum, new_acc)


def backward_block(query_heads, grad_heads, log_total, delta_rows, key_heads, value_heads, allowed):
    scores = score_block(query_heads, key_heads, allowed)
    weights = jnp.where(allowed[None], jnp.exp(scores - log_total[:, :, None]), 0.0)
    prob_grad = jnp.einsum(
        "qhd,khd->hqk", grad_heads, value_heads, preferred_element_type=jnp.float32
    )
    score_grad = (weights * (prob_grad - delta_rows[:, :, None])).astype(jnp.bfloat16)
    factor = 1.0 / math.sqrt(HEAD_DIM)
    query_add = (
        jnp.einsum("hqk,khd->qhd", score_grad, key_heads, preferred_element_type=jnp.float32)
        * factor
    )
    key_grad = (
        jnp.einsum("hqk,qhd->khd", score_grad, query_heads, preferred_element_type=jnp.float32)
        * factor
    )
    value_grad = jnp.einsum(
        "hqk,qhd->khd", weights.astype(jnp.bfloat16), grad_heads, preferred_element_type=jnp.float32
    )
    return (query_add, key_grad, value_grad)


def mixer_terms(route_rows, hidden_in, hidden_wide, router_w, resid_w, const_w, const_v, previous):
    logits = jnp.dot(hidden_wide, router_w, precision=HIGHEST, preferred_element_type=jnp.float32)
    logits = logits + jnp.dot(
        previous, resid_w, precision=HIGHEST, preferred_element_type=jnp.float32
    )
    chances = softmax_rows(logits)
    chosen = jnp.take_along_axis(chances, route_rows, axis=1)
    gate_vals = chosen / jnp.sum(chosen, axis=1, keepdims=True)
    const_outs = []
    for member in range(2):
        mixing = softmax_rows(
            jnp.dot(
                hidden_wide, const_w[member], precision=HIGHEST, preferred_element_type=jnp.float32
            )
        )
        const_outs.append(mixing[:, :1] * hidden_in + mixing[:, 1:] * const_v[member][None, :])
    combined = jnp.zeros_like(hidden_in)
    for picked in range(TOP):
        route_id = route_rows[:, picked][:, None]
        branch_out = jnp.where(route_id == EXPERTS + 1, hidden_in, 0.0)
        for member in range(2):
            branch_out = branch_out + jnp.where(
                route_id == EXPERTS + 2 + member, const_outs[member], 0.0
            )
        combined = combined + gate_vals[:, picked : picked + 1] * branch_out
    return (combined, gate_vals)


def cont_places(side):
    half_len = P_DEV // 2
    local_rows = jnp.arange(P_DEV, dtype=jnp.int32)
    return (side + 2 * (local_rows // half_len)) * half_len + local_rows % half_len


def body(
    tokens,
    prev_logits,
    routes,
    branch_points,
    cotangent,
    attn_gain,
    qkv_weight,
    out_weight,
    ffn_gain,
    router_weight,
    resid_weight,
    const_weight,
    const_vector,
    gate_weight,
    up_weight,
    down_weight,
):
    group_size = lax.axis_size("grp")
    my_index = lax.axis_index("grp")
    prompt_total = P_DEV * group_size
    prompt_blocks = group_size // 2
    inputs = tokens[0].astype(jnp.float32)
    first_gain = attn_gain.astype(jnp.float32)
    normed, attn_back = jax.vjp(rms_norm, inputs, first_gain)
    normed_low = normed.astype(jnp.bfloat16)
    whole_qkv, whole_out = (
        lax.all_gather(qkv_weight, "grp", axis=0, tiled=True),
        lax.all_gather(out_weight, "grp", axis=0, tiled=True),
    )
    projected = jnp.dot(normed_low, whole_qkv, preferred_element_type=jnp.float32).astype(
        jnp.bfloat16
    )
    query_all = projected[:, :D]
    key_all = projected[:, D : 2 * D]
    value_all = projected[:, 2 * D :]
    prompt_keys, prompt_values = (
        lax.all_gather(key_all[:P_DEV], "grp", axis=0, tiled=True),
        lax.all_gather(value_all[:P_DEV], "grp", axis=0, tiled=True),
    )
    partner_keys, partner_values = from_partner((key_all[P_DEV:], value_all[P_DEV:]), "grp", 0)
    cont_keys = split_heads(jnp.concatenate([key_all[P_DEV:], partner_keys], axis=0))
    cont_values = split_heads(jnp.concatenate([value_all[P_DEV:], partner_values], axis=0))
    row_ids = jnp.arange(TOK_DEV)
    is_prompt = row_ids < P_DEV
    parity = my_index % 2
    follow = lax.dynamic_index_in_dim(branch_points[0], my_index // 2, keepdims=False)
    prompt_limit = jnp.where(is_prompt, my_index * P_DEV + row_ids + 1, follow)
    needed = jnp.max(prompt_limit)
    own_places = cont_places(parity)
    cont_query = jnp.concatenate([jnp.full((P_DEV,), -1, jnp.int32), own_places])
    key_places = jnp.concatenate([own_places, cont_places(1 - parity)])
    cont_allowed = key_places[None, :] <= cont_query[:, None]
    block_starts = jnp.arange(prompt_blocks) * TOK_DEV
    query_heads = split_heads(query_all)
    initial = (
        jnp.full((HEADS, TOK_DEV), MASKED, jnp.float32),
        jnp.zeros((HEADS, TOK_DEV), jnp.float32),
        jnp.zeros((TOK_DEV, HEADS, HEAD_DIM), jnp.float32),
    )

    def prompt_forward(running, pieces):
        piece_keys, piece_values, offset = pieces
        allowed = (offset + jnp.arange(TOK_DEV))[None, :] < prompt_limit[:, None]

        def compute(current):
            return forward_block(current, query_heads, piece_keys, piece_values, allowed)

        def passing(current):
            return current

        return (lax.cond(offset < needed, compute, passing, running), None)

    key_blocks = prompt_keys.reshape(prompt_blocks, TOK_DEV, HEADS, HEAD_DIM)
    value_blocks = prompt_values.reshape(prompt_blocks, TOK_DEV, HEADS, HEAD_DIM)
    running, unused = lax.scan(prompt_forward, initial, (key_blocks, value_blocks, block_starts))
    run_max, run_sum, run_acc = forward_block(
        running, query_heads, cont_keys, cont_values, cont_allowed
    )
    attn_heads = run_acc / jnp.transpose(run_sum)[:, :, None]
    log_total = run_max + jnp.log(run_sum)
    attn_low = attn_heads.reshape(TOK_DEV, D).astype(jnp.bfloat16)
    residual = inputs + jnp.dot(attn_low, whole_out, preferred_element_type=jnp.float32)
    second_gain = ffn_gain.astype(jnp.float32)
    hidden_in, ffn_back = jax.vjp(rms_norm, residual, second_gain)
    hidden_low = hidden_in.astype(jnp.bfloat16)
    hidden_wide = hidden_low.astype(jnp.float32)
    route_rows = routes[0]
    (local_mix, gate_vals), mixer_back = jax.vjp(
        partial(mixer_terms, route_rows),
        hidden_in,
        hidden_wide,
        router_weight.astype(jnp.float32),
        resid_weight.astype(jnp.float32),
        const_weight.astype(jnp.float32),
        const_vector.astype(jnp.float32),
        prev_logits[0],
    )
    flat_routes = route_rows.reshape(-1)
    matches = (flat_routes[:, None] == jnp.arange(EXPERTS, dtype=jnp.int32)[None, :]).astype(
        jnp.int32
    )
    slots = jnp.sum((jnp.cumsum(matches, axis=0) - 1) * matches, axis=1)
    is_expert = flat_routes < EXPERTS
    places = jnp.where(is_expert, flat_routes * CAP + slots, EXPERTS * CAP)
    sources = (
        jnp.full((EXPERTS * CAP + 1,), TOP * TOK_DEV, jnp.int32)
        .at[places]
        .set(jnp.arange(TOP * TOK_DEV, dtype=jnp.int32))[: EXPERTS * CAP]
    )
    padded_low = jnp.concatenate([hidden_low, jnp.zeros((1, D), jnp.bfloat16)], axis=0)
    outgoing = padded_low[sources // TOP]
    per_device = max(1, EXPERTS // group_size)
    split_count = max(1, group_size // EXPERTS)
    targets = np.array(
        [
            (target * per_device + member) // split_count
            for target in range(group_size)
            for member in range(per_device)
        ],
        dtype=np.int32,
    )
    ordered = outgoing.reshape(EXPERTS, CAP, D)[targets].reshape(group_size, per_device * CAP, D)
    arrived = lax.all_to_all(ordered, "grp", split_axis=0, concat_axis=0, tiled=True).reshape(
        group_size, per_device, CAP, D
    )
    width = gate_weight.shape[1] // per_device
    gate_local = gate_weight.reshape(D, per_device, width)
    up_local = up_weight.reshape(D, per_device, width)
    down_local = down_weight.reshape(per_device, width, D)
    gate_act = jnp.einsum("nkcd,dkf->nkcf", arrived, gate_local, preferred_element_type=jnp.float32)
    up_act = jnp.einsum("nkcd,dkf->nkcf", arrived, up_local, preferred_element_type=jnp.float32)
    sigmoid = 1.0 / (1.0 + jnp.exp(-gate_act))
    expert_hidden = (gate_act * sigmoid * up_act).astype(jnp.bfloat16)
    pieces_out = jnp.einsum(
        "nkcf,kfd->nkcd", expert_hidden, down_local, preferred_element_type=jnp.float32
    )
    returned = lax.all_to_all(
        pieces_out.reshape(group_size, per_device * CAP, D).astype(jnp.bfloat16),
        "grp",
        split_axis=0,
        concat_axis=0,
        tiled=True,
    ).astype(jnp.float32)
    expert_out = (
        returned.reshape(EXPERTS, split_count, CAP, D).sum(axis=1).reshape(EXPERTS * CAP, D)
    )
    padded_out = jnp.concatenate([expert_out, jnp.zeros((1, D), jnp.float32)], axis=0)
    route_out = padded_out[places].reshape(TOK_DEV, TOP, D)
    layer_out = residual + local_mix + jnp.sum(gate_vals[:, :, None] * route_out, axis=1)
    upstream = cotangent[0].astype(jnp.float32)
    gate_grads = jnp.sum(upstream[:, None, :] * route_out, axis=2)
    slot_gates = jnp.concatenate([gate_vals.reshape(-1), jnp.zeros((1,), jnp.float32)])[sources]
    padded_up = jnp.concatenate([upstream, jnp.zeros((1, D), jnp.float32)], axis=0)
    expert_grad = (slot_gates[:, None] * padded_up[sources // TOP]).astype(jnp.bfloat16)
    ordered_grad = expert_grad.reshape(EXPERTS, CAP, D)[targets].reshape(
        group_size, per_device * CAP, D
    )
    arrived_grad = lax.all_to_all(
        ordered_grad, "grp", split_axis=0, concat_axis=0, tiled=True
    ).reshape(group_size, per_device, CAP, D)
    down_grad = jnp.einsum(
        "nkcf,nkcd->kfd", expert_hidden, arrived_grad, preferred_element_type=jnp.float32
    ).reshape(-1, D)
    hidden_grad = jnp.einsum(
        "nkcd,kfd->nkcf", arrived_grad, down_local, preferred_element_type=jnp.float32
    )
    gate_pre = (hidden_grad * up_act * sigmoid * (1.0 + gate_act * (1.0 - sigmoid))).astype(
        jnp.bfloat16
    )
    up_pre = (hidden_grad * gate_act * sigmoid).astype(jnp.bfloat16)
    gate_grad = jnp.einsum(
        "nkcd,nkcf->dkf", arrived, gate_pre, preferred_element_type=jnp.float32
    ).reshape(D, -1)
    up_grad = jnp.einsum(
        "nkcd,nkcf->dkf", arrived, up_pre, preferred_element_type=jnp.float32
    ).reshape(D, -1)
    input_back = jnp.einsum(
        "nkcf,dkf->nkcd", gate_pre, gate_local, preferred_element_type=jnp.float32
    )
    input_back = input_back + jnp.einsum(
        "nkcf,dkf->nkcd", up_pre, up_local, preferred_element_type=jnp.float32
    )
    returned_grad = lax.all_to_all(
        input_back.reshape(group_size, per_device * CAP, D).astype(jnp.bfloat16),
        "grp",
        split_axis=0,
        concat_axis=0,
        tiled=True,
    ).astype(jnp.float32)
    slot_grad = (
        returned_grad.reshape(EXPERTS, split_count, CAP, D).sum(axis=1).reshape(EXPERTS * CAP, D)
    )
    padded_grad = jnp.concatenate([slot_grad, jnp.zeros((1, D), jnp.float32)], axis=0)
    token_grad = padded_grad[places].reshape(TOK_DEV, TOP, D).sum(axis=1)
    direct_grad, rounded_grad, router_grad, resid_grad, const_grad, vector_grad, prev_grad = (
        mixer_back((upstream, gate_grads))
    )
    hidden_total = direct_grad + rounded_grad + token_grad
    residual_part, gain_two = ffn_back(hidden_total)
    residual_grad = upstream + residual_part
    mix_grad = residual_grad.astype(jnp.bfloat16)
    projection_grad = lax.dot_general(
        attn_low, mix_grad, (((0,), (0,)), ((), ())), preferred_element_type=jnp.float32
    )
    back_qkv, back_out = (
        lax.all_gather(qkv_weight, "grp", axis=0, tiled=True),
        lax.all_gather(out_weight, "grp", axis=0, tiled=True),
    )
    back_keys, back_values = (
        lax.all_gather(key_all[:P_DEV], "grp", axis=0, tiled=True),
        lax.all_gather(value_all[:P_DEV], "grp", axis=0, tiled=True),
    )
    out_grad = lax.dot_general(
        mix_grad, back_out, (((1,), (1,)), ((), ())), preferred_element_type=jnp.float32
    ).astype(jnp.bfloat16)
    grad_heads = split_heads(out_grad)
    delta_rows = jnp.transpose(jnp.sum(grad_heads.astype(jnp.float32) * attn_heads, axis=2))

    def prompt_backward(query_total, pieces):
        piece_keys, piece_values, offset = pieces
        allowed = (offset + jnp.arange(TOK_DEV))[None, :] < prompt_limit[:, None]

        def compute(current):
            query_add, key_grad, value_grad = backward_block(
                query_heads, grad_heads, log_total, delta_rows, piece_keys, piece_values, allowed
            )
            return (current + query_add, key_grad, value_grad)

        def passing(current):
            empty = jnp.zeros((TOK_DEV, HEADS, HEAD_DIM), jnp.float32)
            return (current, empty, empty)

        query_next, key_grad, value_grad = lax.cond(offset < needed, compute, passing, query_total)
        return (query_next, (key_grad, value_grad))

    back_key_blocks = back_keys.reshape(prompt_blocks, TOK_DEV, HEADS, HEAD_DIM)
    back_value_blocks = back_values.reshape(prompt_blocks, TOK_DEV, HEADS, HEAD_DIM)
    query_total, (keys_grad, values_grad) = lax.scan(
        prompt_backward,
        jnp.zeros((TOK_DEV, HEADS, HEAD_DIM), jnp.float32),
        (back_key_blocks, back_value_blocks, block_starts),
    )
    query_add, later_keys, later_values = backward_block(
        query_heads, grad_heads, log_total, delta_rows, cont_keys, cont_values, cont_allowed
    )
    query_low = (query_total + query_add).reshape(TOK_DEV, D).astype(jnp.bfloat16)
    own_keys, own_values = (
        lax.psum_scatter(
            keys_grad.reshape(prompt_total, D).astype(jnp.bfloat16),
            "grp",
            scatter_dimension=0,
            tiled=True,
        ).astype(jnp.float32),
        lax.psum_scatter(
            values_grad.reshape(prompt_total, D).astype(jnp.bfloat16),
            "grp",
            scatter_dimension=0,
            tiled=True,
        ).astype(jnp.float32),
    )
    later_keys = later_keys.reshape(2 * P_DEV, D)
    later_values = later_values.reshape(2 * P_DEV, D)
    next_keys, next_values = (
        from_partner(later_keys[P_DEV:].astype(jnp.bfloat16), "grp", 0).astype(jnp.float32),
        from_partner(later_values[P_DEV:].astype(jnp.bfloat16), "grp", 0).astype(jnp.float32),
    )
    key_low = jnp.concatenate([own_keys, later_keys[:P_DEV] + next_keys], axis=0).astype(
        jnp.bfloat16
    )
    value_low = jnp.concatenate([own_values, later_values[:P_DEV] + next_values], axis=0).astype(
        jnp.bfloat16
    )
    qkv_low = jnp.concatenate([query_low, key_low, value_low], axis=1)
    qkv_full = lax.dot_general(
        normed_low, qkv_low, (((0,), (0,)), ((), ())), preferred_element_type=jnp.float32
    )
    normed_grad = lax.dot_general(
        qkv_low, back_qkv, (((1,), (1,)), ((), ())), preferred_element_type=jnp.float32
    )
    input_part, gain_one = attn_back(normed_grad)
    input_grad = residual_grad + input_part
    qkv_shard, out_shard = (
        lax.psum_scatter(
            qkv_full.astype(jnp.bfloat16), "grp", scatter_dimension=0, tiled=True
        ).astype(jnp.float32),
        lax.psum_scatter(
            projection_grad.astype(jnp.bfloat16), "grp", scatter_dimension=0, tiled=True
        ).astype(jnp.float32),
    )
    qkv_sum, out_sum, gate_sum, up_sum, down_sum = (
        lax.psum(qkv_shard.astype(jnp.bfloat16), "rep").astype(jnp.float32),
        lax.psum(out_shard.astype(jnp.bfloat16), "rep").astype(jnp.float32),
        lax.psum(gate_grad.astype(jnp.bfloat16), "rep").astype(jnp.float32),
        lax.psum(up_grad.astype(jnp.bfloat16), "rep").astype(jnp.float32),
        lax.psum(down_grad.astype(jnp.bfloat16), "rep").astype(jnp.float32),
    )
    gains_sum, router_sum, resid_sum, const_sum, vector_sum = lax.psum(
        (jnp.stack([gain_one, gain_two], axis=0), router_grad, resid_grad, const_grad, vector_grad),
        ("rep", "grp"),
    )
    return (
        layer_out[None],
        input_grad[None],
        prev_grad[None],
        gains_sum,
        qkv_sum,
        out_sum,
        router_sum,
        resid_sum,
        const_sum,
        vector_sum,
        gate_sum,
        up_sum,
        down_sum,
    )


def solution(mesh):
    in_specs = (
        P("rep", "grp", None),
        P("rep", "grp", None),
        P("rep", "grp", None),
        P("rep", None),
        P("rep", "grp", None),
        P(),
        P("grp", None),
        P("grp", None),
        P(),
        P(),
        P(),
        P(),
        P(),
        P(None, "grp"),
        P(None, "grp"),
        P("grp", None),
    )
    out_specs = (
        P("rep", "grp", None),
        P("rep", "grp", None),
        P("rep", "grp", None),
        P(),
        P("grp", None),
        P("grp", None),
        P(),
        P(),
        P(),
        P(),
        P(None, "grp"),
        P(None, "grp"),
        P("grp", None),
    )
    return jax.shard_map(body, mesh=mesh, in_specs=in_specs, out_specs=out_specs, check_vma=False)
```

profile of v0, /device:TPU:0, one launch (start us, length us, event | category | flops | bytes accessed | tf_op | source)
XLA Modules:
  0.0 1194.9 jit_solution(2799540611654396887)
XLA Ops:
  10.6 32.5 %all-gather.5.cloned.1.call-done = bf16[768,2304]{1,0:T(8,128)(2,1)} async-done(((bf16[192,2304]{1,0:T(8,128)(2,1)}), bf16[768,2304]{1,0:T(8,128)(2,1)}) %all-gather.5.cloned.1.call-update) | async-done | bytes 3538960 | tf_op jit(solution)/shard_map/all_gather | solution.py:152
  64.6 11.3 reshape.458
  75.9 11.2 reshape.457
  122.4 27.0 %while.33 = (s32[]{:T(128)}, f32[12,512]{1,0:T(8,128)S(1)}, f32[12,512]{1,0:T(8,128)S(1)}, f32[512,12,64]{0,2,1:T(8,128)}, s32[2]{0:T(128)S(1)}, /*index=5*/s32[...) while((s32[]{:T(128)}, f32[12,512]{1,0:T(8,128)S(1)}, ...), condition=%wide.region_7.8_spmd.clone, body=%wide.region_2.7_spmd.clone.sunk | while | flops 847270400 | bytes 63605152 | solution.py:200
  124.3 11.6 conditional.6
  137.8 11.6 conditional.6
  171.6 8.6 gather_fusion.7
  217.2 11.1 fusion.71
  237.4 13.5 %fusion.54 = (bf16[4,2,128,2048]{3,2,0,1:T(8,128)(2,1)}, bf16[4,2,128,2048]{3,2,0,1:T(8,128)(2,1)S(1)}, bf16[4,2,128,2048]{3,2,0,1:T(8,128)(2,1)}) fusion(f32[2,4,128,2048]{3,2,1,0:T(8,128)} %fusion.71, f32[2,4,128,2048]{3,2,1,0:T(8,128)} %fusion.75, bf16[2,2048,768,1]{2,1,3,0:T(8,128)(2,1)} %bitcast.415, bf16[4,2,128,768]{3,2,1,0:T(8,128)(2,1)} %bitcast.64), kind=kOutput, calls=%fused_computation.82 | convolution fusion | flops 3254779904 | bytes 37224448 | tf_op jit(solution)/shard_map/nkcd,kfd->nkcf/dot_general | solution.py:289
  264.8 12.2 %fusion.69 = f32[2,4,128,768]{3,2,1,0:T(8,128)S(1)} fusion(bf16[4,2,128,2048]{3,2,0,1:T(8,128)(2,1)} %get-tuple-element.746, bf16[768,2,2048,1]{2,1,0,3:T(2,128)(2,1)} %bitcast.372), kind=kOutput, calls=%fused_computation.99 | convolution fusion | flops 3221225472 | bytes 13631488 | tf_op jit(solution)/shard_map/nkcf,dkf->nkcd/dot_general | solution.py:305
  301.8 17.6 %multiply_reduce_fusion = (f32[512,2]{1,0:T(8,128)}, f32[512,768]{1,0:T(8,128)S(1)}) fusion(f32[512,2,768]{2,1,0:T(2,128)} %reshape.461, f32[512,768]{1,0:T(8,128)S(1)} %copy-done.17, f32[512,2]{1,0:T(8,128)S(1)} %copy-done.29), kind=kLoop, calls=%fused_computation.116 | loop fusion | flops 2751488 | bytes 6299648 | tf_op jit(solution)/shard_map/reduce_sum | solution.py:276
  362.2 54.7 %while.34 = (s32[]{:T(128)}, f32[512,12,64]{0,2,1:T(8,128)}, bf16[2,512,12,64]{1,3,2,0:T(8,128)(2,1)}, bf16[2,512,12,64]{1,3,2,0:T(8,128)(2,1)}, s32[2]{0:T(128)...) while((s32[]{:T(128)}, f32[512,12,64]{0,2,1:T(8,128)}, ...), condition=%wide.region_47.48_spmd.clone, body=%wide.region_44.47_spmd.clone.sunk | while | flops 2052852224 | bytes 74019176 | solution.py:363
  364.3 22.7 %conditional.7 = (f32[512,12,64]{0,2,1:T(8,128)}, bf16[1,512,12,64]{1,3,2,0:T(8,128)(2,1)}, bf16[1,512,12,64]{1,3,2,0:T(8,128)(2,1)}) conditional(s32[]{:T(128)} %convert_element_type.336, f32[512,12,64]{0,2,1:T(8,128)} %get-tuple-element.1015, (s32[]{:T(128)}, s32[1,512]{1,0:T(1,128)S(1)}, s32[512]{0:T(512)S(1)}, ...), branch_computations={%region_45.45_spmd, %region_46.46_spmd.clone} | conditional | flops 2052852224 | bytes 70868552 | solution.py:358
  391.6 22.7 %conditional.7 = (f32[512,12,64]{0,2,1:T(8,128)}, bf16[1,512,12,64]{1,3,2,0:T(8,128)(2,1)}, bf16[1,512,12,64]{1,3,2,0:T(8,128)(2,1)}) conditional(s32[]{:T(128)} %convert_element_type.336, f32[512,12,64]{0,2,1:T(8,128)} %get-tuple-element.1015, (s32[]{:T(128)}, s32[1,512]{1,0:T(1,128)S(1)}, s32[512]{0:T(512)S(1)}, ...), branch_computations={%region_45.45_spmd, %region_46.46_spmd.clone} | conditional | flops 2052852224 | bytes 70868552 | solution.py:358
  456.1 25.0 %reduce-scatter.7.cloned.1.call-done = bf16[256,768]{0,1:T(8,128)(2,1)} async-done(((bf16[1024,768]{0,1:T(8,128)(2,1)}), bf16[256,768]{0,1:T(8,128)(2,1)}) %reduce-scatter.7.cloned.1.call-update) | async-done | bytes 393232 | tf_op jit(solution)/shard_map/reduce_scatter | solution.py:379
  486.7 9.0 bitcast_convert_fusion.2
  495.8 8.6 copy.201
  504.4 8.9 bitcast_convert_fusion.1
  513.3 8.9 copy.204
  522.2 9.0 bitcast_convert_fusion
  531.1 21.5 %reduce-scatter.9.cloned.1.call-done = bf16[192,2304]{1,0:T(8,128)(2,1)} async-done(((bf16[768,2304]{1,0:T(8,128)(2,1)}), bf16[192,2304]{1,0:T(8,128)(2,1)}) %reduce-scatter.9.cloned.1.call-update) | async-done | bytes 884752 | tf_op jit(solution)/shard_map/reduce_scatter | solution.py:408
  561.2 46.1 %all-reduce.15 = (f32[2,768]{1,0:T(2,128)}, f32[768,12]{0,1:T(8,128)}, f32[12,12]{0,1:T(8,128)S(1)}, f32[2,768,2]{1,2,0:T(2,128)}, f32[2,768]{1,0:T(2,128)}) all-reduce(f32[2,768]{1,0:T(2,128)S(1)} %pad_maximum_fusion.3, f32[768,12]{0,1:T(8,128)S(1)} %fusion.140, ...), channel_id=1, replica_groups=mesh['rep'=8,'grp'=4] {'rep','grp'}, use_global_device_ids=true, to_apply=%region_53.54 | all-reduce | flops 15504 | bytes 124032 | tf_op jit(solution)/shard_map/psum | solution.py:422
  611.0 553.2 %all-reduce.19.cloned.1.call-done = (bf16[192,2304]{1,0:T(8,128)(2,1)}, bf16[192,768]{1,0:T(8,128)(2,1)}, bf16[768,4096]{1,0:T(8,128)(2,1)}, bf16[768,4096]{1,0:T(8,128)(2,1)}, bf16[4096,768]{1,0:T(8,128)(2,1)}) async-done(((bf16[192,2304]{1,0:T(8,128)(2,1)}, bf16[192,768]{1,0:T(8,128)(2,1)}, bf16[768,4096]{1,0:T(8,128)(2,1)}, bf16[768,4096]{1,0:T(8,128)(2,1)}, bf16[4096,768]{1,0:T(8,128)(2,1)}), ...) | async-done | bytes 20054032 | tf_op jit(solution)/shard_map/psum | solution.py:416
  1164.2 9.5 convert_element_type.264
  (562 shorter events, 355.1 us)
Async XLA Ops:
  7.2 162.6 %copy-start = (bf16[768,12]{0,1:T(8,128)(2,1)S(1)}, bf16[768,12]{0,1:T(8,128)(2,1)}, u32[]{:S(2)}) copy-start(bf16[768,12]{0,1:T(8,128)(2,1)} %param.36) | copy-start | bytes 55300
  7.2 35.9 %all-gather.5.cloned.1.call-start = ((), (), s32[]{:S(2)}) async-start(), calls=%async_computation.8 | async-start | bytes 4423680 | tf_op jit(solution)/shard_map/all_gather | solution.py:152
  7.9 98.0 %all-gather.7.cloned.1.call-start = ((), (), s32[]{:S(2)}) async-start(), calls=%async_computation.9 | async-start | bytes 1966080 | tf_op jit(solution)/shard_map/all_gather | solution.py:162
  49.8 61.9 %all-gather.9.cloned.1.call-start = ((), (), s32[]{:S(2)}) async-start(), calls=%async_computation.10 | async-start | bytes 1966080 | tf_op jit(solution)/shard_map/all_gather | solution.py:163
  50.6 115.2 %all-gather.11.cloned.1.call-start = ((), (), s32[]{:S(2)}) async-start(), calls=%async_computation.11 | async-start | bytes 1474560 | tf_op jit(solution)/shard_map/all_gather | solution.py:153
  63.6 32.2 %collective-permute-start = (bf16[256,768]{1,0:T(8,128)(2,1)}, bf16[256,768]{1,0:T(8,128)(2,1)}, u32[]{:S(2)}, u32[]{:S(2)}) collective-permute-start(bf16[256,768]{1,0:T(8,128)(2,1)} %get-tuple-element.747), channel_id=1, source_target_pairs={{0,1},{1,0},{2,3},{3,2},{4,5},{5,4},{6,7},{7,6},{8,9},{9,8},{10,11... | collective-permute-start | bytes 1179656 | tf_op jit(solution)/shard_map/ppermute | solution.py:28
  63.9 33.3 %collective-permute-start.1 = (bf16[256,768]{1,0:T(8,128)(2,1)}, bf16[256,768]{1,0:T(8,128)(2,1)}, u32[]{:S(2)}, u32[]{:S(2)}) collective-permute-start(bf16[256,768]{1,0:T(8,128)(2,1)} %get-tuple-element.748), channel_id=1, source_target_pairs={{0,1},{1,0},{2,3},{3,2},{4,5},{5,4},{6,7},{7,6},{8,9},{9,8},{10,11... | collective-permute-start | bytes 1179656 | tf_op jit(solution)/shard_map/ppermute | solution.py:28
  64.2 104.1 %copy-start.63 = (f32[768]{0:T(1024)}, f32[768]{0:T(1024)S(1)}, u32[]{:S(2)}) copy-start(f32[768]{0:T(1024)S(1)} %convert_element_type.223) | copy-start | bytes 9220
  95.5 62.4 %copy-start.35 = (pred[512,512]{0,1:T(8,128)(4,1)}, pred[512,512]{0,1:T(8,128)(4,1)S(1)}, u32[]{:S(2)}) copy-start(pred[512,512]{0,1:T(8,128)(4,1)S(1)} %broadcast_compare_fusion.2) | copy-start | bytes 786436
  99.0 58.8 %copy-start.51 = (bf16[512,768]{0,1:T(8,128)(2,1)}, bf16[512,768]{0,1:T(8,128)(2,1)S(1)}, u32[]{:S(2)}) copy-start(bf16[512,768]{0,1:T(8,128)(2,1)S(1)} %copy.170) | copy-start | bytes 2359300
  187.8 24.6 %all-to-all-start = ((bf16[4,256,768]{2,1,0:T(8,128)(2,1)}), bf16[4,256,768]{2,1,0:T(8,128)(2,1)}, u32[]{:S(2)}, u32[]{:S(2)}) async-start(bf16[4,256,768]{2,1,0:T(8,128)(2,1)} %bitcast.38), calls=%async_computation | async-start | bytes 3145728 | tf_op jit(solution)/shard_map/all_to_all | solution.py:248
  203.8 144.7 %copy-start.87 = (pred[512,2]{0,1:T(4,128)(4,1)}, pred[512,2]{0,1:T(4,128)(4,1)S(1)}, u32[]{:S(2)}) copy-start(pred[512,2]{0,1:T(4,128)(4,1)S(1)} %get-tuple-element.733) | copy-start | bytes 3076
  204.4 145.0 %copy-start.89 = (pred[512,2]{0,1:T(4,128)(4,1)}, pred[512,2]{0,1:T(4,128)(4,1)S(1)}, u32[]{:S(2)}) copy-start(pred[512,2]{0,1:T(4,128)(4,1)S(1)} %get-tuple-element.737) | copy-start | bytes 3076
  212.5 24.9 %all-to-all-start.2 = ((bf16[4,256,768]{2,1,0:T(8,128)(2,1)}), bf16[4,256,768]{2,1,0:T(8,128)(2,1)}, u32[]{:S(2)}, u32[]{:S(2)}) async-start(bf16[4,256,768]{2,1,0:T(8,128)(2,1)} %bitcast.380), calls=%async_computation.2 | async-start | bytes 3145728 | tf_op jit(solution)/shard_map/all_to_all | solution.py:283
  260.3 24.7 %all-to-all-start.1 = ((bf16[4,256,768]{2,1,0:T(8,128)(2,1)}), bf16[4,256,768]{2,1,0:T(8,128)(2,1)}, u32[]{:S(2)}, u32[]{:S(2)}) async-start(bf16[4,256,768]{2,1,0:T(8,128)(2,1)} %bitcast.377), calls=%async_computation.1 | async-start | bytes 3145728 | tf_op jit(solution)/shard_map/all_to_all | solution.py:262
  284.9 47.1 %all-to-all-start.3 = ((bf16[4,256,768]{2,1,0:T(8,128)(2,1)}), bf16[4,256,768]{2,1,0:T(8,128)(2,1)}, u32[]{:S(2)}, u32[]{:S(2)}) async-start(bf16[4,256,768]{2,1,0:T(8,128)(2,1)} %bitcast.71), calls=%async_computation.3 | async-start | bytes 3145728 | tf_op jit(solution)/shard_map/all_to_all | solution.py:308
  289.3 166.8 %reduce-scatter.5.cloned.1.call-start = ((), (), s32[]{:S(2)}) async-start(), calls=%async_computation.12 | async-start | bytes 1966080 | tf_op jit(solution)/shard_map/reduce_scatter | solution.py:373
  421.6 59.5 %reduce-scatter.7.cloned.1.call-start = ((), (), s32[]{:S(2)}) async-start(), calls=%async_computation.13 | async-start | bytes 1966080 | tf_op jit(solution)/shard_map/reduce_scatter | solution.py:379
  425.4 105.8 %reduce-scatter.11.cloned.1.call-start = ((), (), s32[]{:S(2)}) async-start(), calls=%async_computation.15 | async-start | bytes 1474560 | tf_op jit(solution)/shard_map/reduce_scatter | solution.py:411
  437.5 14.7 %collective-permute-start.2 = (bf16[256,768]{0,1:T(8,128)(2,1)}, bf16[256,768]{0,1:T(8,128)(2,1)}, u32[]{:S(2)}, u32[]{:S(2)}) collective-permute-start(bf16[256,768]{0,1:T(8,128)(2,1)} %bitcast.79), channel_id=1, source_target_pairs={{0,1},{1,0},{2,3},{3,2},{4,5},{5,4},{6,7},{7,6},{8,9},{9,8},{10,11... | collective-permute-start | bytes 1179656 | tf_op jit(solution)/shard_map/ppermute | solution.py:28
  439.8 112.9 %reduce-scatter.9.cloned.1.call-start = ((), (), s32[]{:S(2)}) async-start(), calls=%async_computation.14 | async-start | bytes 4423680 | tf_op jit(solution)/shard_map/reduce_scatter | solution.py:408
  446.4 8.8 collective-permute-start.3
  486.5 677.7 %all-reduce.19.cloned.1.call-start = ((), (), s32[]{:S(2)}) async-start(), calls=%async_computation.16 | async-start | bytes 40108032 | tf_op jit(solution)/shard_map/psum | solution.py:416
  555.8 52.2 %copy-start.92 = (f32[512]{0:T(512)S(1)}, f32[512]{0:T(512)}, u32[]{:S(2)}) copy-start(f32[512]{0:T(512)} %copy-done.91) | copy-start | bytes 6148
  (139 other events, 1064.4 us)
Sparse Core Ops, SparseCore 0:
  9.6 33.4 all-gather.4
  49.9 19.6 all-gather.6
  71.8 19.6 all-gather.8
  92.9 17.4 all-gather.10
  421.7 28.6 reduce-scatter.4
  452.9 28.1 reduce-scatter.6
  483.7 25.7 reduce-scatter.10
  512.2 40.4 reduce-scatter.8
  558.5 605.6 all-reduce.18
where the time goes:
time: 1200 us; the launch traced here: 1190 us
  waiting for transfers between devices  645 us (54%)
  matrix products  202 us (17%)
  local copies, waits for them, and re-layouts  153 us (13%)
  other arithmetic  107 us (9%)
  blocking collectives  46.1 us (4%)
  starting transfers between devices  20.2 us (2%)
  between operations  16.2 us (1%)
    psum x1, waiting for transfers between devices, body(): lax.psum(qkv_shard.astype(jnp.bfloat16), 'rep').astype(jnp.float32)  553 us
    psum x1, blocking collectives, body(): lax.psum((jnp.stack([gain_one, gain_two], axis=0), router_grad, resid_gra...  46.1 us
    all_gather x1, waiting for transfers between devices, body(): lax.all_gather(qkv_weight, 'grp', axis=0, tiled=True)  32.5 us
    reduce_scatter x1, waiting for transfers between devices, body(): lax.psum_scatter(values_grad.reshape(prompt_total, D).astype(jnp.bfloat16...  25 us
  transfers between devices with their start and end apart: 17, of which 7 were waited for; matrix products, arithmetic and copies ran while one was open for 25% of the time, Pallas kernels for 0%

commit v1 on v0

v1 whole, which is shorter than its diff:
```python
from functools import partial
import math

import jax
import jax.numpy as jnp
import numpy as np
from jax import lax
from jax.experimental import pallas as pl
from jax.experimental.pallas import tpu as pltpu
from jax.sharding import PartitionSpec as P

D = 768
HEADS = 12
HEAD_DIM = 64
EXPERTS = 8
TOP = 2
P_DEV = 256
TOK_DEV = 512
CAP = 128
IDS = EXPERTS + 4
EXT = 16
BLOCK = TOK_DEV + EXT
LANES = 128
PAIRS = D // LANES

NORM_EPS = 1e-06
MASKED = -1e30
HIGHEST = lax.Precision.HIGHEST
F32 = jnp.float32
BF16 = jnp.bfloat16
VMEM_LIMIT = 56 * 2**20
SMALL_ROWS = 40


def mm(left, right):
    return jnp.dot(left, right, preferred_element_type=F32)


def mm_nt(left, right):
    return lax.dot_general(left, right, (((1,), (1,)), ((), ())), preferred_element_type=F32)


def mm_tn(left, right):
    return lax.dot_general(left, right, (((0,), (0,)), ((), ())), preferred_element_type=F32)


def split(values):
    high = values.astype(BF16)
    return high, (values - high.astype(F32)).astype(BF16)


def shape_of(dims, dtype):
    return jax.ShapeDtypeStruct(dims, dtype)


def estimate(flops, bytes_accessed):
    return pl.CostEstimate(
        flops=int(flops), bytes_accessed=int(bytes_accessed), transcendentals=0
    )


def params():
    return pltpu.CompilerParams(vmem_limit_bytes=VMEM_LIMIT)


def whole_call(kernel, name, scalars, arrays, outs, flops, scratch=()):
    vmem = pl.BlockSpec(memory_space=pltpu.VMEM)
    moved = sum(a.size * a.dtype.itemsize for a in arrays)
    moved += sum(math.prod(o.shape) * np.dtype(o.dtype).itemsize for o in outs)
    return pl.pallas_call(
        kernel,
        out_shape=tuple(outs),
        in_specs=[pl.BlockSpec(memory_space=pltpu.SMEM)] + [vmem] * len(arrays),
        out_specs=tuple([vmem] * len(outs)),
        scratch_shapes=list(scratch),
        compiler_params=params(),
        cost_estimate=estimate(flops, moved),
        name=name,
    )(scalars, *arrays)


def xor_permute(value, offset):
    pairs = [(source, source ^ offset) for source in range(lax.axis_size("grp"))]
    return lax.ppermute(value, "grp", pairs)


def ring_permute(value, step):
    count = lax.axis_size("rep")
    order = list(range(0, count, 2)) + list(range(count - 1, 0, -2))
    pairs = [(order[at], order[(at + step) % count]) for at in range(count)]
    return lax.ppermute(value, "rep", pairs)


def gather_group(value, lowest):
    pieces = {0: value}
    bit = lax.axis_size("grp") // 2
    while bit >= lowest:
        for offset in list(pieces):
            pieces[offset | bit] = xor_permute(pieces[offset], bit)
        bit //= 2
    return pieces


def projection_kernel(group, scal, gain, tok, partner, *rest):
    prompts, shards = rest[: group - 1], rest[group - 1 : 2 * group - 1]
    q_out, kp_out, vp_out, kc_out, vc_out, w_out, n_out = rest[2 * group - 1 :]
    rows = D // group
    for offset in range(group):
        start = pl.multiple_of(scal[offset] * rows, rows)
        w_out[pl.ds(start, rows), :] = shards[offset][...]

    def normed(values):
        wide = values.astype(F32)
        scale = lax.rsqrt(jnp.mean(wide * wide, axis=-1, keepdims=True) + NORM_EPS)
        return (wide * scale * gain[...]).astype(BF16)

    own = normed(tok[...])
    n_out[...] = own
    q_out[...] = mm(own, w_out[:, :D]).astype(BF16)
    kv = mm(own, w_out[:, D:]).astype(BF16)
    start = pl.multiple_of(scal[0] * P_DEV, P_DEV)
    kp_out[pl.ds(start, P_DEV), :] = kv[:P_DEV, :D]
    vp_out[pl.ds(start, P_DEV), :] = kv[:P_DEV, D:]
    kc_out[:P_DEV, :] = kv[P_DEV:, :D]
    vc_out[:P_DEV, :] = kv[P_DEV:, D:]
    kv = mm(normed(partner[...]), w_out[:, D:]).astype(BF16)
    kc_out[P_DEV:, :] = kv[:, :D]
    vc_out[P_DEV:, :] = kv[:, D:]
    for offset in range(1, group):
        kv = mm(normed(prompts[offset - 1][...]), w_out[:, D:]).astype(BF16)
        start = pl.multiple_of(scal[offset] * P_DEV, P_DEV)
        kp_out[pl.ds(start, P_DEV), :] = kv[:, :D]
        vp_out[pl.ds(start, P_DEV), :] = kv[:, D:]


def place_of(local, side):
    half = P_DEV // 2
    return (side + 2 * (local // half)) * half + local % half


def attention_kernel(group, scal, q_ref, kp_ref, vp_ref, kc_ref, vc_ref, o_ref, lse_ref):
    prompt = kp_ref.shape[0]
    index, follow, side = scal[0], scal[group], scal[group + 1]
    lane = lax.broadcasted_iota(jnp.int32, (1, LANES), 1)
    row = lax.broadcasted_iota(jnp.int32, (P_DEV, 1), 0)
    key_at = lax.broadcasted_iota(jnp.int32, (1, prompt), 1)
    cont_at = lax.broadcasted_iota(jnp.int32, (1, 2 * P_DEV), 1)
    cont_place = place_of(cont_at % P_DEV, jnp.where(cont_at < P_DEV, side, 1 - side))
    row_place = place_of(row, side)
    for part in range(2):
        rows = pl.ds(part * P_DEV, P_DEV)
        scaled = q_ref[rows, :] * BF16(1.0 / math.sqrt(HEAD_DIM))
        limit = index * P_DEV + row + 1 if part == 0 else jnp.broadcast_to(follow, (P_DEV, 1))
        mixed, logs = [], []
        for head in range(2):
            masked = jnp.where(lane // HEAD_DIM == head, scaled, BF16(0))
            scores = jnp.where(key_at < limit, mm_nt(masked, kp_ref[...]), MASKED)
            top = jnp.max(scores, axis=1, keepdims=True)
            if part == 1:
                later = jnp.where(cont_place <= row_place, mm_nt(masked, kc_ref[...]), MASKED)
                top = jnp.maximum(top, jnp.max(later, axis=1, keepdims=True))
            weights = jnp.exp(scores - top)
            total = jnp.sum(weights, axis=1, keepdims=True)
            out = mm(weights.astype(BF16), vp_ref[...])
            if part == 1:
                weights = jnp.exp(later - top)
                total = total + jnp.sum(weights, axis=1, keepdims=True)
                out = out + mm(weights.astype(BF16), vc_ref[...])
            mixed.append(out / total)
            logs.append(top + jnp.log(total))
        o_ref[rows, :] = jnp.where(lane < HEAD_DIM, mixed[0], mixed[1])
        lse_ref[rows, :] = jnp.where(lane < HEAD_DIM, logs[0], logs[1])


def attention(scal, q, kp, vp, kc, vc, group):
    prompt = kp.shape[0]
    column = lambda rows: pl.BlockSpec((rows, LANES), lambda p: (0, p))
    flops = 4 * 2 * HEADS * P_DEV * (2 * prompt + 2 * P_DEV) * LANES
    return pl.pallas_call(
        partial(attention_kernel, group),
        out_shape=(shape_of((TOK_DEV, D), F32), shape_of((TOK_DEV, D), F32)),
        grid=(PAIRS,),
        in_specs=[pl.BlockSpec(memory_space=pltpu.SMEM)]
        + [column(n) for n in (TOK_DEV, prompt, prompt, 2 * P_DEV, 2 * P_DEV)],
        out_specs=(column(TOK_DEV), column(TOK_DEV)),
        compiler_params=params(),
        cost_estimate=estimate(flops, 10 * TOK_DEV * D * 2),
        name="attention_forward",
    )(scal, q, kp, vp, kc, vc)


def attention_back_kernel(group, scal, q_ref, kp_ref, vp_ref, kc_ref, vc_ref, do_ref, o_ref, lse_ref, *rest):
    prompt = kp_ref.shape[0]
    dq_ref = rest[0]
    pieces = rest[1 : 1 + group]
    own_ref, other_ref, dkp_acc, dvp_acc, dkc_acc, dvc_acc = rest[1 + group :]
    index, follow, side = scal[0], scal[group], scal[group + 1]
    lane = lax.broadcasted_iota(jnp.int32, (1, LANES), 1)
    sub = lax.broadcasted_iota(jnp.int32, (LANES, 1), 0)
    col = lax.broadcasted_iota(jnp.int32, (1, P_DEV), 1)
    key_at = lax.broadcasted_iota(jnp.int32, (prompt, 1), 0)
    cont_at = lax.broadcasted_iota(jnp.int32, (2 * P_DEV, 1), 0)
    cont_place = place_of(cont_at % P_DEV, jnp.where(cont_at < P_DEV, side, 1 - side))
    col_place = place_of(col, side)
    logs = jnp.transpose(lse_ref[...])
    products = jnp.transpose(do_ref[...].astype(F32) * o_ref[...])
    keys_t = jnp.transpose(kp_ref[...])
    later_t = jnp.transpose(kc_ref[...])
    for part in range(2):
        rows = pl.ds(part * P_DEV, P_DEV)
        span = slice(part * P_DEV, (part + 1) * P_DEV)
        scaled = q_ref[rows, :] * BF16(1.0 / math.sqrt(HEAD_DIM))
        grads = do_ref[rows, :]
        limit = index * P_DEV + col + 1 if part == 0 else jnp.broadcast_to(follow, (1, P_DEV))
        turned = []
        for head in range(2):
            mine = lane // HEAD_DIM == head
            query = jnp.where(mine, scaled, BF16(0))
            grad = jnp.where(mine, grads, BF16(0))
            log_row = logs[head * HEAD_DIM : head * HEAD_DIM + 1, span]
            delta = jnp.sum(
                products[head * HEAD_DIM : (head + 1) * HEAD_DIM, span], axis=0, keepdims=True
            )

            def back(keys, values, allowed):
                probs = jnp.exp(jnp.where(allowed, mm_nt(keys, query) - log_row, MASKED))
                score_grad = (probs * (mm_nt(values, grad) - delta)).astype(BF16)
                return score_grad, mm(score_grad, query), mm(probs.astype(BF16), grad)

            score_grad, dk, dv = back(kp_ref[...], vp_ref[...], key_at < limit)
            dq_t = mm(keys_t, score_grad)
            if part == 0 and head == 0:
                dkp_acc[...] = dk
                dvp_acc[...] = dv
            else:
                dkp_acc[...] += dk
                dvp_acc[...] += dv
            if part == 1:
                score_grad, dk, dv = back(kc_ref[...], vc_ref[...], cont_place <= col_place)
                dq_t = dq_t + mm(later_t, score_grad)
                if head == 0:
                    dkc_acc[...] = dk
                    dvc_acc[...] = dv
                else:
                    dkc_acc[...] += dk
                    dvc_acc[...] += dv
            turned.append(dq_t)
        both = jnp.where(sub < HEAD_DIM, turned[0], turned[1]) * (1.0 / math.sqrt(HEAD_DIM))
        dq_ref[rows, :] = jnp.transpose(both).astype(BF16)
    for offset in range(group):
        start = pl.multiple_of(scal[offset] * P_DEV, P_DEV)
        pieces[offset][0] = dkp_acc[pl.ds(start, P_DEV), :].astype(BF16)
        pieces[offset][1] = dvp_acc[pl.ds(start, P_DEV), :].astype(BF16)
    own_ref[0] = dkc_acc[:P_DEV, :]
    own_ref[1] = dvc_acc[:P_DEV, :]
    other_ref[0] = dkc_acc[P_DEV:, :].astype(BF16)
    other_ref[1] = dvc_acc[P_DEV:, :].astype(BF16)


def attention_back(scal, q, kp, vp, kc, vc, do, o32, lse, group):
    prompt = kp.shape[0]
    column = lambda rows: pl.BlockSpec((rows, LANES), lambda p: (0, p))
    double = pl.BlockSpec((2, P_DEV, LANES), lambda p: (0, 0, p))
    flops = 10 * 2 * HEADS * P_DEV * (2 * prompt + 2 * P_DEV) * LANES
    return pl.pallas_call(
        partial(attention_back_kernel, group),
        out_shape=(
            shape_of((TOK_DEV, D), BF16),
            *[shape_of((2, P_DEV, D), BF16)] * group,
            shape_of((2, P_DEV, D), F32),
            shape_of((2, P_DEV, D), BF16),
        ),
        grid=(PAIRS,),
        in_specs=[pl.BlockSpec(memory_space=pltpu.SMEM)]
        + [
            column(n)
            for n in (TOK_DEV, prompt, prompt, 2 * P_DEV, 2 * P_DEV, TOK_DEV, TOK_DEV, TOK_DEV)
        ],
        out_specs=(column(TOK_DEV), *[double] * group, double, double),
        scratch_shapes=[
            pltpu.VMEM((prompt, LANES), F32),
            pltpu.VMEM((prompt, LANES), F32),
            pltpu.VMEM((2 * P_DEV, LANES), F32),
            pltpu.VMEM((2 * P_DEV, LANES), F32),
        ],
        compiler_params=params(),
        cost_estimate=estimate(flops, 20 * TOK_DEV * D * 2),
        name="attention_backward",
    )(scal, q, kp, vp, kc, vc, do, o32, lse)


def columns(values):
    lane = lax.broadcasted_iota(jnp.int32, (1, LANES), 1)
    packed = None
    for at, value in values.items():
        term = jnp.where(lane == at, value, 0.0)
        packed = term if packed is None else packed + term
    return packed


def routing_kernel(group, scal, tok, o32, *rest):
    shards = rest[:group]
    gain, mixers, vectors, previous, routes = rest[group : group + 5]
    w_out, res_out, base_out, blk_out, info_out, low_out = rest[group + 5 :]
    rows = D // group
    for offset in range(group):
        start = pl.multiple_of(scal[offset] * rows, rows)
        w_out[pl.ds(start, rows), :] = shards[offset][...]
    low = o32[...].astype(BF16)
    low_out[...] = low
    res = tok[...].astype(F32) + mm(low, w_out[...])
    res_out[...] = res
    scale = lax.rsqrt(jnp.mean(res * res, axis=-1, keepdims=True) + NORM_EPS)
    hidden = res * scale * gain[...]
    hidden_low = hidden.astype(BF16)
    blk_out[:TOK_DEV, :] = hidden_low
    lane = lax.broadcasted_iota(jnp.int32, (1, LANES), 1)
    dots = mm(hidden_low, mixers[...])
    logits = jnp.where(lane < IDS, dots + previous[...], MASKED)
    weights = jnp.exp(logits - jnp.max(logits, axis=1, keepdims=True))
    chances = weights / jnp.sum(weights, axis=1, keepdims=True)
    first, second = routes[:, 0:1], routes[:, 1:2]
    chosen0 = jnp.sum(jnp.where(lane == first, chances, 0.0), axis=1, keepdims=True)
    chosen1 = jnp.sum(jnp.where(lane == second, chances, 0.0), axis=1, keepdims=True)
    both = chosen0 + chosen1
    gate0, gate1 = chosen0 / both, chosen1 / both

    def gate_of(ident):
        return jnp.where(first == ident, gate0, 0.0) + jnp.where(second == ident, gate1, 0.0)

    info = {12: gate0, 13: gate1, 21: both}
    hidden_part = gate_of(EXPERTS + 1)
    base = res
    for member in range(2):
        left = dots[:, IDS + 2 * member : IDS + 2 * member + 1]
        right = dots[:, IDS + 2 * member + 1 : IDS + 2 * member + 2]
        top = jnp.maximum(left, right)
        left, right = jnp.exp(left - top), jnp.exp(right - top)
        alpha0, alpha1 = left / (left + right), right / (left + right)
        gate = gate_of(EXPERTS + 2 + member)
        hidden_part = hidden_part + gate * alpha0
        base = base + (gate * alpha1) * vectors[member : member + 1, :]
        info[15 + member] = gate * alpha1
        info[17 + 2 * member] = alpha0
        info[18 + 2 * member] = alpha1
        info[22 + member] = gate
    info[14] = hidden_part
    base_out[...] = base + hidden_part * hidden
    info_out[...] = jnp.where(lane < IDS, chances, columns(info))
    gates = jnp.where(lane == first, gate0, 0.0) + jnp.where(lane == second, gate1, 0.0)
    turned = jnp.transpose(gates)[:EXPERTS, :]
    high = turned.astype(BF16).astype(F32)
    ext = jnp.concatenate([high, turned - high], axis=0).astype(BF16)
    blk_out[TOK_DEV:, :TOK_DEV] = ext
    blk_out[TOK_DEV:, TOK_DEV:] = jnp.zeros((EXT, D - TOK_DEV), BF16)


def rows_kernel(group, per, share, aliased, scal, *rest):
    hidden = rest[:group]
    grads = rest[group : 2 * group]
    outs = rest[2 * group + aliased :]
    x_out, s_out, xt_out, st_out, slots, gates = outs
    slot = lax.broadcasted_iota(jnp.int32, (CAP, 1), 0).astype(F32)
    for at in range(group):
        slots[...] = grads[at][TOK_DEV:, :TOK_DEV].astype(F32)
        pair = hidden[at][TOK_DEV:, :TOK_DEV].astype(F32)
        gates[...] = pair[:EXPERTS, :] + pair[EXPERTS:, :]
        for member in range(per):
            expert = (scal[0] * per + member) // share
            picked = slots[pl.ds(expert, 1), :] == slot
            gate = jnp.sum(
                jnp.where(picked, gates[pl.ds(expert, 1), :], 0.0), axis=1, keepdims=True
            )
            chooser = jnp.where(picked, 1.0, 0.0).astype(BF16)
            span = pl.ds(at * CAP, CAP)
            x_out[0, member, span, :] = mm(chooser, hidden[at][:TOK_DEV, :]).astype(BF16)
            s_out[0, member, span, :] = (mm(chooser, grads[at][:TOK_DEV, :]) * gate).astype(BF16)
    for member in range(per):
        xt_out[0, member] = jnp.transpose(x_out[0, member])
        st_out[0, member] = jnp.transpose(s_out[0, member])


def expert_rows(scal, hidden, grads, at, count, stacks, group, per, share):
    rows = group * CAP
    natural, turned = (count, per, rows, D), (count, per, D, rows)
    block = lambda dims: pl.BlockSpec((1, *dims[1:]), lambda i: (at, 0, 0, 0))
    vmem = pl.BlockSpec((BLOCK, D), lambda i: (0, 0))
    held = [pl.BlockSpec(memory_space=pl.ANY)] * len(stacks)
    first = 1 + 2 * group
    return pl.pallas_call(
        partial(rows_kernel, group, per, share, len(stacks)),
        out_shape=tuple(shape_of(d, BF16) for d in (natural, natural, turned, turned)),
        grid=(1,),
        in_specs=[pl.BlockSpec(memory_space=pltpu.SMEM)] + [vmem] * (2 * group) + held,
        out_specs=tuple(block(d) for d in (natural, natural, turned, turned)),
        scratch_shapes=[pltpu.VMEM((EXT, TOK_DEV), F32), pltpu.VMEM((EXPERTS, TOK_DEV), F32)],
        input_output_aliases={first + n: n for n in range(len(stacks))},
        compiler_params=params(),
        cost_estimate=estimate(
            4 * group * per * CAP * TOK_DEV * D, 2 * (2 * group * BLOCK + 4 * per * rows) * D
        ),
        name="expert_rows",
    )(scal, *hidden, *grads, *stacks)


def sigmoid(values):
    return 0.5 * jnp.tanh(0.5 * values) + 0.5


def expert_terms(x, s, gate_w, up_w, down_w):
    act_a, act_b = mm(x, gate_w), mm(x, up_w)
    sig = sigmoid(act_a)
    silu = act_a * sig
    hidden = (silu * act_b).astype(BF16)
    hidden_grad = mm_nt(s, down_w)
    grad_a = (hidden_grad * act_b * (sig + silu * (1.0 - sig))).astype(BF16)
    grad_b = (hidden_grad * silu).astype(BF16)
    return hidden, grad_a, grad_b


def expert_kernel(group, offsets, x_ref, s_ref, wg, wu, wd, *rest):
    outs, out_acc, in_acc = rest[:group], rest[group], rest[group + 1]
    step = pl.program_id(0)
    rows = x_ref.shape[2]
    chunk = min(rows, 512)
    for start in range(0, rows, chunk):
        span = pl.ds(start, chunk)
        hidden, grad_a, grad_b = expert_terms(
            x_ref[0, 0, span, :], s_ref[0, 0, span, :], wg[...], wu[...], wd[...]
        )
        out = mm(hidden, wd[...])
        back = mm_nt(grad_a, wg[...]) + mm_nt(grad_b, wu[...])

        @pl.when(step == 0)
        def _():
            out_acc[span, :] = out
            in_acc[span, :] = back

        @pl.when(step > 0)
        def _():
            out_acc[span, :] += out
            in_acc[span, :] += back

    @pl.when(step == pl.num_programs(0) - 1)
    def _():
        for at in range(group):
            outs[offsets[at]][0] = out_acc[at * CAP : (at + 1) * CAP, :].astype(BF16)
            outs[offsets[at]][1] = in_acc[at * CAP : (at + 1) * CAP, :].astype(BF16)


def local_expert(x, s, gate_w, up_w, down_w, member, offsets, group, per):
    width = gate_w.shape[1] // per
    tile = min(512, width)
    steps = width // tile
    rows = group * CAP
    side = pl.BlockSpec((1, 1, rows, D), lambda t: (0, member, 0, 0))
    wide = pl.BlockSpec((D, tile), lambda t: (0, member * steps + t))
    tall = pl.BlockSpec((tile, D), lambda t: (member * steps + t, 0))
    piece = pl.BlockSpec((2, CAP, D), lambda t: (0, 0, 0))
    return pl.pallas_call(
        partial(expert_kernel, group, offsets),
        out_shape=tuple([shape_of((2, CAP, D), BF16)] * group),
        grid=(steps,),
        in_specs=[side, side, wide, wide, tall],
        out_specs=tuple([piece] * group),
        scratch_shapes=[pltpu.VMEM((rows, D), F32), pltpu.VMEM((rows, D), F32)],
        compiler_params=params(),
        cost_estimate=estimate(12 * rows * D * width, 6 * D * width + 8 * rows * D),
        name="local_expert",
    )(x, s, gate_w, up_w, down_w)


def slice_kernel(mode, at_ref, x, s, xt, st, wg, wu, wd, *rest):
    outs, (gate_acc, up_acc, down_acc) = rest[:-3], rest[-3:]
    step = pl.program_id(1)
    batches, rows = x.shape[0], x.shape[2]
    terms = [
        expert_terms(x[n, 0], s[n, 0], wg[...], wu[...], wd[...]) for n in range(batches)
    ]
    gate = sum(mm(xt[n, 0], terms[n][1]) for n in range(batches))
    up = sum(mm(xt[n, 0], terms[n][2]) for n in range(batches))
    down = sum(mm(st[n, 0], terms[n][0]) for n in range(batches))

    @pl.when(step == 0)
    def _():
        gate_acc[...] = gate
        up_acc[...] = up
        down_acc[...] = down

    @pl.when(step > 0)
    def _():
        gate_acc[...] += gate
        up_acc[...] += up
        down_acc[...] += down

    @pl.when(step == pl.num_programs(1) - 1)
    def _():
        if mode == "pack":
            outs[0][0] = gate_acc[...].astype(BF16)
            outs[0][1] = up_acc[...].astype(BF16)
            outs[0][2] = down_acc[...].astype(BF16)
        else:
            outs[0][...] = gate_acc[...]
            outs[1][...] = up_acc[...]
            outs[2][...] = jnp.transpose(down_acc[...])


def weight_slices(at, stacks, weights, member, tile, tiles, mode, batches, per):
    x, s, xt, st = stacks
    count, rows = x.shape[0], x.shape[2]
    steps = count // batches
    natural = pl.BlockSpec((batches, 1, rows, D), lambda t, d, ref: (d, member, 0, 0))
    turned = pl.BlockSpec((batches, 1, D, rows), lambda t, d, ref: (d, member, 0, 0))
    wide = pl.BlockSpec((D, tile), lambda t, d, ref: (0, ref[0] + t))
    tall = pl.BlockSpec((tile, D), lambda t, d, ref: (ref[0] + t, 0))
    units = weights[0].shape[1]
    if mode == "pack":
        outs = (shape_of((3, D, tile), BF16),)
        specs = (pl.BlockSpec((3, D, tile), lambda t, d, ref: (0, 0, 0)),)
    else:
        outs = (shape_of((D, units), F32), shape_of((D, units), F32), shape_of((units, D), F32))
        specs = (wide, wide, tall)
    return pl.pallas_call(
        partial(slice_kernel, mode),
        out_shape=outs,
        grid_spec=pltpu.PrefetchScalarGridSpec(
            num_scalar_prefetch=1,
            grid=(tiles, steps),
            in_specs=[natural, natural, turned, turned, wide, wide, tall],
            out_specs=specs,
            scratch_shapes=[pltpu.VMEM((D, tile), F32)] * 3,
        ),
        compiler_params=params(),
        cost_estimate=estimate(
            12 * count * rows * D * tile * tiles, tiles * (8 * count * rows * D + 6 * D * tile)
        ),
        name="weight_slices",
    )(at, *stacks, *weights)


def place_kernel(held, at_ref, piece, *rest):
    gate_out, up_out, down_out = rest[held:]
    gate_out[...] = piece[0].astype(F32)
    up_out[...] = piece[1].astype(F32)
    down_out[...] = jnp.transpose(piece[2].astype(F32))


def place_slice(at, piece, held, units):
    tile = piece.shape[2]
    wide = pl.BlockSpec((D, tile), lambda t, ref: (0, ref[0]))
    tall = pl.BlockSpec((tile, D), lambda t, ref: (ref[0], 0))
    return pl.pallas_call(
        partial(place_kernel, len(held)),
        out_shape=(shape_of((D, units), F32), shape_of((D, units), F32), shape_of((units, D), F32)),
        grid_spec=pltpu.PrefetchScalarGridSpec(
            num_scalar_prefetch=1,
            grid=(1,),
            in_specs=[pl.BlockSpec((3, D, tile), lambda t, ref: (0, 0, 0))]
            + [pl.BlockSpec(memory_space=pl.ANY)] * len(held),
            out_specs=(wide, wide, tall),
        ),
        input_output_aliases={2 + n: n for n in range(len(held))},
        compiler_params=params(),
        cost_estimate=estimate(0, 18 * D * tile),
        name="place_slice",
    )(at, piece, *held)


def combine_kernel(group, per, share, scal, *refs):
    pieces = refs[: group * per]
    (base, cot, blk, info_ref, slots, routes, res_ref, gain, vectors, mixers_t, resid_t, prev, w_out) = refs[
        group * per : group * per + 13
    ]
    layer_out, grad_out, mix_out, mixed_out, prev_out, small_out = refs[group * per + 13 :]
    info = info_ref[...]
    first, second = routes[:, 0:1], routes[:, 1:2]
    lane = lax.broadcasted_iota(jnp.int32, (1, LANES), 1)
    slot_lane = lane.astype(F32)
    taken = slots[...]
    out0 = out1 = back = None
    for offset in range(group):
        for member in range(per):
            expert = (scal[offset] * per + member) // share
            column = jnp.sum(jnp.where(lane == expert, taken, 0.0), axis=1, keepdims=True)
            chooser = column == slot_lane
            piece = pieces[offset * per + member]
            pick0 = jnp.where(chooser & (first == expert), 1.0, 0.0).astype(BF16)
            pick1 = jnp.where(chooser & (second == expert), 1.0, 0.0).astype(BF16)
            add0, add1 = mm(pick0, piece[0]), mm(pick1, piece[0])
            add2 = mm(pick0 + pick1, piece[1])
            out0 = add0 if out0 is None else out0 + add0
            out1 = add1 if out1 is None else out1 + add1
            back = add2 if back is None else back + add2
    get = lambda at: info[:, at : at + 1]
    gate0, gate1, hidden_part, both = get(12), get(13), get(14), get(21)
    layer_out[...] = base[...] + gate0 * out0 + gate1 * out1
    grad = cot[...].astype(F32)
    res = res_ref[...]
    scale = lax.rsqrt(jnp.mean(res * res, axis=-1, keepdims=True) + NORM_EPS)
    unit = res * scale
    total = lambda values: jnp.sum(values, axis=1, keepdims=True)
    dot_hidden = total(grad * (unit * gain[...]))
    dot_vector = [total(grad * vectors[k : k + 1, :]) for k in range(2)]

    def gate_grad(route, out):
        value = total(grad * out) + jnp.where(route == EXPERTS + 1, dot_hidden, 0.0)
        for k in range(2):
            const = get(17 + 2 * k) * dot_hidden + get(18 + 2 * k) * dot_vector[k]
            value = value + jnp.where(route == EXPERTS + 2 + k, const, 0.0)
        return value

    dgate0, dgate1 = gate_grad(first, out0), gate_grad(second, out1)
    mean = gate0 * dgate0 + gate1 * dgate1
    dchance = (
        jnp.where(lane == first, dgate0 - mean, 0.0) + jnp.where(lane == second, dgate1 - mean, 0.0)
    ) / both
    chances = jnp.where(lane < IDS, info, 0.0)
    logits_grad = chances * (dchance - total(chances * dchance))
    extra = {16: get(15), 17: get(16)}
    for k in range(2):
        alpha0, alpha1, gate = get(17 + 2 * k), get(18 + 2 * k), get(22 + k)
        d0, d1 = gate * dot_hidden, gate * dot_vector[k]
        inner = alpha0 * d0 + alpha1 * d1
        extra[IDS + 2 * k] = alpha0 * (d0 - inner)
        extra[IDS + 2 * k + 1] = alpha1 * (d1 - inner)
    packed = logits_grad + columns(extra)
    high, low = split(packed)
    prev_out[...] = mm(high, resid_t[...]) + mm(low, resid_t[...])
    hidden_total = (
        back + hidden_part * grad + mm(high, mixers_t[...]) + mm(low, mixers_t[...])
    )
    turned = jnp.transpose(packed)[:32, :]
    t_high, t_low = split(turned)
    hidden_low = blk[:TOK_DEV, :]
    by_hidden = mm(t_high, hidden_low) + mm(t_low, hidden_low)
    by_grad = mm(t_high, cot[...]) + mm(t_low, cot[...])
    prev_high, prev_low = split(prev[...])
    by_prev = mm(t_high, prev_high) + mm(t_high, prev_low) + mm(t_low, prev_high)
    gain_grad = jnp.sum(hidden_total * unit, axis=0, keepdims=True)
    sub = lax.broadcasted_iota(jnp.int32, (8, 1), 0)
    small_out[:16, :] = by_hidden[:16, :]
    small_out[16:24, :] = jnp.where(sub == 2, gain_grad, by_grad[16:24, :])
    small_out[24:40, :] = jnp.zeros((16, D), F32)
    small_out[24:40, :LANES] = by_prev[:16, :]
    u = gain[...] * hidden_total
    inner = jnp.mean(res * u, axis=1, keepdims=True)
    residual_grad = grad + scale * u - res * (scale * scale * scale * inner)
    grad_out[...] = residual_grad
    mix = residual_grad.astype(BF16)
    mix_out[...] = mix
    mixed_out[...] = mm_nt(mix, w_out[...]).astype(BF16)


def finish_kernel(prompt_terms, scal, dq, own, received, *rest):
    terms = rest[:prompt_terms]
    weights, tok, gain, res_grad = rest[prompt_terms : prompt_terms + 4]
    low_out, grad_out, small_out = rest[prompt_terms + 4 :]
    low_out[:, :D] = dq[...]
    for half in range(2):
        columns_at = slice((half + 1) * D, (half + 2) * D)
        prompt = terms[0][half].astype(F32)
        for term in terms[1:]:
            prompt = prompt + term[half].astype(F32)
        low_out[:P_DEV, columns_at] = prompt.astype(BF16)
        low_out[P_DEV:, columns_at] = (own[half] + received[half].astype(F32)).astype(BF16)
    normed_grad = mm_nt(low_out[...], weights[...])
    x = tok[...].astype(F32)
    scale = lax.rsqrt(jnp.mean(x * x, axis=-1, keepdims=True) + NORM_EPS)
    u = gain[...] * normed_grad
    inner = jnp.mean(x * u, axis=1, keepdims=True)
    grad_out[...] = res_grad[...] + scale * u - x * (scale * scale * scale * inner)
    row = jnp.sum(normed_grad * (x * scale), axis=0, keepdims=True)
    sub = lax.broadcasted_iota(jnp.int32, (8, 1), 0)
    small_out[...] = jnp.where(sub == 0, row, 0.0)


def sum_everywhere(value):
    for axis in ("rep", "grp"):
        count = lax.axis_size(axis)
        bit = 1
        while bit < count:
            pairs = [(source, source ^ bit) for source in range(count)]
            value = value + lax.ppermute(value, axis, pairs)
            bit *= 2
    return value


def sum_replicas(value):
    count = lax.axis_size("rep")
    index = lax.axis_index("rep")
    bits = [1 << n for n in range(count.bit_length() - 1)]
    for bit in bits:
        half = value.shape[1] // 2
        left, right = value[:, :half], value[:, half:]
        upper = (index & bit) != 0
        keep = jnp.where(upper, right, left)
        give = jnp.where(upper, left, right).astype(BF16)
        pairs = [(source, source ^ bit) for source in range(count)]
        value = keep + lax.ppermute(give, "rep", pairs).astype(F32)
    value = value.astype(BF16)
    for bit in reversed(bits):
        pairs = [(source, source ^ bit) for source in range(count)]
        other = lax.ppermute(value, "rep", pairs)
        upper = (index & bit) != 0
        value = jnp.concatenate(
            [jnp.where(upper, other, value), jnp.where(upper, value, other)], axis=1
        )
    return value.astype(F32)


def body(
    tokens,
    prev_logits,
    routes,
    branch_points,
    cotangent,
    attn_gain,
    qkv_weight,
    out_weight,
    ffn_gain,
    router_weight,
    resid_weight,
    const_weight,
    const_vector,
    gate_weight,
    up_weight,
    down_weight,
):
    group, count = lax.axis_size("grp"), lax.axis_size("rep")
    index, replica = lax.axis_index("grp"), lax.axis_index("rep")
    per, share = max(1, EXPERTS // group), max(1, group // EXPERTS)
    prompt = P_DEV * group
    spread = group * count <= 32
    tok, cot, route_rows, prev = tokens[0], cotangent[0], routes[0], prev_logits[0]
    follow = lax.dynamic_index_in_dim(branch_points[0], index // 2, keepdims=True)
    scal = jnp.concatenate(
        [
            index ^ jnp.arange(group, dtype=jnp.int32),
            follow.astype(jnp.int32),
            (index % 2)[None].astype(jnp.int32),
        ]
    )

    shards = gather_group(qkv_weight, 1)
    prompts = gather_group(tok[:P_DEV], 1)
    partner = xor_permute(tok[P_DEV:], 1)
    out_shards = gather_group(out_weight, 1)

    ids = jnp.arange(LANES, dtype=jnp.int32)[None, :]
    named = (route_rows[:, :1] == ids) | (route_rows[:, 1:] == ids)
    at = jnp.arange(TOK_DEV)
    before = (at[None, :] < at[:, None]).astype(BF16)
    slots = jnp.where(named, mm(before, named.astype(BF16)), -1.0)
    ext = jnp.pad(
        jnp.transpose(slots[:, :EXT]).astype(BF16), ((0, 0), (0, D - TOK_DEV)), constant_values=-1
    )
    grad_block = jnp.concatenate([cot, ext], axis=0)
    route_lanes = jnp.pad(route_rows, ((0, 0), (0, LANES - TOP)))
    prev_lanes = jnp.pad(prev, ((0, 0), (0, LANES - IDS)))
    previous = jnp.pad(
        jnp.dot(prev, resid_weight.astype(F32), precision=HIGHEST, preferred_element_type=F32),
        ((0, 0), (0, LANES - IDS)),
    )
    mixers = jnp.pad(
        jnp.concatenate([router_weight, const_weight[0], const_weight[1]], axis=1),
        ((0, 0), (0, LANES - IDS - 4)),
    )
    mixers_t = jnp.transpose(mixers)
    resid_t = jnp.pad(jnp.transpose(resid_weight), ((0, LANES - IDS), (0, LANES - IDS)))
    vectors = jnp.pad(const_vector.astype(F32), ((0, 6), (0, 0)))
    gain_one = attn_gain.astype(F32)[None]
    gain_two = ffn_gain.astype(F32)[None]

    offsets = [o for o in range(0, group, 2)] + [o for o in range(1, group, 2)]

    def group_blocks(block):
        held = gather_group(block, 2)
        own = [held[o] for o in range(0, group, 2)]
        return own, own + [xor_permute(piece, 1) for piece in own]

    def all_blocks(own):
        half = max(1, len(own) // 2)
        forth, back = own[:half], own[half:]
        result = []
        for _ in range(count - 1):
            forth = [ring_permute(piece, 1) for piece in forth]
            back = [ring_permute(piece, -1) for piece in back]
            now = forth + back
            result.append(now + [xor_permute(piece, 1) for piece in now])
        return result

    grad_own, grad_group = group_blocks(grad_block)
    if spread:
        grad_far = all_blocks(grad_own)

    q, kp, vp, kc, vc, w_qkv, normed = whole_call(
        partial(projection_kernel, group),
        "projections",
        scal,
        [gain_one, tok, partner]
        + [prompts[o] for o in range(1, group)]
        + [shards[o] for o in range(group)],
        [
            shape_of((TOK_DEV, D), BF16),
            shape_of((prompt, D), BF16),
            shape_of((prompt, D), BF16),
            shape_of((2 * P_DEV, D), BF16),
            shape_of((2 * P_DEV, D), BF16),
            shape_of((D, 3 * D), BF16),
            shape_of((TOK_DEV, D), BF16),
        ],
        2 * TOK_DEV * D * D + 4 * (prompt + 2 * P_DEV) * D * D,
    )
    o32, lse = attention(scal, q, kp, vp, kc, vc, group)
    w_out, res, base, block, info, mixed_low = whole_call(
        partial(routing_kernel, group),
        "routing",
        scal,
        [tok, o32]
        + [out_shards[o] for o in range(group)]
        + [gain_two, mixers, vectors, previous, route_lanes],
        [
            shape_of((D, D), BF16),
            shape_of((TOK_DEV, D), F32),
            shape_of((TOK_DEV, D), F32),
            shape_of((BLOCK, D), BF16),
            shape_of((TOK_DEV, LANES), F32),
            shape_of((TOK_DEV, D), BF16),
        ],
        2 * TOK_DEV * D * D,
    )

    own, near = group_blocks(block)
    local = expert_rows(scal, near, grad_group, 0, 1, (), group, per, share)
    if spread:
        far = all_blocks(own)

    weights = (gate_weight, up_weight, down_weight)
    returned = {}
    for member in range(per):
        outs = local_expert(local[0], local[1], *weights, member, offsets, group, per)
        for offset in range(group):
            returned[offset, member] = xor_permute(outs[offset], offset) if offset else outs[0]

    layer_out, res_grad, mix_grad, mixed_grad, prev_grad, small = whole_call(
        partial(combine_kernel, group, per, share),
        "combine",
        scal,
        [returned[o, m] for o in range(group) for m in range(per)]
        + [
            base,
            cot,
            block,
            info,
            slots,
            route_lanes,
            res,
            gain_two,
            vectors,
            mixers_t,
            resid_t,
            prev_lanes,
            w_out,
        ],
        [
            shape_of((TOK_DEV, D), F32),
            shape_of((TOK_DEV, D), F32),
            shape_of((TOK_DEV, D), BF16),
            shape_of((TOK_DEV, D), BF16),
            shape_of((TOK_DEV, LANES), F32),
            shape_of((SMALL_ROWS, D), F32),
        ],
        6 * TOK_DEV * group * per * CAP * D + 2 * TOK_DEV * D * D,
    )

    back = attention_back(scal, q, kp, vp, kc, vc, mixed_grad, o32, lse, group)
    dq, pieces, later_own, later_other = back[0], list(back[1 : 1 + group]), back[-2], back[-1]
    later_in = xor_permute(later_other, 1)
    held = {o: [pieces[o]] for o in range(group)}
    bit = 1
    while bit < group:
        for offset in sorted(held):
            if offset & bit:
                terms = held.pop(offset)
                value = terms[0]
                if len(terms) > 1:
                    value = sum(t.astype(F32) for t in terms).astype(BF16)
                held[offset ^ bit].append(xor_permute(value, bit))
        bit *= 2
    terms = held[0]
    qkv_low, input_grad, small_two = whole_call(
        partial(finish_kernel, len(terms)),
        "finish",
        scal,
        [dq, later_own, later_in] + terms + [w_qkv, tok, gain_one, res_grad],
        [
            shape_of((TOK_DEV, 3 * D), BF16),
            shape_of((TOK_DEV, D), F32),
            shape_of((8, D), F32),
        ],
        6 * TOK_DEV * D * D,
    )
    full = jnp.concatenate([mm_tn(normed, qkv_low), mm_tn(mixed_low, mix_grad)], axis=1)
    rows = D // group
    held = {
        o: lax.dynamic_slice_in_dim(full, (index ^ o) * rows, rows, axis=0) for o in range(group)
    }
    bit = 1
    while bit < group:
        for offset in sorted(held):
            if offset & bit:
                value = xor_permute(held.pop(offset).astype(BF16), bit)
                held[offset ^ bit] = held[offset ^ bit] + value.astype(F32)
        bit *= 2
    dense = sum_replicas(held[0])
    small = sum_everywhere(jnp.concatenate([small, small_two], axis=0))

    units = gate_weight.shape[1]
    width = units // per
    if spread:
        stacks = ()
        for step in range(count):
            hidden = near if step == 0 else far[step - 1]
            grads = grad_group if step == 0 else grad_far[step - 1]
            stacks = expert_rows(scal, hidden, grads, step, count, stacks, group, per, share)
        tile = width // count
        first = replica.astype(jnp.int32)[None]
        finished = [
            weight_slices(
                first + member * count, stacks, weights, member, tile, 1, "pack", 2, per
            )[0]
            for member in range(per)
        ]
        spot = jnp.where(replica % 2 == 0, replica // 2, count - 1 - replica // 2)
        held = ()
        for step in range(count):
            for member in range(per):
                toward = 1 if member % 2 == 0 else -1
                if step:
                    finished[member] = ring_permute(finished[member], toward)
                source = (spot - toward * step) % count
                source = jnp.where(
                    source < count // 2, 2 * source, 2 * (count - 1 - source) + 1
                ).astype(jnp.int32)[None]
                held = place_slice(source + member * count, finished[member], held, units)
        gate_sum, up_sum, down_sum = held
    else:
        tile = min(512, width)
        sums = weight_slices(
            jnp.zeros((1,), jnp.int32), local, weights, 0, tile, width // tile, "write", 1, per
        )
        gate_sum, up_sum, down_sum = [
            lax.psum(part.astype(BF16), "rep").astype(F32) for part in sums
        ]

    gains = jnp.stack([small[SMALL_ROWS], small[18]], axis=0)
    router_grad = jnp.transpose(small[:IDS])
    const_grad = jnp.transpose(small[IDS : IDS + 4].reshape(2, 2, D), (0, 2, 1))
    resid_grad = jnp.transpose(small[24 : 24 + IDS, :IDS])
    return (
        layer_out[None],
        input_grad[None],
        prev_grad[:, :IDS][None],
        gains,
        dense[:, : 3 * D],
        dense[:, 3 * D :],
        router_grad,
        resid_grad,
        const_grad,
        small[16:18],
        gate_sum,
        up_sum,
        down_sum,
    )


def solution(mesh):
    in_specs = (
        P("rep", "grp", None),
        P("rep", "grp", None),
        P("rep", "grp", None),
        P("rep", None),
        P("rep", "grp", None),
        P(),
        P("grp", None),
        P("grp", None),
        P(),
        P(),
        P(),
        P(),
        P(),
        P(None, "grp"),
        P(None, "grp"),
        P("grp", None),
    )
    out_specs = (
        P("rep", "grp", None),
        P("rep", "grp", None),
        P("rep", "grp", None),
        P(),
        P("grp", None),
        P("grp", None),
        P(),
        P(),
        P(),
        P(),
        P(None, "grp"),
        P(None, "grp"),
        P("grp", None),
    )
    return jax.shard_map(body, mesh=mesh, in_specs=in_specs, out_specs=out_specs, check_vma=False)
```

time: 1200 us -> 745 us (0.62)
  waiting for transfers between devices: 645 us -> 333 us
  Pallas kernels: 0 us -> 269 us
  matrix products: 202 us -> 5.39 us
  local copies, waits for them, and re-layouts: 153 us -> 26.4 us
  other arithmetic: 107 us -> 22.4 us
  starting transfers between devices: 20.2 us -> 82.7 us
  blocking collectives: 46.1 us -> 0 us
  between operations: 16.2 us -> 2.41 us
    psum x1 -> x0, waiting for transfers between devices: 553 us -> none  [body(): lax.psum(qkv_shard.astype(jnp.bfloat16), 'rep').astype(jnp.float32)]
    ppermute x4 -> x110, waiting for transfers between devices: 0.01 us -> 333 us  [the longest x42 182 us: ring_permute(): return lax.ppermute(value, 'rep', pairs)]
    pallas_call x0 -> x35, Pallas kernels: none -> 269 us  [the longest x9 67.2 us: expert_rows(): pl.pallas_call(partial(rows_kernel, group, per, share, len(stacks)), out_...]
    dot_general x47 -> x4, matrix products: 202 us -> 5.39 us  [the longest x2 4.84 us: mm_tn(): lax.dot_general(left, right, (((0,), (0,)), ((), ())), preferred_element_...]
    ppermute x4 -> x110, starting transfers between devices: 1.18 us -> 82.7 us  [the longest x42 48.8 us: ring_permute(): return lax.ppermute(value, 'rep', pairs)]
    reduce_sum x22 -> x0, other arithmetic: 47.3 us -> none  [the longest x1 17.6 us: body(): gate_grads = jnp.sum(upstream[:, None, :] * route_out, axis=2)]
    reduce_scatter x4 -> x0, waiting for transfers between devices: 46.5 us -> none  [the longest x1 25 us: body(): lax.psum_scatter(values_grad.reshape(prompt_total, D).astype(jnp.bfloat16...]
    psum x1 -> x0, blocking collectives: 46.1 us -> none  [body(): lax.psum((jnp.stack([gain_one, gain_two], axis=0), router_grad, resid_gra...]
  transfers between devices with their start and end apart: 17 -> 110, of which waited for: 7 -> 37; matrix products, arithmetic and copies ran while one was open for 25% -> 6% of each run, Pallas kernels for 0% -> 33%
where the time goes in v1:
time: 745 us; the launch traced here: 741 us
  waiting for transfers between devices  333 us (45%)
  Pallas kernels  269 us (36%)
  starting transfers between devices  82.7 us (11%)
  local copies, waits for them, and re-layouts  26.4 us (4%)
  other arithmetic  22.4 us (3%)
    ppermute x42, waiting for transfers between devices, ring_permute(): return lax.ppermute(value, 'rep', pairs)  182 us
    ppermute x57, waiting for transfers between devices, xor_permute(): return lax.ppermute(value, 'grp', pairs)  79.2 us
    pallas_call x9, Pallas kernels, expert_rows(): pl.pallas_call(partial(rows_kernel, group, per, share, len(stacks)), out_...  67.2 us
    pallas_call x4, Pallas kernels, whole_call(): pl.pallas_call(kernel, out_shape=tuple(outs), in_specs=[pl.BlockSpec(memo...  49.4 us
    ppermute x42, starting transfers between devices, ring_permute(): return lax.ppermute(value, 'rep', pairs)  48.8 us
    pallas_call x16, Pallas kernels, place_slice(): pl.pallas_call(partial(place_kernel, len(held)), out_shape=(shape_of((D,...  45.5 us
    ppermute x3, waiting for transfers between devices, sum_replicas(): value = keep + lax.ppermute(give, 'rep', pairs).astype(F32)  43.4 us
    pallas_call x2, Pallas kernels, weight_slices(): pl.pallas_call(partial(slice_kernel, mode), out_shape=outs, grid_spec=plt...  32.4 us
  transfers between devices with their start and end apart: 110, of which 37 were waited for; matrix products, arithmetic and copies ran while one was open for 6% of the time, Pallas kernels for 33%

profile of v1, /device:TPU:0, one launch (start us, length us, event | category | flops | bytes accessed | tf_op | source)
XLA Modules:
  0.0 741.4 jit_solution(5721590614597932694)
XLA Ops:
  11.1 13.4 %collective-permute-done.5.rest_5_ = bf16[192,2304]{1,0:T(8,128)(2,1)} collective-permute-done((bf16[192,2304]{1,0:T(8,128)(2,1)}, bf16[192,2304]{1,0:T(8,128)(2,1)}, u32[]{:S(2)}, u32[]{:S(2)}) %collective-permute-start.5) | collective-permute-done | bytes 884768 | tf_op jit(solution)/shard_map/ppermute | solution.py:84
  26.1 12.2 %collective-permute-done.8.rest_2_ = bf16[192,768]{1,0:T(8,128)(2,1)S(1)} collective-permute-done((bf16[192,768]{1,0:T(8,128)(2,1)}, bf16[192,768]{1,0:T(8,128)(2,1)S(1)}, u32[]{:S(2)}, u32[]{:S(2)}) %collective-permute-start.8) | collective-permute-done | bytes 294944 | tf_op jit(solution)/shard_map/ppermute | solution.py:84
  47.8 9.8 %projections.1 = (bf16[512,768]{1,0:T(8,128)(2,1)}, bf16[1024,768]{1,0:T(8,128)(2,1)}, bf16[1024,768]{1,0:T(8,128)(2,1)}, bf16[512,768]{1,0:T(8,128)(2,1)}, bf16...) custom-call(s32[6]{0:T(128)} %pad_add_fusion.scal, f32[1,768]{1,0:T(1,128)} %reshape.47.gain.rest_5_, ...), custom_call_target="tpu_custom_call" | custom-call | flops 4227858432 | bytes 15731712 | tf_op jit(solution)/shard_map/projections/pallas_call | solution.py:70
  57.6 18.4 %attention_forward.1 = (f32[512,768]{1,0:T(8,128)}, f32[512,768]{1,0:T(8,128)}) custom-call(s32[6]{0:T(128)} %pad_add_fusion.scal, bf16[512,768]{1,0:T(8,128)(2,1)} %get-tuple-element.134.q_ref, bf16[1024,768]{1,0:T(8,128)(2,1)} %get-tuple-element.135.kp_ref, bf16[1024,768]{1,0:T(8,128)(2,1)} %get-tuple-element.136.vp_ref, ...), custom_call_target="tpu_custom_call" | custom-call | flops 8053063680 | bytes 7864320 | tf_op jit(solution)/shard_map/attention_forward/pallas_call | solution.py:179
  76.8 10.0 %routing.1 = (bf16[768,768]{1,0:T(8,128)(2,1)}, f32[512,768]{1,0:T(8,128)}, f32[512,768]{1,0:T(8,128)}, bf16[528,768]{1,0:T(8,128)(2,1)}, f32[512,128]{1,0:T(8,128)}, /*index=5*/bf16[512,768]{1,0:T(8,128)(2,1)}) custom-call(s32[6]{0:T(128)} %pad_add_fusion.scal, bf16[512,768]{1,0:T(8,128)(2,1)} %bitcast.52, f32[512,768]{1,0:T(8,128)} %get-tuple-element.139.o32.o_ref, ...), custom_call_target="tpu_custom_call" | custom-call | flops 603979776 | bytes 10472448 | tf_op jit(solution)/shard_map/routing/pallas_call | solution.py:70
  89.7 17.9 %collective-permute-done.10.rest_1_ = bf16[528,768]{1,0:T(8,128)(2,1)S(1)} collective-permute-done((bf16[528,768]{1,0:T(8,128)(2,1)}, bf16[528,768]{1,0:T(8,128)(2,1)S(1)}, u32[]{:S(2)}, u32[]{:S(2)}) %collective-permute-start.10) | collective-permute-done | bytes 811040 | tf_op jit(solution)/shard_map/ppermute | solution.py:84
  128.5 15.5 %local_expert.3 = (bf16[2,128,768]{2,1,0:T(8,128)(2,1)}, bf16[2,128,768]{2,1,0:T(8,128)(2,1)}, bf16[2,128,768]{2,1,0:T(8,128)(2,1)}, bf16[2,128,768]{2,1,0:T(8,128)(2,1)}) custom-call(bf16[1,2,512,768]{3,2,1,0:T(8,128)(2,1)} %get-tuple-element.141.x_ref, bf16[1,2,512,768]{3,2,1,0:T(8,128)(2,1)} %get-tuple-element.142.s_ref, bf16[768,4096]{1,0:T(8,128)(2,1)} %wg.7, ...), custom_call_target="tpu_custom_call" | custom-call | flops 9663676416 | bytes 12582912 | tf_op jit(solution)/shard_map/local_expert/pallas_call | solution.py:460
  148.7 15.7 %local_expert.2 = (bf16[2,128,768]{2,1,0:T(8,128)(2,1)}, bf16[2,128,768]{2,1,0:T(8,128)(2,1)}, bf16[2,128,768]{2,1,0:T(8,128)(2,1)}, bf16[2,128,768]{2,1,0:T(8,128)(2,1)}) custom-call(bf16[1,2,512,768]{3,2,1,0:T(8,128)(2,1)} %get-tuple-element.141.x_ref, bf16[1,2,512,768]{3,2,1,0:T(8,128)(2,1)} %get-tuple-element.142.s_ref, bf16[768,4096]{1,0:T(8,128)(2,1)} %wg.7, ...), custom_call_target="tpu_custom_call" | custom-call | flops 9663676416 | bytes 12582912 | tf_op jit(solution)/shard_map/local_expert/pallas_call | solution.py:460
  167.3 14.8 %collective-permute-done.47.rest_1_ = bf16[528,768]{1,0:T(8,128)(2,1)S(1)} collective-permute-done((bf16[528,768]{1,0:T(8,128)(2,1)S(1)}, bf16[528,768]{1,0:T(8,128)(2,1)S(1)}, u32[]{:S(2)}, u32[]{:S(2)}) %collective-permute-start.47) | collective-permute-done | bytes 811040 | tf_op jit(solution)/shard_map/ppermute | solution.py:91
  205.7 21.7 %combine.1 = (f32[512,768]{1,0:T(8,128)}, f32[512,768]{1,0:T(8,128)}, bf16[512,768]{1,0:T(8,128)(2,1)}, bf16[512,768]{1,0:T(8,128)(2,1)}, f32[512,128]{1,0:T(8,128)}, /*index=5*/f32[40,768]{1,0:T(8,128)}) custom-call(s32[6]{0:T(128)} %pad_add_fusion.scal, bf16[2,128,768]{2,1,0:T(8,128)(2,1)} %get-tuple-element.143.refs_0_, ...), custom_call_target="tpu_custom_call" | custom-call | flops 3019898880 | bytes 15477760 | tf_op jit(solution)/shard_map/combine/pallas_call | solution.py:70
  231.3 24.6 %attention_backward.1 = (bf16[512,768]{1,0:T(8,128)(2,1)}, bf16[2,256,768]{2,1,0:T(8,128)(2,1)}, bf16[2,256,768]{2,1,0:T(8,128)(2,1)}, bf16[2,256,768]{2,1,0:T(8...) custom-call(s32[6]{0:T(128)} %pad_add_fusion.scal, ...), custom_call_target="tpu_custom_call" | custom-call | flops 20132659200 | bytes 15728640 | tf_op jit(solution)/shard_map/attention_backward/pallas_call | solution.py:265
  268.9 8.6 %collective-permute-done.67.rest_5_ = bf16[528,768]{1,0:T(8,128)(2,1)S(1)} collective-permute-done((bf16[528,768]{1,0:T(8,128)(2,1)S(1)}, bf16[528,768]{1,0:T(8,128)(2,1)S(1)}, u32[]{:S(2)}, u32[]{:S(2)}) %collective-permute-start.67) | collective-permute-done | bytes 811040 | tf_op jit(solution)/shard_map/ppermute | solution.py:91
  303.7 17.9 %collective-permute-done.25.rest_2_ = bf16[2,256,768]{2,1,0:T(8,128)(2,1)S(1)} collective-permute-done((bf16[2,256,768]{2,1,0:T(8,128)(2,1)S(1)}, bf16[2,256,768]{2,1,0:T(8,128)(2,1)S(1)}, u32[]{:S(2)}, u32[]{:S(2)}) %collective-permute-start.25) | collective-permute-done | bytes 786464 | tf_op jit(solution)/shard_map/ppermute | solution.py:84
  329.4 13.2 %collective-permute-done.62.rest_4_ = bf16[528,768]{1,0:T(8,128)(2,1)S(1)} collective-permute-done((bf16[528,768]{1,0:T(8,128)(2,1)S(1)}, bf16[528,768]{1,0:T(8,128)(2,1)S(1)}, u32[]{:S(2)}, u32[]{:S(2)}) %collective-permute-start.62) | collective-permute-done | bytes 811040 | tf_op jit(solution)/shard_map/ppermute | solution.py:91
  344.6 13.0 %collective-permute-done.44.rest_0_ = bf16[528,768]{1,0:T(8,128)(2,1)} collective-permute-done((bf16[528,768]{1,0:T(8,128)(2,1)S(1)}, bf16[528,768]{1,0:T(8,128)(2,1)}, u32[]{:S(2)}, u32[]{:S(2)}) %collective-permute-start.44) | collective-permute-done | bytes 811040 | tf_op jit(solution)/shard_map/ppermute | solution.py:91
  452.9 16.3 %weight_slices.3.piece = bf16[3,768,256]{2,1,0:T(8,128)(2,1)} custom-call(s32[1]{0:T(128)} %bitcast.20.at_ref, bf16[8,2,512,768]{3,2,1,0:T(8,128)(2,1)} %get-tuple-element.203.x, bf16[8,2,512,768]{3,2,1,0:T(8,128)(2,1)} %get-tuple-element.204.s, bf16[8,2,768,512]{3,2,1,0:T(8,128)(2,1)} %get-tuple-element.205.xt, ...), custom_call_target="tpu_custom_call" | custom-call | flops 9663676416 | bytes 26345472 | tf_op jit(solution)/shard_map/weight_slices/pallas_call | solution.py:523
  471.0 16.1 %weight_slices.2.piece = bf16[3,768,256]{2,1,0:T(8,128)(2,1)} custom-call(s32[1]{0:T(128)S(6)} %add.245.at_ref, bf16[8,2,512,768]{3,2,1,0:T(8,128)(2,1)} %get-tuple-element.203.x, bf16[8,2,512,768]{3,2,1,0:T(8,128)(2,1)} %get-tuple-element.204.s, bf16[8,2,768,512]{3,2,1,0:T(8,128)(2,1)} %get-tuple-element.205.xt, ...), custom_call_target="tpu_custom_call" | custom-call | flops 9663676416 | bytes 26345472 | tf_op jit(solution)/shard_map/weight_slices/pallas_call | solution.py:523
  497.6 16.0 %collective-permute-done.96.piece = bf16[3,768,256]{2,1,0:T(8,128)(2,1)} collective-permute-done((bf16[3,768,256]{2,1,0:T(8,128)(2,1)}, bf16[3,768,256]{2,1,0:T(8,128)(2,1)}, u32[]{:S(2)}, u32[]{:S(2)}) %collective-permute-start.96) | collective-permute-done | bytes 1179680 | tf_op jit(solution)/shard_map/ppermute | solution.py:91
  523.5 16.2 %collective-permute-done.97.piece = bf16[3,768,256]{2,1,0:T(8,128)(2,1)} collective-permute-done((bf16[3,768,256]{2,1,0:T(8,128)(2,1)}, bf16[3,768,256]{2,1,0:T(8,128)(2,1)}, u32[]{:S(2)}, u32[]{:S(2)}) %collective-permute-start.97) | collective-permute-done | bytes 1179680 | tf_op jit(solution)/shard_map/ppermute | solution.py:91
  550.0 16.9 %collective-permute-done.98.piece = bf16[3,768,256]{2,1,0:T(8,128)(2,1)S(1)} collective-permute-done((bf16[3,768,256]{2,1,0:T(8,128)(2,1)}, bf16[3,768,256]{2,1,0:T(8,128)(2,1)S(1)}, u32[]{:S(2)}, u32[]{:S(2)}) %collective-permute-start.98) | collective-permute-done | bytes 1179680 | tf_op jit(solution)/shard_map/ppermute | solution.py:91
  569.3 10.2 %collective-permute-done.34 = bf16[192,1536]{1,0:T(8,128)(2,1)} collective-permute-done((bf16[192,1536]{1,0:T(8,128)(2,1)S(1)}, bf16[192,1536]{1,0:T(8,128)(2,1)}, u32[]{:S(2)}, u32[]{:S(2)}) %collective-permute-start.34) | collective-permute-done | bytes 589856 | tf_op jit(solution)/shard_map/ppermute | solution.py:699
  586.1 17.3 %collective-permute-done.26 = f32[48,768]{1,0:T(8,128)} collective-permute-done((f32[48,768]{1,0:T(8,128)}, f32[48,768]{1,0:T(8,128)}, u32[]{:S(2)}, u32[]{:S(2)}) %collective-permute-start.26) | collective-permute-done | bytes 147488 | tf_op jit(solution)/shard_map/ppermute | solution.py:683
  615.4 33.3 %collective-permute-done.36 = bf16[192,384]{1,0:T(8,128)(2,1)S(1)} collective-permute-done((bf16[192,384]{1,0:T(8,128)(2,1)S(1)}, bf16[192,384]{1,0:T(8,128)(2,1)S(1)}, u32[]{:S(2)}, u32[]{:S(2)}) %collective-permute-start.36) | collective-permute-done | bytes 147488 | tf_op jit(solution)/shard_map/ppermute | solution.py:699
  668.3 16.6 %collective-permute-done.108.piece = bf16[3,768,256]{2,1,0:T(8,128)(2,1)} collective-permute-done((bf16[3,768,256]{2,1,0:T(8,128)(2,1)}, bf16[3,768,256]{2,1,0:T(8,128)(2,1)}, u32[]{:S(2)}, u32[]{:S(2)}) %collective-permute-start.108) | collective-permute-done | bytes 1179680 | tf_op jit(solution)/shard_map/ppermute | solution.py:91
  (441 shorter events, 353.6 us)
Async XLA Ops:
  5.0 38.6 %collective-permute-start.1 = (bf16[256,768]{1,0:T(8,128)(2,1)S(1)}, bf16[256,768]{1,0:T(8,128)(2,1)}, u32[]{:S(2)}, u32[]{:S(2)}) collective-permute-start(bf16[256,768]{1,0:T(8,128)(2,1)S(1)} %get-tuple-element.287), channel_id=1, source_target_pairs={{0,1},{1,0},{2,3},{3,2},{4,5},{5,4},{6,7},{7,6},{8,9},{9,8},{10,11... | collective-permute-start | bytes 1179656 | tf_op jit(solution)/shard_map/ppermute | solution.py:84
  5.1 40.6 %collective-permute-start.4 = (bf16[192,2304]{1,0:T(8,128)(2,1)}, bf16[192,2304]{1,0:T(8,128)(2,1)}, u32[]{:S(2)}, u32[]{:S(2)}) collective-permute-start(bf16[192,2304]{1,0:T(8,128)(2,1)} %rest_3_.1), channel_id=1, source_target_pairs={{0,1},{1,0},{2,3},{3,2},{4,5},{5,4},{6,7},{7,6},{8,9},{9,8},{10,11... | collective-permute-start | bytes 2654216 | tf_op jit(solution)/shard_map/ppermute | solution.py:84
  43.7 43.8 %collective-permute-start.13 = (bf16[528,768]{1,0:T(8,128)(2,1)S(1)}, bf16[528,768]{1,0:T(8,128)(2,1)S(1)}, u32[]{:S(2)}, u32[]{:S(2)}) collective-permute-start(bf16[528,768]{1,0:T(8,128)(2,1)S(1)} %fusion.11.rest_4_), channel_id=1, source_target_pairs={{0,2},{1,3},{2,0},{3,1},{4,6},{5,7},{6,4},{7,5},{8,10},{9,11},{10,... | collective-permute-start | bytes 2433032 | tf_op jit(solution)/shard_map/ppermute | solution.py:84
  45.5 44.2 %collective-permute-start.14 = (bf16[528,768]{1,0:T(8,128)(2,1)S(1)}, bf16[528,768]{1,0:T(8,128)(2,1)S(1)}, u32[]{:S(2)}, u32[]{:S(2)}) collective-permute-start(bf16[528,768]{1,0:T(8,128)(2,1)S(1)} %fusion.11.rest_4_), channel_id=1, source_target_pairs={{0,1},{1,0},{2,3},{3,2},{4,5},{5,4},{6,7},{7,6},{8,9},{9,8},{10,11... | collective-permute-start | bytes 2433032 | tf_op jit(solution)/shard_map/ppermute | solution.py:84
  45.6 42.3 %collective-permute-start.56 = (bf16[528,768]{1,0:T(8,128)(2,1)S(1)}, bf16[528,768]{1,0:T(8,128)(2,1)S(1)}, u32[]{:S(2)}, u32[]{:S(2)}) collective-permute-start(bf16[528,768]{1,0:T(8,128)(2,1)S(1)} %fusion.11.rest_4_), channel_id=1, source_target_pairs={{0,8},{8,16},{16,24},{24,28},{28,20},{20,12},{12,4},{4,0},{1,9},{9... | collective-permute-start | bytes 2433032 | tf_op jit(solution)/shard_map/ppermute | solution.py:91
  108.6 36.1 %collective-permute-start.90 = (bf16[528,768]{1,0:T(8,128)(2,1)}, bf16[528,768]{1,0:T(8,128)(2,1)}, u32[]{:S(2)}, u32[]{:S(2)}) collective-permute-start(bf16[528,768]{1,0:T(8,128)(2,1)} %collective-permute-done.57.rest_4_), channel_id=1, source_target_pairs={{0,1},{1,0},{2,3},{3,2},{4,5},{5,4},{6,7},{7,6},{8,9},{9,8},{10,11... | collective-permute-start | bytes 2433032 | tf_op jit(solution)/shard_map/ppermute | solution.py:84
  183.2 44.2 %collective-permute-start.92 = (bf16[528,768]{1,0:T(8,128)(2,1)}, bf16[528,768]{1,0:T(8,128)(2,1)}, u32[]{:S(2)}, u32[]{:S(2)}) collective-permute-start(bf16[528,768]{1,0:T(8,128)(2,1)} %collective-permute-done.40.rest_0_), channel_id=1, source_target_pairs={{0,1},{1,0},{2,3},{3,2},{4,5},{5,4},{6,7},{7,6},{8,9},{9,8},{10,11... | collective-permute-start | bytes 2433032 | tf_op jit(solution)/shard_map/ppermute | solution.py:84
  184.3 44.8 %collective-permute-start.41 = (bf16[528,768]{1,0:T(8,128)(2,1)}, bf16[528,768]{1,0:T(8,128)(2,1)}, u32[]{:S(2)}, u32[]{:S(2)}) collective-permute-start(bf16[528,768]{1,0:T(8,128)(2,1)} %collective-permute-done.40.rest_0_), channel_id=1, source_target_pairs={{0,8},{8,16},{16,24},{24,28},{28,20},{20,12},{12,4},{4,0},{1,9},{9... | collective-permute-start | bytes 2433032 | tf_op jit(solution)/shard_map/ppermute | solution.py:91
  185.8 43.2 %collective-permute-start.87 = (bf16[528,768]{1,0:T(8,128)(2,1)S(1)}, bf16[528,768]{1,0:T(8,128)(2,1)}, u32[]{:S(2)}, u32[]{:S(2)}) collective-permute-start(bf16[528,768]{1,0:T(8,128)(2,1)S(1)} %collective-permute-done.65.rest_5_), channel_id=1, source_target_pairs={{0,1},{1,0},{2,3},{3,2},{4,5},{5,4},{6,7},{7,6},{8,9},{9,8},{10,11... | collective-permute-start | bytes 2433032 | tf_op jit(solution)/shard_map/ppermute | solution.py:84
  286.3 36.9 %collective-permute-start.79 = (bf16[528,768]{1,0:T(8,128)(2,1)S(1)}, bf16[528,768]{1,0:T(8,128)(2,1)S(1)}, u32[]{:S(2)}, u32[]{:S(2)}) collective-permute-start(bf16[528,768]{1,0:T(8,128)(2,1)S(1)} %collective-permute-done.67.rest_5_), channel_id=1, source_target_pairs={{0,1},{1,0},{2,3},{3,2},{4,5},{5,4},{6,7},{7,6},{8,9},{9,8},{10,11... | collective-permute-start | bytes 2433032 | tf_op jit(solution)/shard_map/ppermute | solution.py:84
  286.3 36.9 %collective-permute-start.68 = (bf16[528,768]{1,0:T(8,128)(2,1)S(1)}, bf16[528,768]{1,0:T(8,128)(2,1)}, u32[]{:S(2)}, u32[]{:S(2)}) collective-permute-start(bf16[528,768]{1,0:T(8,128)(2,1)S(1)} %collective-permute-done.67.rest_5_), channel_id=1, source_target_pairs={{0,4},{8,0},{16,8},{24,16},{28,24},{20,28},{12,20},{4,12},{1,5},{9... | collective-permute-start | bytes 2433032 | tf_op jit(solution)/shard_map/ppermute | solution.py:91
  369.0 41.6 %collective-permute-start.76 = (bf16[528,768]{1,0:T(8,128)(2,1)}, bf16[528,768]{1,0:T(8,128)(2,1)S(1)}, u32[]{:S(2)}, u32[]{:S(2)}) collective-permute-start(bf16[528,768]{1,0:T(8,128)(2,1)} %collective-permute-done.44.rest_0_), channel_id=1, source_target_pairs={{0,1},{1,0},{2,3},{3,2},{4,5},{5,4},{6,7},{7,6},{8,9},{9,8},{10,11... | collective-permute-start | bytes 2433032 | tf_op jit(solution)/shard_map/ppermute | solution.py:84
  369.1 41.7 %collective-permute-start.77 = (bf16[528,768]{1,0:T(8,128)(2,1)}, bf16[528,768]{1,0:T(8,128)(2,1)S(1)}, u32[]{:S(2)}, u32[]{:S(2)}) collective-permute-start(bf16[528,768]{1,0:T(8,128)(2,1)} %collective-permute-done.51.rest_1_), channel_id=1, source_target_pairs={{0,1},{1,0},{2,3},{3,2},{4,5},{5,4},{6,7},{7,6},{8,9},{9,8},{10,11... | collective-permute-start | bytes 2433032 | tf_op jit(solution)/shard_map/ppermute | solution.py:84
  375.5 35.8 %collective-permute-start.72 = (bf16[528,768]{1,0:T(8,128)(2,1)}, bf16[528,768]{1,0:T(8,128)(2,1)S(1)}, u32[]{:S(2)}, u32[]{:S(2)}) collective-permute-start(bf16[528,768]{1,0:T(8,128)(2,1)} %collective-permute-done.45.rest_0_), channel_id=1, source_target_pairs={{0,1},{1,0},{2,3},{3,2},{4,5},{5,4},{6,7},{7,6},{8,9},{9,8},{10,11... | collective-permute-start | bytes 2433032 | tf_op jit(solution)/shard_map/ppermute | solution.py:84
  375.5 35.9 %collective-permute-start.46 = (bf16[528,768]{1,0:T(8,128)(2,1)}, bf16[528,768]{1,0:T(8,128)(2,1)S(1)}, u32[]{:S(2)}, u32[]{:S(2)}) collective-permute-start(bf16[528,768]{1,0:T(8,128)(2,1)} %collective-permute-done.45.rest_0_), channel_id=1, source_target_pairs={{0,8},{8,16},{16,24},{24,28},{28,20},{20,12},{12,4},{4,0},{1,9},{9... | collective-permute-start | bytes 2433032 | tf_op jit(solution)/shard_map/ppermute | solution.py:91
  487.6 52.6 %collective-permute-start.31 = (bf16[192,3072]{1,0:T(8,128)(2,1)}, bf16[192,3072]{1,0:T(8,128)(2,1)}, u32[]{:S(2)}, u32[]{:S(2)}) collective-permute-start(bf16[192,3072]{1,0:T(8,128)(2,1)} %get-tuple-element.283), channel_id=1, source_target_pairs={{0,1},{1,0},{2,3},{3,2},{4,5},{5,4},{6,7},{7,6},{8,9},{9,8},{10,11... | collective-permute-start | bytes 3538952 | tf_op jit(solution)/shard_map/ppermute | solution.py:84
  548.5 57.1 %collective-permute-start.106 = (bf16[3,768,256]{2,1,0:T(8,128)(2,1)}, bf16[3,768,256]{2,1,0:T(8,128)(2,1)}, u32[]{:S(2)}, u32[]{:S(2)}) collective-permute-start(bf16[3,768,256]{2,1,0:T(8,128)(2,1)} %collective-permute-done.105.piece), channel_id=1, source_target_pairs={{0,8},{8,16},{16,24},{24,28},{28,20},{20,12},{12,4},{4,0},{1,9},{9... | collective-permute-start | bytes 3538952 | tf_op jit(solution)/shard_map/ppermute | solution.py:91
  566.9 40.8 %collective-permute-start.99 = (bf16[3,768,256]{2,1,0:T(8,128)(2,1)S(1)}, bf16[3,768,256]{2,1,0:T(8,128)(2,1)S(1)}, u32[]{:S(2)}, u32[]{:S(2)}) collective-permute-start(bf16[3,768,256]{2,1,0:T(8,128)(2,1)S(1)} %collective-permute-done.98.piece), channel_id=1, source_target_pairs={{0,4},{8,0},{16,8},{24,16},{28,24},{20,28},{12,20},{4,12},{1,5},{9... | collective-permute-start | bytes 3538952 | tf_op jit(solution)/shard_map/ppermute | solution.py:91
  605.6 49.9 %collective-permute-start.107 = (bf16[3,768,256]{2,1,0:T(8,128)(2,1)}, bf16[3,768,256]{2,1,0:T(8,128)(2,1)}, u32[]{:S(2)}, u32[]{:S(2)}) collective-permute-start(bf16[3,768,256]{2,1,0:T(8,128)(2,1)} %collective-permute-done.106.piece), channel_id=1, source_target_pairs={{0,8},{8,16},{16,24},{24,28},{28,20},{20,12},{12,4},{4,0},{1,9},{9... | collective-permute-start | bytes 3538952 | tf_op jit(solution)/shard_map/ppermute | solution.py:91
  607.7 49.5 %collective-permute-start.100 = (bf16[3,768,256]{2,1,0:T(8,128)(2,1)S(1)}, bf16[3,768,256]{2,1,0:T(8,128)(2,1)S(1)}, u32[]{:S(2)}, u32[]{:S(2)}) collective-permute-start(bf16[3,768,256]{2,1,0:T(8,128)(2,1)S(1)} %collective-permute-done.99.piece), channel_id=1, source_target_pairs={{0,4},{8,0},{16,8},{24,16},{28,24},{20,28},{12,20},{4,12},{1,5},{9... | collective-permute-start | bytes 3538952 | tf_op jit(solution)/shard_map/ppermute | solution.py:91
  608.3 40.4 %collective-permute-start.36 = (bf16[192,384]{1,0:T(8,128)(2,1)S(1)}, bf16[192,384]{1,0:T(8,128)(2,1)S(1)}, u32[]{:S(2)}, u32[]{:S(2)}) collective-permute-start(bf16[192,384]{1,0:T(8,128)(2,1)S(1)} %select_convert_fusion.2), channel_id=1, source_target_pairs={{0,16},{4,20},{8,24},{12,28},{16,0},{20,4},{24,8},{28,12},{1,17},{... | collective-permute-start | bytes 442376 | tf_op jit(solution)/shard_map/ppermute | solution.py:699
  613.8 36.4 %collective-permute-start.28 = (f32[48,768]{1,0:T(8,128)S(1)}, f32[48,768]{1,0:T(8,128)S(1)}, u32[]{:S(2)}, u32[]{:S(2)}) collective-permute-start(f32[48,768]{1,0:T(8,128)S(1)} %add.226), channel_id=1, source_target_pairs={{0,16},{4,20},{8,24},{12,28},{16,0},{20,4},{24,8},{28,12},{1,17},{... | collective-permute-start | bytes 442376 | tf_op jit(solution)/shard_map/ppermute | solution.py:683
  684.8 49.4 %collective-permute-start.109 = (bf16[3,768,256]{2,1,0:T(8,128)(2,1)}, bf16[3,768,256]{2,1,0:T(8,128)(2,1)S(1)}, u32[]{:S(2)}, u32[]{:S(2)}) collective-permute-start(bf16[3,768,256]{2,1,0:T(8,128)(2,1)} %collective-permute-done.108.piece), channel_id=1, source_target_pairs={{0,8},{8,16},{16,24},{24,28},{28,20},{20,12},{12,4},{4,0},{1,9},{9... | collective-permute-start | bytes 3538952 | tf_op jit(solution)/shard_map/ppermute | solution.py:91
  687.3 50.8 %collective-permute-start.102 = (bf16[3,768,256]{2,1,0:T(8,128)(2,1)}, bf16[3,768,256]{2,1,0:T(8,128)(2,1)}, u32[]{:S(2)}, u32[]{:S(2)}) collective-permute-start(bf16[3,768,256]{2,1,0:T(8,128)(2,1)} %collective-permute-done.101.piece), channel_id=1, source_target_pairs={{0,4},{8,0},{16,8},{24,16},{28,24},{20,28},{12,20},{4,12},{1,5},{9... | collective-permute-start | bytes 3538952 | tf_op jit(solution)/shard_map/ppermute | solution.py:91
  (161 other events, 3687.2 us)

commit v2 on v1

--- a/solution.py
+++ b/solution.py
@@ -30,6 +30,18 @@
 BF16 = jnp.bfloat16
 VMEM_LIMIT = 56 * 2**20
 SMALL_ROWS = 40
+COST = {"column_rows": 4.0}
+W_KEYS = 1
+SC_DENSE = 1
+W_DENSE = 1
+SC_SMALL = 0
+W_PACK = 0
+W_NEAR = 1
+W_FRONT = 1
+W_RING = 0
+W_LOCAL = 1
+W_SLICE = 0
+W_BACK = 1
 
 
 def mm(left, right):
@@ -53,9 +65,10 @@
     return jax.ShapeDtypeStruct(dims, dtype)
 
 
-def estimate(flops, bytes_accessed):
+def estimate(name, flops, bytes_accessed):
+    scale = COST.get(name, 1.0)
     return pl.CostEstimate(
-        flops=int(flops), bytes_accessed=int(bytes_accessed), transcendentals=0
+        flops=int(scale * flops), bytes_accessed=int(scale * bytes_accessed), transcendentals=0
     )
 
 
@@ -63,20 +76,35 @@
     return pltpu.CompilerParams(vmem_limit_bytes=VMEM_LIMIT)
 
 
-def whole_call(kernel, name, scalars, arrays, outs, flops, scratch=()):
+def without(kernel, first, count):
+    if not count:
+        return kernel
+
+    def run(*refs):
+        return kernel(*refs[:first], *refs[first + count :])
+
+    return run
+
+
+HELD = pl.BlockSpec(memory_space=pl.ANY)
+
+
+def whole_call(kernel, name, scalars, arrays, outs, flops, scratch=(), waits=()):
     vmem = pl.BlockSpec(memory_space=pltpu.VMEM)
     moved = sum(a.size * a.dtype.itemsize for a in arrays)
     moved += sum(math.prod(o.shape) * np.dtype(o.dtype).itemsize for o in outs)
     return pl.pallas_call(
-        kernel,
+        without(kernel, 1 + len(arrays), len(waits)),
         out_shape=tuple(outs),
-        in_specs=[pl.BlockSpec(memory_space=pltpu.SMEM)] + [vmem] * len(arrays),
+        in_specs=[pl.BlockSpec(memory_space=pltpu.SMEM)]
+        + [vmem] * len(arrays)
+        + [HELD] * len(waits),
         out_specs=tuple([vmem] * len(outs)),
         scratch_shapes=list(scratch),
         compiler_params=params(),
-        cost_estimate=estimate(flops, moved),
+        cost_estimate=estimate(name, flops, moved),
         name=name,
-    )(scalars, *arrays)
+    )(scalars, *arrays, *waits)
 
 
 def xor_permute(value, offset):
@@ -101,9 +129,83 @@
     return pieces
 
 
-def projection_kernel(group, scal, gain, tok, partner, *rest):
+def lanes_of(values):
+    rows, width = values.shape
+    return jnp.concatenate([values, jnp.zeros((rows, LANES - width), values.dtype)], axis=1)
+
+
+def prepare_kernel(routes, prev, cot, router, resid, const_w, const_v, prompt, *rest):
+    prompt_out, block, slots_out, routes_out, prev_out, previous_out, mixers_out, turned_out, resid_out, vectors_out = rest
+    prompt_out[...] = prompt[:P_DEV, :]
+    lane = lax.broadcasted_iota(jnp.int32, (1, LANES), 1)
+    ids = routes[...]
+    named = (ids[:, 0:1] == lane) | (ids[:, 1:2] == lane)
+    row = lax.broadcasted_iota(jnp.int32, (TOK_DEV, 1), 0)
+    col = lax.broadcasted_iota(jnp.int32, (1, TOK_DEV), 1)
+    before = jnp.where(col < row, 1.0, 0.0).astype(BF16)
+    slots = jnp.where(named, mm(before, jnp.where(named, 1.0, 0.0).astype(BF16)), -1.0)
+    slots_out[...] = slots
+    block[:TOK_DEV, :] = cot[...]
+    block[TOK_DEV:, :TOK_DEV] = jnp.transpose(slots)[:EXT, :].astype(BF16)
+    block[TOK_DEV:, TOK_DEV:] = jnp.full((EXT, D - TOK_DEV), -1, BF16)
+    routes_out[...] = jnp.where(lane == 0, ids[:, 0:1], jnp.where(lane == 1, ids[:, 1:2], 0))
+    wide = lanes_of(prev[...])
+    prev_out[...] = wide
+    square = jnp.concatenate(
+        [lanes_of(resid[...].astype(F32)), jnp.zeros((LANES - IDS, LANES), F32)], axis=0
+    )
+    turned_resid = jnp.transpose(square).astype(BF16)
+    resid_out[...] = turned_resid
+    high, rest_of = split(wide)
+    low = (wide - high.astype(F32) - rest_of.astype(F32)).astype(BF16)
+    resid_low = square.astype(BF16)
+    previous_out[...] = mm(high, resid_low) + mm(rest_of, resid_low) + mm(low, resid_low)
+    mixers = jnp.concatenate(
+        [
+            router[...].astype(F32),
+            const_w[0].astype(F32),
+            const_w[1].astype(F32),
+            jnp.zeros((D, LANES - IDS - 4), F32),
+        ],
+        axis=1,
+    )
+    mixers_out[...] = mixers.astype(BF16)
+    turned_out[...] = jnp.transpose(mixers).astype(BF16)
+    vectors_out[...] = jnp.concatenate([const_v[...].astype(F32), jnp.zeros((6, D), F32)], axis=0)
+
+
+def prepare(routes, prev, cot, router, resid, const_w, const_v, tok, waits):
+    vmem = pl.BlockSpec(memory_space=pltpu.VMEM)
+    arrays = (routes, prev, cot, router, resid, const_w, const_v, tok)
+    outs = (
+        shape_of((P_DEV, D), BF16),
+        shape_of((BLOCK, D), BF16),
+        shape_of((TOK_DEV, LANES), F32),
+        shape_of((TOK_DEV, LANES), jnp.int32),
+        shape_of((TOK_DEV, LANES), F32),
+        shape_of((TOK_DEV, LANES), F32),
+        shape_of((D, LANES), BF16),
+        shape_of((LANES, D), BF16),
+        shape_of((LANES, LANES), BF16),
+        shape_of((8, D), F32),
+    )
+    return pl.pallas_call(
+        without(prepare_kernel, len(arrays), len(waits)),
+        out_shape=outs,
+        in_specs=[vmem] * len(arrays) + [HELD] * len(waits),
+        out_specs=tuple([vmem] * len(outs)),
+        compiler_params=params(),
+        cost_estimate=estimate("prepare", 2 * TOK_DEV * TOK_DEV * LANES, 8 * TOK_DEV * D),
+        name="prepare",
+    )(*arrays, *waits)
+
+
+def projection_kernel(group, scal, gain, tok, *rest):
     prompts, shards = rest[: group - 1], rest[group - 1 : 2 * group - 1]
-    q_out, kp_out, vp_out, kc_out, vc_out, w_out, n_out = rest[2 * group - 1 :]
+    passed = (len(rest) - 2 * group + 1 - 7) // 2
+    q_out, kp_out, vp_out, kc_out, vc_out, w_out, n_out = rest[2 * group - 1 + passed : 2 * group + 6 + passed]
+    for at in range(passed):
+        rest[2 * group + 6 + passed + at][...] = rest[2 * group - 1 + at][...]
     rows = D // group
     for offset in range(group):
         start = pl.multiple_of(scal[offset] * rows, rows)
@@ -123,11 +225,11 @@
     vp_out[pl.ds(start, P_DEV), :] = kv[:P_DEV, D:]
     kc_out[:P_DEV, :] = kv[P_DEV:, :D]
     vc_out[:P_DEV, :] = kv[P_DEV:, D:]
-    kv = mm(normed(partner[...]), w_out[:, D:]).astype(BF16)
+    kv = mm(normed(prompts[0][P_DEV:, :]), w_out[:, D:]).astype(BF16)
     kc_out[P_DEV:, :] = kv[:, :D]
     vc_out[P_DEV:, :] = kv[:, D:]
     for offset in range(1, group):
-        kv = mm(normed(prompts[offset - 1][...]), w_out[:, D:]).astype(BF16)
+        kv = mm(normed(prompts[offset - 1][:P_DEV, :]), w_out[:, D:]).astype(BF16)
         start = pl.multiple_of(scal[offset] * P_DEV, P_DEV)
         kp_out[pl.ds(start, P_DEV), :] = kv[:, :D]
         vp_out[pl.ds(start, P_DEV), :] = kv[:, D:]
@@ -172,21 +274,22 @@
         lse_ref[rows, :] = jnp.where(lane < HEAD_DIM, logs[0], logs[1])
 
 
-def attention(scal, q, kp, vp, kc, vc, group):
+def attention(scal, q, kp, vp, kc, vc, group, waits):
     prompt = kp.shape[0]
     column = lambda rows: pl.BlockSpec((rows, LANES), lambda p: (0, p))
     flops = 4 * 2 * HEADS * P_DEV * (2 * prompt + 2 * P_DEV) * LANES
     return pl.pallas_call(
-        partial(attention_kernel, group),
+        without(partial(attention_kernel, group), 6, len(waits)),
         out_shape=(shape_of((TOK_DEV, D), F32), shape_of((TOK_DEV, D), F32)),
         grid=(PAIRS,),
         in_specs=[pl.BlockSpec(memory_space=pltpu.SMEM)]
-        + [column(n) for n in (TOK_DEV, prompt, prompt, 2 * P_DEV, 2 * P_DEV)],
+        + [column(n) for n in (TOK_DEV, prompt, prompt, 2 * P_DEV, 2 * P_DEV)]
+        + [HELD] * len(waits),
         out_specs=(column(TOK_DEV), column(TOK_DEV)),
         compiler_params=params(),
-        cost_estimate=estimate(flops, 10 * TOK_DEV * D * 2),
+        cost_estimate=estimate("attention_forward", flops, 10 * TOK_DEV * D * 2),
         name="attention_forward",
-    )(scal, q, kp, vp, kc, vc)
+    )(scal, q, kp, vp, kc, vc, *waits)
 
 
 def attention_back_kernel(group, scal, q_ref, kp_ref, vp_ref, kc_ref, vc_ref, do_ref, o_ref, lse_ref, *rest):
@@ -257,13 +360,13 @@
     other_ref[1] = dvc_acc[P_DEV:, :].astype(BF16)
 
 
-def attention_back(scal, q, kp, vp, kc, vc, do, o32, lse, group):
+def attention_back(scal, q, kp, vp, kc, vc, do, o32, lse, group, waits):
     prompt = kp.shape[0]
     column = lambda rows: pl.BlockSpec((rows, LANES), lambda p: (0, p))
     double = pl.BlockSpec((2, P_DEV, LANES), lambda p: (0, 0, p))
     flops = 10 * 2 * HEADS * P_DEV * (2 * prompt + 2 * P_DEV) * LANES
     return pl.pallas_call(
-        partial(attention_back_kernel, group),
+        without(partial(attention_back_kernel, group), 9, len(waits)),
         out_shape=(
             shape_of((TOK_DEV, D), BF16),
             *[shape_of((2, P_DEV, D), BF16)] * group,
@@ -275,7 +378,8 @@
         + [
             column(n)
             for n in (TOK_DEV, prompt, prompt, 2 * P_DEV, 2 * P_DEV, TOK_DEV, TOK_DEV, TOK_DEV)
-        ],
+        ]
+        + [HELD] * len(waits),
         out_specs=(column(TOK_DEV), *[double] * group, double, double),
         scratch_shapes=[
             pltpu.VMEM((prompt, LANES), F32),
@@ -284,9 +388,9 @@
             pltpu.VMEM((2 * P_DEV, LANES), F32),
         ],
         compiler_params=params(),
-        cost_estimate=estimate(flops, 20 * TOK_DEV * D * 2),
+        cost_estimate=estimate("attention_backward", flops, 20 * TOK_DEV * D * 2),
         name="attention_backward",
-    )(scal, q, kp, vp, kc, vc, do, o32, lse)
+    )(scal, q, kp, vp, kc, vc, do, o32, lse, *waits)
 
 
 def columns(values):
@@ -355,64 +459,102 @@
     blk_out[TOK_DEV:, TOK_DEV:] = jnp.zeros((EXT, D - TOK_DEV), BF16)
 
 
-def rows_kernel(group, per, share, aliased, scal, *rest):
-    hidden = rest[:group]
-    grads = rest[group : 2 * group]
-    outs = rest[2 * group + aliased :]
-    x_out, s_out, xt_out, st_out, slots, gates = outs
+def fill_rows(hidden, grads, experts, slots, gates, chooser, scales):
     slot = lax.broadcasted_iota(jnp.int32, (CAP, 1), 0).astype(F32)
+    slots[...] = grads[TOK_DEV:, :TOK_DEV].astype(F32)
+    pair = hidden[TOK_DEV:, :TOK_DEV].astype(F32)
+    gates[...] = pair[:EXPERTS, :] + pair[EXPERTS:, :]
+    for at, expert in enumerate(experts):
+        picked = slots[pl.ds(expert, 1), :] == slot
+        span = pl.ds(at * CAP, CAP)
+        chooser[span, :] = jnp.where(picked, 1.0, 0.0).astype(BF16)
+        scales[span, :] = jnp.sum(
+            jnp.where(picked, gates[pl.ds(expert, 1), :], 0.0), axis=1, keepdims=True
+        )
+    x = mm(chooser[...], hidden[:TOK_DEV, :]).astype(BF16)
+    s = (mm(chooser[...], grads[:TOK_DEV, :]) * scales[...]).astype(BF16)
+    return x, s
+
+
+def row_scratch(experts):
+    return (
+        pltpu.VMEM((EXT, TOK_DEV), F32),
+        pltpu.VMEM((EXPERTS, TOK_DEV), F32),
+        pltpu.VMEM((experts * CAP, TOK_DEV), BF16),
+        pltpu.VMEM((experts * CAP, 1), F32),
+    )
+
+
+def near_rows_kernel(group, per, share, scal, *rest):
+    hidden, grads = rest[:group], rest[group : 2 * group]
+    x_out, s_out = rest[2 * group : 2 * group + 2]
+    experts = [(scal[0] * per + member) // share for member in range(per)]
     for at in range(group):
-        slots[...] = grads[at][TOK_DEV:, :TOK_DEV].astype(F32)
-        pair = hidden[at][TOK_DEV:, :TOK_DEV].astype(F32)
-        gates[...] = pair[:EXPERTS, :] + pair[EXPERTS:, :]
+        x, s = fill_rows(hidden[at], grads[at], experts, *rest[2 * group + 2 :])
         for member in range(per):
-            expert = (scal[0] * per + member) // share
-            picked = slots[pl.ds(expert, 1), :] == slot
-            gate = jnp.sum(
-                jnp.where(picked, gates[pl.ds(expert, 1), :], 0.0), axis=1, keepdims=True
-            )
-            chooser = jnp.where(picked, 1.0, 0.0).astype(BF16)
-            span = pl.ds(at * CAP, CAP)
-            x_out[0, member, span, :] = mm(chooser, hidden[at][:TOK_DEV, :]).astype(BF16)
-            s_out[0, member, span, :] = (mm(chooser, grads[at][:TOK_DEV, :]) * gate).astype(BF16)
-    for member in range(per):
-        xt_out[0, member] = jnp.transpose(x_out[0, member])
-        st_out[0, member] = jnp.transpose(s_out[0, member])
-
-
-def expert_rows(scal, hidden, grads, at, count, stacks, group, per, share):
-    rows = group * CAP
-    natural, turned = (count, per, rows, D), (count, per, D, rows)
-    block = lambda dims: pl.BlockSpec((1, *dims[1:]), lambda i: (at, 0, 0, 0))
-    vmem = pl.BlockSpec((BLOCK, D), lambda i: (0, 0))
-    held = [pl.BlockSpec(memory_space=pl.ANY)] * len(stacks)
-    first = 1 + 2 * group
+            part = slice(member * CAP, (member + 1) * CAP)
+            x_out[member, at * CAP : (at + 1) * CAP, :] = x[part]
+            s_out[member, at * CAP : (at + 1) * CAP, :] = s[part]
+
+
+def near_rows(scal, hidden, grads, group, per, share, waits):
+    dims = (per, group * CAP, D)
+    return whole_call(
+        partial(near_rows_kernel, group, per, share),
+        "near_rows",
+        scal,
+        [*hidden, *grads],
+        [shape_of(dims, BF16), shape_of(dims, BF16)],
+        4 * group * per * CAP * TOK_DEV * D,
+        row_scratch(per),
+        waits,
+    )
+
+
+def column_rows_kernel(many, *refs):
+    x_out, s_out = refs[-6:-4]
+    for at in range(many):
+
+        @pl.when(pl.program_id(0) == at)
+        def _():
+            x, s = fill_rows(refs[at], refs[many + at], range(EXPERTS), *refs[-4:])
+            x_out[...] = x.reshape(1, EXPERTS, CAP, D)
+            s_out[...] = s.reshape(1, EXPERTS, CAP, D)
+
+
+def column_rows(hidden, grads, first, count, stacks, waits):
+    many = len(hidden)
+    dims = (count, EXPERTS, CAP, D)
+    block = pl.BlockSpec((1, *dims[1:]), lambda i: (first + i, 0, 0, 0))
+    token = pl.BlockSpec((BLOCK, D), lambda i: (0, 0))
     return pl.pallas_call(
-        partial(rows_kernel, group, per, share, len(stacks)),
-        out_shape=tuple(shape_of(d, BF16) for d in (natural, natural, turned, turned)),
-        grid=(1,),
-        in_specs=[pl.BlockSpec(memory_space=pltpu.SMEM)] + [vmem] * (2 * group) + held,
-        out_specs=tuple(block(d) for d in (natural, natural, turned, turned)),
-        scratch_shapes=[pltpu.VMEM((EXT, TOK_DEV), F32), pltpu.VMEM((EXPERTS, TOK_DEV), F32)],
-        input_output_aliases={first + n: n for n in range(len(stacks))},
+        partial(column_rows_kernel, many),
+        out_shape=(shape_of(dims, BF16), shape_of(dims, BF16)),
+        grid=(many,),
+        in_specs=[token] * (2 * many) + [HELD] * (len(stacks) + len(waits)),
+        out_specs=(block, block),
+        scratch_shapes=list(row_scratch(EXPERTS)),
+        input_output_aliases={2 * many + n: n for n in range(len(stacks))},
         compiler_params=params(),
-        cost_estimate=estimate(
-            4 * group * per * CAP * TOK_DEV * D, 2 * (2 * group * BLOCK + 4 * per * rows) * D
+        cost_estimate=estimate("column_rows",
+            4 * many * EXPERTS * CAP * TOK_DEV * D, 4 * many * (BLOCK + EXPERTS * CAP) * D
         ),
-        name="expert_rows",
-    )(scal, *hidden, *grads, *stacks)
+        name="column_rows",
+    )(*hidden, *grads, *stacks, *waits)
 
 
 def sigmoid(values):
     return 0.5 * jnp.tanh(0.5 * values) + 0.5
 
 
-def expert_terms(x, s, gate_w, up_w, down_w):
-    act_a, act_b = mm(x, gate_w), mm(x, up_w)
+def add_low(left, right):
+    return (left.astype(F32) + right.astype(F32)).astype(BF16)
+
+
+def expert_terms(act_a, act_b, hidden_grad):
     sig = sigmoid(act_a)
     silu = act_a * sig
     hidden = (silu * act_b).astype(BF16)
-    hidden_grad = mm_nt(s, down_w)
     grad_a = (hidden_grad * act_b * (sig + silu * (1.0 - sig))).astype(BF16)
     grad_b = (hidden_grad * silu).astype(BF16)
     return hidden, grad_a, grad_b
@@ -421,12 +563,13 @@
 def expert_kernel(group, offsets, x_ref, s_ref, wg, wu, wd, *rest):
     outs, out_acc, in_acc = rest[:group], rest[group], rest[group + 1]
     step = pl.program_id(0)
-    rows = x_ref.shape[2]
+    rows = x_ref.shape[1]
     chunk = min(rows, 512)
     for start in range(0, rows, chunk):
         span = pl.ds(start, chunk)
+        x = x_ref[0, span, :]
         hidden, grad_a, grad_b = expert_terms(
-            x_ref[0, 0, span, :], s_ref[0, 0, span, :], wg[...], wu[...], wd[...]
+            mm(x, wg[...]), mm(x, wu[...]), mm_nt(s_ref[0, span, :], wd[...])
         )
         out = mm(hidden, wd[...])
         back = mm_nt(grad_a, wg[...]) + mm_nt(grad_b, wu[...])
@@ -448,105 +591,99 @@
             outs[offsets[at]][1] = in_acc[at * CAP : (at + 1) * CAP, :].astype(BF16)
 
 
-def local_expert(x, s, gate_w, up_w, down_w, member, offsets, group, per):
+def local_expert(x, s, gate_w, up_w, down_w, member, offsets, group, per, waits):
     width = gate_w.shape[1] // per
     tile = min(512, width)
     steps = width // tile
     rows = group * CAP
-    side = pl.BlockSpec((1, 1, rows, D), lambda t: (0, member, 0, 0))
+    side = pl.BlockSpec((1, rows, D), lambda t: (member, 0, 0))
     wide = pl.BlockSpec((D, tile), lambda t: (0, member * steps + t))
     tall = pl.BlockSpec((tile, D), lambda t: (member * steps + t, 0))
     piece = pl.BlockSpec((2, CAP, D), lambda t: (0, 0, 0))
     return pl.pallas_call(
-        partial(expert_kernel, group, offsets),
+        without(partial(expert_kernel, group, offsets), 5, len(waits)),
         out_shape=tuple([shape_of((2, CAP, D), BF16)] * group),
         grid=(steps,),
-        in_specs=[side, side, wide, wide, tall],
+        in_specs=[side, side, wide, wide, tall] + [HELD] * len(waits),
         out_specs=tuple([piece] * group),
         scratch_shapes=[pltpu.VMEM((rows, D), F32), pltpu.VMEM((rows, D), F32)],
         compiler_params=params(),
-        cost_estimate=estimate(12 * rows * D * width, 6 * D * width + 8 * rows * D),
+        cost_estimate=estimate("local_expert", 12 * rows * D * width, 6 * D * width + 8 * rows * D),
         name="local_expert",
-    )(x, s, gate_w, up_w, down_w)
-
-
-def slice_kernel(mode, at_ref, x, s, xt, st, wg, wu, wd, *rest):
-    outs, (gate_acc, up_acc, down_acc) = rest[:-3], rest[-3:]
-    step = pl.program_id(1)
-    batches, rows = x.shape[0], x.shape[2]
-    terms = [
-        expert_terms(x[n, 0], s[n, 0], wg[...], wu[...], wd[...]) for n in range(batches)
-    ]
-    gate = sum(mm(xt[n, 0], terms[n][1]) for n in range(batches))
-    up = sum(mm(xt[n, 0], terms[n][2]) for n in range(batches))
-    down = sum(mm(st[n, 0], terms[n][0]) for n in range(batches))
-
-    @pl.when(step == 0)
-    def _():
-        gate_acc[...] = gate
-        up_acc[...] = up
-        down_acc[...] = down
-
-    @pl.when(step > 0)
-    def _():
-        gate_acc[...] += gate
-        up_acc[...] += up
-        down_acc[...] += down
-
-    @pl.when(step == pl.num_programs(1) - 1)
-    def _():
-        if mode == "pack":
-            outs[0][0] = gate_acc[...].astype(BF16)
-            outs[0][1] = up_acc[...].astype(BF16)
-            outs[0][2] = down_acc[...].astype(BF16)
-        else:
-            outs[0][...] = gate_acc[...]
-            outs[1][...] = up_acc[...]
-            outs[2][...] = jnp.transpose(down_acc[...])
-
-
-def weight_slices(at, stacks, weights, member, tile, tiles, mode, batches, per):
-    x, s, xt, st = stacks
-    count, rows = x.shape[0], x.shape[2]
-    steps = count // batches
-    natural = pl.BlockSpec((batches, 1, rows, D), lambda t, d, ref: (d, member, 0, 0))
-    turned = pl.BlockSpec((batches, 1, D, rows), lambda t, d, ref: (d, member, 0, 0))
-    wide = pl.BlockSpec((D, tile), lambda t, d, ref: (0, ref[0] + t))
-    tall = pl.BlockSpec((tile, D), lambda t, d, ref: (ref[0] + t, 0))
-    units = weights[0].shape[1]
-    if mode == "pack":
-        outs = (shape_of((3, D, tile), BF16),)
-        specs = (pl.BlockSpec((3, D, tile), lambda t, d, ref: (0, 0, 0)),)
-    else:
-        outs = (shape_of((D, units), F32), shape_of((D, units), F32), shape_of((units, D), F32))
-        specs = (wide, wide, tall)
+    )(x, s, gate_w, up_w, down_w, *waits)
+
+
+def pack_kernel(at_ref, wg, wu, wd, out):
+    out[0, 0] = jnp.transpose(wg[...])
+    out[0, 1] = jnp.transpose(wu[...])
+    out[0, 2] = wd[...]
+
+
+def pack_weights(at, weights, member, per, count, waits):
+    tile = weights[0].shape[1] // per // count
+    wide = pl.BlockSpec((D, tile), lambda m, ref: (0, ref[0] + member * count))
+    tall = pl.BlockSpec((tile, D), lambda m, ref: (ref[0] + member * count, 0))
     return pl.pallas_call(
-        partial(slice_kernel, mode),
-        out_shape=outs,
+        without(pack_kernel, 4, len(waits)),
+        out_shape=shape_of((1, 3, tile, D), BF16),
         grid_spec=pltpu.PrefetchScalarGridSpec(
             num_scalar_prefetch=1,
-            grid=(tiles, steps),
-            in_specs=[natural, natural, turned, turned, wide, wide, tall],
-            out_specs=specs,
-            scratch_shapes=[pltpu.VMEM((D, tile), F32)] * 3,
+            grid=(1,),
+            in_specs=[wide, wide, tall] + [HELD] * len(waits),
+            out_specs=pl.BlockSpec((1, 3, tile, D), lambda m, ref: (0, 0, 0, 0)),
         ),
         compiler_params=params(),
-        cost_estimate=estimate(
-            12 * count * rows * D * tile * tiles, tiles * (8 * count * rows * D + 6 * D * tile)
+        cost_estimate=estimate("pack_weights", 0, 12 * tile * D),
+        name="pack_weights",
+    )(at, *weights, *waits)
+
+
+def slice_kernel(many, experts, x_ref, s_ref, *rest):
+    weights, outs = rest[:many], rest[many:]
+    for at in range(many):
+
+        @pl.when(pl.program_id(0) == at)
+        def _():
+            rows = x_ref.shape[0] * x_ref.shape[2]
+            x, s = x_ref[...].reshape(rows, D), s_ref[...].reshape(rows, D)
+            gate_w, up_w, down_w = (weights[at][0, n] for n in range(3))
+            act_a, act_b = mm_nt(gate_w, x), mm_nt(up_w, x)
+            hidden, grad_a, grad_b = expert_terms(act_a, act_b, mm_nt(down_w, s))
+            outs[at][0] = mm(grad_a, x).astype(BF16)
+            outs[at][1] = mm(grad_b, x).astype(BF16)
+            outs[at][2] = mm(hidden, s).astype(BF16)
+
+
+def weight_slices(experts, stacks, packed, waits):
+    count, tile, many = stacks[0].shape[0], packed[0].shape[2], len(packed)
+    side = pl.BlockSpec((count, 1, CAP, D), lambda t, ref: (0, ref[t], 0, 0))
+    held = pl.BlockSpec((1, 3, tile, D), lambda t, ref: (0, 0, 0, 0))
+    out = pl.BlockSpec((3, tile, D), lambda t, ref: (0, 0, 0))
+    rows = count * CAP
+    return pl.pallas_call(
+        without(partial(slice_kernel, many), 3 + many, len(waits)),
+        out_shape=tuple([shape_of((3, tile, D), BF16)] * many),
+        grid_spec=pltpu.PrefetchScalarGridSpec(
+            num_scalar_prefetch=1,
+            grid=(many,),
+            in_specs=[side, side] + [held] * many + [HELD] * len(waits),
+            out_specs=tuple([out] * many),
         ),
+        compiler_params=params(),
+        cost_estimate=estimate("weight_slices", 12 * many * rows * D * tile, many * (4 * rows + 12 * tile) * D),
         name="weight_slices",
-    )(at, *stacks, *weights)
+    )(experts, *stacks, *packed, *waits)
 
 
 def place_kernel(held, at_ref, piece, *rest):
     gate_out, up_out, down_out = rest[held:]
-    gate_out[...] = piece[0].astype(F32)
-    up_out[...] = piece[1].astype(F32)
-    down_out[...] = jnp.transpose(piece[2].astype(F32))
+    gate_out[...] = jnp.transpose(piece[0].astype(F32))
+    up_out[...] = jnp.transpose(piece[1].astype(F32))
+    down_out[...] = piece[2].astype(F32)
 
 
 def place_slice(at, piece, held, units):
-    tile = piece.shape[2]
+    tile = piece.shape[1]
     wide = pl.BlockSpec((D, tile), lambda t, ref: (0, ref[0]))
     tall = pl.BlockSpec((tile, D), lambda t, ref: (ref[0], 0))
     return pl.pallas_call(
@@ -555,13 +692,13 @@
         grid_spec=pltpu.PrefetchScalarGridSpec(
             num_scalar_prefetch=1,
             grid=(1,),
-            in_specs=[pl.BlockSpec((3, D, tile), lambda t, ref: (0, 0, 0))]
-            + [pl.BlockSpec(memory_space=pl.ANY)] * len(held),
+            in_specs=[pl.BlockSpec((3, tile, D), lambda t, ref: (0, 0, 0))]
+            + [HELD] * len(held),
             out_specs=(wide, wide, tall),
         ),
         input_output_aliases={2 + n: n for n in range(len(held))},
         compiler_params=params(),
-        cost_estimate=estimate(0, 18 * D * tile),
+        cost_estimate=estimate("place_slice", 0, 18 * D * tile),
         name="place_slice",
     )(at, piece, *held)
 
@@ -742,32 +879,36 @@
     )
 
     shards = gather_group(qkv_weight, 1)
-    prompts = gather_group(tok[:P_DEV], 1)
-    partner = xor_permute(tok[P_DEV:], 1)
-    out_shards = gather_group(out_weight, 1)
-
-    ids = jnp.arange(LANES, dtype=jnp.int32)[None, :]
-    named = (route_rows[:, :1] == ids) | (route_rows[:, 1:] == ids)
-    at = jnp.arange(TOK_DEV)
-    before = (at[None, :] < at[:, None]).astype(BF16)
-    slots = jnp.where(named, mm(before, named.astype(BF16)), -1.0)
-    ext = jnp.pad(
-        jnp.transpose(slots[:, :EXT]).astype(BF16), ((0, 0), (0, D - TOK_DEV)), constant_values=-1
-    )
-    grad_block = jnp.concatenate([cot, ext], axis=0)
-    route_lanes = jnp.pad(route_rows, ((0, 0), (0, LANES - TOP)))
-    prev_lanes = jnp.pad(prev, ((0, 0), (0, LANES - IDS)))
-    previous = jnp.pad(
-        jnp.dot(prev, resid_weight.astype(F32), precision=HIGHEST, preferred_element_type=F32),
-        ((0, 0), (0, LANES - IDS)),
-    )
-    mixers = jnp.pad(
-        jnp.concatenate([router_weight, const_weight[0], const_weight[1]], axis=1),
-        ((0, 0), (0, LANES - IDS - 4)),
-    )
-    mixers_t = jnp.transpose(mixers)
-    resid_t = jnp.pad(jnp.transpose(resid_weight), ((0, LANES - IDS), (0, LANES - IDS)))
-    vectors = jnp.pad(const_vector.astype(F32), ((0, 6), (0, 0)))
+    weights = (gate_weight, up_weight, down_weight)
+    mine = replica.astype(jnp.int32)[None]
+    early = []
+    if spread:
+        early = [pack_weights(mine, weights, 0, per, count, ())]
+    (
+        prompt_rows,
+        grad_block,
+        slots,
+        route_lanes,
+        prev_lanes,
+        previous,
+        mixers,
+        mixers_t,
+        resid_t,
+        vectors,
+    ) = prepare(
+        route_rows,
+        prev,
+        cot,
+        router_weight,
+        resid_weight,
+        const_weight,
+        const_vector,
+        tok,
+        early,
+    )
+    prompts = gather_group(prompt_rows, 2)
+    for offset in range(0, group, 2):
+        prompts[offset + 1] = xor_permute(prompts[offset] if offset else tok, 1)
     gain_one = attn_gain.astype(F32)[None]
     gain_two = ffn_gain.astype(F32)[None]
 
@@ -776,30 +917,32 @@
     def group_blocks(block):
         held = gather_group(block, 2)
         own = [held[o] for o in range(0, group, 2)]
-        return own, own + [xor_permute(piece, 1) for piece in own]
-
-    def all_blocks(own):
-        half = max(1, len(own) // 2)
-        forth, back = own[:half], own[half:]
-        result = []
-        for _ in range(count - 1):
-            forth = [ring_permute(piece, 1) for piece in forth]
-            back = [ring_permute(piece, -1) for piece in back]
-            now = forth + back
-            result.append(now + [xor_permute(piece, 1) for piece in now])
+        return own + [xor_permute(piece, 1) for piece in own]
+
+    def all_blocks(block):
+        result, forth, back = [[block]], block, block
+        for step in range(1, count // 2 + 1):
+            forth = ring_permute(forth, 1)
+            result.append([forth])
+            if step < count - step:
+                back = ring_permute(back, -1)
+                result[-1].append(back)
         return result
 
-    grad_own, grad_group = group_blocks(grad_block)
-    if spread:
-        grad_far = all_blocks(grad_own)
-
-    q, kp, vp, kc, vc, w_qkv, normed = whole_call(
+    grad_far = all_blocks(grad_block) if spread else [[grad_block]]
+    hops = len(grad_far) - 1
+
+    def hop_of(blocks, at):
+        return blocks[at] if 0 < at <= hops else []
+
+    q, kp, vp, kc, vc, w_qkv, normed, later_block, later_shard, *early = whole_call(
         partial(projection_kernel, group),
         "projections",
         scal,
-        [gain_one, tok, partner]
+        [gain_one, tok]
         + [prompts[o] for o in range(1, group)]
-        + [shards[o] for o in range(group)],
+        + [shards[o] for o in range(group)]
+        + [grad_block, out_weight, *early],
         [
             shape_of((TOK_DEV, D), BF16),
             shape_of((prompt, D), BF16),
@@ -808,10 +951,16 @@
             shape_of((2 * P_DEV, D), BF16),
             shape_of((D, 3 * D), BF16),
             shape_of((TOK_DEV, D), BF16),
+            shape_of((BLOCK, D), BF16),
+            shape_of((D // group, D), BF16),
+            *[shape_of(v.shape, BF16) for v in early],
         ],
         2 * TOK_DEV * D * D + 4 * (prompt + 2 * P_DEV) * D * D,
     )
-    o32, lse = attention(scal, q, kp, vp, kc, vc, group)
+    out_shards = gather_group(later_shard, 1)
+    grad_near = group_blocks(later_block)
+    packed = [gather_group(v, 1) for v in early]
+    o32, lse = attention(scal, q, kp, vp, kc, vc, group, hop_of(grad_far, 1) if W_FRONT else [])
     w_out, res, base, block, info, mixed_low = whole_call(
         partial(routing_kernel, group),
         "routing",
@@ -828,20 +977,117 @@
             shape_of((TOK_DEV, D), BF16),
         ],
         2 * TOK_DEV * D * D,
-    )
-
-    own, near = group_blocks(block)
-    local = expert_rows(scal, near, grad_group, 0, 1, (), group, per, share)
-    if spread:
-        far = all_blocks(own)
-
-    weights = (gate_weight, up_weight, down_weight)
-    returned = {}
+        waits=[*(hop_of(grad_far, 2) if W_FRONT else []), *(grad_near[1:-1] if W_NEAR else [])],
+    )
+
+    near = group_blocks(block)
+    rings, returned, locals_out = [], {}, []
+
+    def give_back(member):
+        for offset in range(group):
+            value = locals_out[member][offset]
+            returned[offset, member] = xor_permute(value, offset) if offset else value
+        return [returned[offset, member] for offset in range(1, group)]
+
+    if not spread:
+        local = near_rows(scal, near, grad_near, group, per, share, ())
+        locals_out = [
+            local_expert(*local, *weights, member, offsets, group, per, ())
+            for member in range(per)
+        ]
+    else:
+        forth = back = block
+        stacks, done, kept = (), 0, []
+        for hop in range(1, hops + 1):
+            forth = ring_permute(forth, 1)
+            back = ring_permute(back, -1) if hop < count - hop else None
+            take, waits = [(block, grad_block)], hop_of(grad_far, 3)
+            if hop == 2:
+                take, waits = kept, hop_of(grad_far, 4)
+            elif hop > 2:
+                take, waits = kept if hop == hops else (), locals_out[-1][:1] if locals_out else ()
+            kept = [] if hop == 1 or take is kept else kept
+            if take:
+                stacks = column_rows(
+                    [h for h, g in take], [g for h, g in take], done, count, stacks, waits
+                )
+                done += len(take)
+            if hop == 2:
+                for member in range(1, per):
+                    later = pack_weights(mine, weights, member, per, count, [near[1], *([h for h, g in take] if W_PACK else [])])
+                    packed.append(gather_group(later, 1))
+            if hop == 3:
+                waits = [packed[-1][0], *packed[0].values(), stacks[0]]
+                local = near_rows(scal, near, grad_near, group, per, share, waits[:-1])
+                locals_out.append(
+                    local_expert(*local, *weights, 0, offsets, group, per, ())
+                )
+            kept = kept + list(zip([v for v in (forth, back) if v is not None], grad_far[hop]))
+        stacks = column_rows(
+            [h for h, g in kept], [g for h, g in kept], done, count, stacks, ()
+        )
+        parts = [{} for _ in range(per)]
+        last = [v for p in packed for v in p.values()]
+        for low in range(group - 2, -1, -2):
+            chosen = [(m, o) for m in range(per) for o in (low + 1, low)]
+            experts = jnp.stack([(index ^ o) * per + m for m, o in chosen]).astype(jnp.int32)
+            outs = weight_slices(experts, stacks, [packed[m][o] for m, o in chosen], last)
+            for m in range(per):
+                parts[m][low] = add_low(outs[2 * m + 1], xor_permute(outs[2 * m], 1))
+            last = [outs[0]]
+            if low:
+                last += [parts[0][low]]
+                last += give_back(0) if W_SLICE else []
+        for member, part in enumerate(parts):
+            bit = 2
+            while bit < group:
+                for offset in sorted(part, reverse=True):
+                    if offset & bit:
+                        value = part.pop(offset)
+                        if rings:
+                            value, rings[-1][0] = lax.optimization_barrier((value, rings[-1][0]))
+                        value = xor_permute(value, bit)
+                        if rings:
+                            waits = [last[0], rings[0][0]] if W_LOCAL else []
+                            outs = local_expert(
+                                *local, *weights, member, offsets, group, per, waits
+                            )
+                            if W_LOCAL:
+                                value, *outs = lax.optimization_barrier((value, *outs))
+                            locals_out.append(outs)
+                            give_back(member)
+                        part[offset ^ bit] = add_low(part[offset ^ bit], value)
+                bit *= 2
+            rings.append([part[0]])
     for member in range(per):
-        outs = local_expert(local[0], local[1], *weights, member, offsets, group, per)
-        for offset in range(group):
-            returned[offset, member] = xor_permute(outs[offset], offset) if offset else outs[0]
-
+        if (0, member) not in returned:
+            give_back(member)
+    placed = ()
+    units = gate_weight.shape[1]
+    spot = jnp.where(replica % 2 == 0, replica // 2, count - 1 - replica // 2)
+
+    def advance(step):
+        nonlocal placed
+        for member, ring in enumerate(rings):
+            toward = 1 - 2 * (member % 2)
+            if step < count:
+                ring.append(ring_permute(ring[-1], toward))
+            source = (spot - toward * (step - 1)) % count
+            source = jnp.where(source < count // 2, 2 * source, 2 * (count - 1 - source) + 1)
+            at = source.astype(jnp.int32)[None] + member * count
+            placed = place_slice(at, ring[step - 1], placed, units)
+            if step < count and W_BACK:
+                ring[step], *placed = lax.optimization_barrier((ring[step], *placed))
+
+    def advance_to(*steps):
+        for step in steps:
+            if spread:
+                advance(step)
+
+    def arrived(*steps):
+        return [ring[step] for ring, step in zip(rings, steps) if step >= 0]
+
+    advance_to(1, 2, 3)
     layer_out, res_grad, mix_grad, mixed_grad, prev_grad, small = whole_call(
         partial(combine_kernel, group, per, share),
         "combine",
@@ -871,10 +1117,18 @@
             shape_of((SMALL_ROWS, D), F32),
         ],
         6 * TOK_DEV * group * per * CAP * D + 2 * TOK_DEV * D * D,
-    )
-
-    back = attention_back(scal, q, kp, vp, kc, vc, mixed_grad, o32, lse, group)
+        waits=arrived(1, 0) if W_RING else (),
+    )
+
+    back = attention_back(
+        scal, q, kp, vp, kc, vc, mixed_grad, o32, lse, group, arrived(2, 1) if W_RING else []
+    )
     dq, pieces, later_own, later_other = back[0], list(back[1 : 1 + group]), back[-2], back[-1]
+    if W_KEYS and spread:
+        tied = lax.optimization_barrier((later_other, *pieces[1:], rings[0][3], rings[1][2]))
+        later_other, rings[0][3], rings[1][2] = tied[0], tied[-2], tied[-1]
+        pieces = [pieces[0], *tied[1:-2]]
+    advance_to(4, 5)
     later_in = xor_permute(later_other, 1)
     held = {o: [pieces[o]] for o in range(group)}
     bit = 1
@@ -899,56 +1153,43 @@
             shape_of((8, D), F32),
         ],
         6 * TOK_DEV * D * D,
+        waits=(arrived(4, 3) if W_KEYS else arrived(3, 2)) if W_RING else (),
     )
     full = jnp.concatenate([mm_tn(normed, qkv_low), mm_tn(mixed_low, mix_grad)], axis=1)
     rows = D // group
     held = {
         o: lax.dynamic_slice_in_dim(full, (index ^ o) * rows, rows, axis=0) for o in range(group)
     }
-    bit = 1
+    bit, at = 1, 5
     while bit < group:
         for offset in sorted(held):
             if offset & bit:
                 value = xor_permute(held.pop(offset).astype(BF16), bit)
+                if W_DENSE and spread and offset == bit:
+                    value, rings[0][at], rings[1][at - 1] = lax.optimization_barrier(
+                        (value, rings[0][at], rings[1][at - 1])
+                    )
+                    at += 1
+                    advance_to(at)
                 held[offset ^ bit] = held[offset ^ bit] + value.astype(F32)
         bit *= 2
-    dense = sum_replicas(held[0])
-    small = sum_everywhere(jnp.concatenate([small, small_two], axis=0))
-
-    units = gate_weight.shape[1]
-    width = units // per
+    if SC_DENSE:
+        dense = lax.psum(held[0].astype(BF16), "rep").astype(F32)
+    else:
+        dense = sum_replicas(held[0])
+    small = jnp.concatenate([small, small_two], axis=0)
+    small = lax.psum(small, ("rep", "grp")) if SC_SMALL else sum_everywhere(small)
+
     if spread:
-        stacks = ()
-        for step in range(count):
-            hidden = near if step == 0 else far[step - 1]
-            grads = grad_group if step == 0 else grad_far[step - 1]
-            stacks = expert_rows(scal, hidden, grads, step, count, stacks, group, per, share)
-        tile = width // count
-        first = replica.astype(jnp.int32)[None]
-        finished = [
-            weight_slices(
-                first + member * count, stacks, weights, member, tile, 1, "pack", 2, per
-            )[0]
-            for member in range(per)
-        ]
-        spot = jnp.where(replica % 2 == 0, replica // 2, count - 1 - replica // 2)
-        held = ()
-        for step in range(count):
-            for member in range(per):
-                toward = 1 if member % 2 == 0 else -1
-                if step:
-                    finished[member] = ring_permute(finished[member], toward)
-                source = (spot - toward * step) % count
-                source = jnp.where(
-                    source < count // 2, 2 * source, 2 * (count - 1 - source) + 1
-                ).astype(jnp.int32)[None]
-                held = place_slice(source + member * count, finished[member], held, units)
-        gate_sum, up_sum, down_sum = held
+        for step in range(len(rings[0]), count + 1):
+            advance(step)
+        gate_sum, up_sum, down_sum = placed
     else:
-        tile = min(512, width)
-        sums = weight_slices(
-            jnp.zeros((1,), jnp.int32), local, weights, 0, tile, width // tile, "write", 1, per
+        x, s = local[0][0], local[1][0]
+        hidden, grad_a, grad_b = expert_terms(
+            mm(x, gate_weight), mm(x, up_weight), mm_nt(s, down_weight)
         )
+        sums = (mm_tn(x, grad_a), mm_tn(x, grad_b), mm_tn(hidden, s))
         gate_sum, up_sum, down_sum = [
             lax.psum(part.astype(BF16), "rep").astype(F32) for part in sums
         ]

time: 745 us -> 653 us (0.88)
  waiting for transfers between devices: 333 us -> 262 us
  starting transfers between devices: 82.7 us -> 65.1 us
  Pallas kernels: 269 us -> 254 us
  between operations: 2.41 us -> 15.2 us
    ppermute x42 -> x28, waiting for transfers between devices: 182 us -> 88.3 us  [ring_permute(): return lax.ppermute(value, 'rep', pairs)]
    psum x0 -> x1, waiting for transfers between devices: none -> 55.6 us  [body(): dense = lax.psum(held[0].astype(BF16), 'rep').astype(F32)]
    ppermute x6 -> x0, waiting for transfers between devices: 50.4 us -> none  [the longest x3 43.4 us: sum_replicas(): value = keep + lax.ppermute(give, 'rep', pairs).astype(F32)]
    pallas_call x19 -> x18, Pallas kernels: 223 us -> 206 us  [the longest x5 58 us: whole_call(): pl.pallas_call(without(kernel, 1 + len(arrays), len(waits)), out_shape=tu...]
    ppermute x42 -> x28, starting transfers between devices: 48.8 us -> 33.7 us  [ring_permute(): return lax.ppermute(value, 'rep', pairs)]
    ppermute x5, waiting for transfers between devices: 21.9 us -> 34.6 us  [sum_everywhere(): value = value + lax.ppermute(value, axis, pairs)]
    unnamed x156 -> x115, local copies, waits for them, and re-layouts: 11.1 us -> 17.1 us
    ppermute x57 -> x40, waiting for transfers between devices: 79.2 us -> 84 us  [xor_permute(): return lax.ppermute(value, 'grp', pairs)]
  transfers between devices with their start and end apart: 110 -> 74, of which waited for: 37 -> 29; matrix products, arithmetic and copies ran while one was open for 6% -> 6% of each run, Pallas kernels for 33% -> 36%
where the time goes in v2:
time: 653 us; the launch traced here: 644 us
  waiting for transfers between devices  262 us (40%)
  Pallas kernels  254 us (39%)
  starting transfers between devices  65.1 us (10%)
  local copies, waits for them, and re-layouts  24.1 us (4%)
  other arithmetic  18.1 us (3%)
  between operations  15.2 us (2%)
    ppermute x28, waiting for transfers between devices, ring_permute(): return lax.ppermute(value, 'rep', pairs)  88.3 us
    ppermute x40, waiting for transfers between devices, xor_permute(): return lax.ppermute(value, 'grp', pairs)  84 us
    pallas_call x5, Pallas kernels, whole_call(): pl.pallas_call(without(kernel, 1 + len(arrays), len(waits)), out_shape=tu...  58 us
    psum x1, waiting for transfers between devices, body(): dense = lax.psum(held[0].astype(BF16), 'rep').astype(F32)  55.6 us
    pallas_call x16, Pallas kernels, place_slice(): pl.pallas_call(partial(place_kernel, len(held)), out_shape=(shape_of((D,...  48.1 us
    pallas_call x2, Pallas kernels, weight_slices(): pl.pallas_call(without(partial(slice_kernel, many), 3 + many, len(waits))...  35.7 us
    ppermute x5, waiting for transfers between devices, sum_everywhere(): value = value + lax.ppermute(value, axis, pairs)  34.6 us
    ppermute x28, starting transfers between devices, ring_permute(): return lax.ppermute(value, 'rep', pairs)  33.7 us
  transfers between devices with their start and end apart: 74, of which 29 were waited for; matrix products, arithmetic and copies ran while one was open for 6% of the time, Pallas kernels for 36%

profile of v2, /device:TPU:0, one launch (start us, length us, event | category | flops | bytes accessed | tf_op | source)
XLA Modules:
  0.0 644.4 jit_solution(16917951480596465035)
XLA Ops:
  25.2 13.4 %collective-permute-done.1.rest_1_ = bf16[256,768]{1,0:T(8,128)(2,1)} collective-permute-done((bf16[256,768]{1,0:T(8,128)(2,1)}, bf16[256,768]{1,0:T(8,128)(2,1)}, u32[]{:S(2)}, u32[]{:S(2)}) %collective-permute-start.1) | collective-permute-done | bytes 393248 | tf_op jit(solution)/shard_map/ppermute | solution.py:112
  50.4 12.2 %projections.1 = (bf16[512,768]{1,0:T(8,128)(2,1)}, bf16[1024,768]{1,0:T(8,128)(2,1)}, bf16[1024,768]{1,0:T(8,128)(2,1)}, bf16[512,768]{1,0:T(8,128)(2,1)}, bf16...) custom-call(s32[6]{0:T(128)} %pad_add_fusion.scal.refs_0_, ...), custom_call_target="tpu_custom_call" | custom-call | flops 4227858432 | bytes 20302848 | tf_op jit(solution)/shard_map/projections/pallas_call | solution.py:96
  72.7 18.6 %attention_forward.1 = (f32[512,768]{1,0:T(8,128)}, f32[512,768]{1,0:T(8,128)}) custom-call(s32[6]{0:T(128)} %pad_add_fusion.scal.refs_0_, bf16[512,768]{1,0:T(8,128)(2,1)} %get-tuple-element.205.refs_1_.q_ref, bf16[1024,768]{1,0:T(8,128)(2,1)} %get-tuple-element.206.refs_2_.kp_ref, bf16[1024,768]{1,0:T(8,128)(2,1)} %get-tuple-element.207.refs_3_.vp_ref, ...), custom_call_target="tpu_custom_call" | custom-call | flops 8053063680 | bytes 7864320 | tf_op jit(solution)/shard_map/attention_forward/pallas_call | solution.py:281
  94.6 10.0 %routing.1 = (bf16[768,768]{1,0:T(8,128)(2,1)}, f32[512,768]{1,0:T(8,128)}, f32[512,768]{1,0:T(8,128)}, bf16[528,768]{1,0:T(8,128)(2,1)}, f32[512,128]{1,0:T(8,128)}, /*index=5*/bf16[512,768]{1,0:T(8,128)(2,1)}) custom-call(s32[6]{0:T(128)} %pad_add_fusion.scal.refs_0_, bf16[512,768]{1,0:T(8,128)(2,1)} %bitcast.49, ...), custom_call_target="tpu_custom_call" | custom-call | flops 603979776 | bytes 10472448 | tf_op jit(solution)/shard_map/routing/pallas_call | solution.py:96
  117.3 15.0 %collective-permute-done.15.refs_4_.refs_2_ = bf16[528,768]{1,0:T(8,128)(2,1)S(1)} collective-permute-done((bf16[528,768]{1,0:T(8,128)(2,1)}, bf16[528,768]{1,0:T(8,128)(2,1)S(1)}, u32[]{:S(2)}, u32[]{:S(2)}) %collective-permute-start.15) | collective-permute-done | bytes 811040 | tf_op jit(solution)/shard_map/ppermute | solution.py:112
  154.1 7.6 %column_rows.5 = (bf16[8,8,128,768]{3,2,1,0:T(8,128)(2,1)}, bf16[8,8,128,768]{3,2,1,0:T(8,128)(2,1)}) custom-call(bf16[528,768]{1,0:T(8,128)(2,1)} %collective-permute-done.22.refs_0_, bf16[528,768]{1,0:T(8,128)(2,1)} %collective-permute-done.28.refs_1_, ...), custom_call_target="tpu_custom_call", output_to_operand_aliasing={{0}: (4, {}), {1}: (5, {})} | custom-call | flops 12884901888 | bytes 38141952 | tf_op jit(solution)/shard_map/column_rows/pallas_call | solution.py:530
  180.9 15.4 %local_expert.2 = (bf16[2,128,768]{2,1,0:T(8,128)(2,1)}, bf16[2,128,768]{2,1,0:T(8,128)(2,1)}, bf16[2,128,768]{2,1,0:T(8,128)(2,1)}, bf16[2,128,768]{2,1,0:T(8,128)(2,1)}) custom-call(bf16[2,512,768]{2,1,0:T(8,128)(2,1)} %get-tuple-element.219.x_ref.refs_0_, bf16[2,512,768]{2,1,0:T(8,128)(2,1)} %get-tuple-element.220.s_ref.refs_1_, ...), custom_call_target="tpu_custom_call" | custom-call | flops 9663676416 | bytes 12582912 | tf_op jit(solution)/shard_map/local_expert/pallas_call | solution.py:603
  197.3 12.5 %column_rows.6 = (bf16[8,8,128,768]{3,2,1,0:T(8,128)(2,1)}, bf16[8,8,128,768]{3,2,1,0:T(8,128)(2,1)}) custom-call(bf16[528,768]{1,0:T(8,128)(2,1)} %copy-done.46, bf16[528,768]{1,0:T(8,128)(2,1)} %collective-permute-done.29.refs_1_, bf16[528,768]{1,0:T(8,128)(2,1)} %copy-done.47, ...), custom_call_target="tpu_custom_call", output_to_operand_aliasing={{0}: (8, {}), {1}: (9, {})} | custom-call | flops 25769803776 | bytes 76283904 | tf_op jit(solution)/shard_map/column_rows/pallas_call | solution.py:530
  223.6 17.8 %weight_slices.2 = (bf16[3,256,768]{2,1,0:T(8,128)(2,1)}, bf16[3,256,768]{2,1,0:T(8,128)(2,1)}, bf16[3,256,768]{2,1,0:T(8,128)(2,1)}, bf16[3,256,768]{2,1,0:T(8,128)(2,1)}) custom-call(s32[4]{0:T(128)} %pad_add_fusion.1.refs_0_, bf16[8,8,128,768]{3,2,1,0:T(8,128)(2,1)} %get-tuple-element.228.refs_1_, bf16[8,8,128,768]{3,2,1,0:T(8,128)(2,1)} %get-tuple-element.229.refs_2_, ...), custom_call_target="tpu_custom_call" | custom-call | flops 9663676416 | bytes 22020096 | tf_op jit(solution)/shard_map/weight_slices/pallas_call | solution.py:663
  247.6 17.9 %weight_slices.3 = (bf16[3,256,768]{2,1,0:T(8,128)(2,1)}, bf16[3,256,768]{2,1,0:T(8,128)(2,1)}, bf16[3,256,768]{2,1,0:T(8,128)(2,1)}, bf16[3,256,768]{2,1,0:T(8,128)(2,1)}) custom-call(s32[4]{0:T(128)} %pad_add_fusion.2.refs_0_, bf16[8,8,128,768]{3,2,1,0:T(8,128)(2,1)} %get-tuple-element.228.refs_1_, bf16[8,8,128,768]{3,2,1,0:T(8,128)(2,1)} %get-tuple-element.229.refs_2_, ...), custom_call_target="tpu_custom_call" | custom-call | flops 9663676416 | bytes 22020096 | tf_op jit(solution)/shard_map/weight_slices/pallas_call | solution.py:663
  265.8 8.3 %collective-permute-done.38 = bf16[3,256,768]{2,1,0:T(8,128)(2,1)S(1)} collective-permute-done((bf16[3,256,768]{2,1,0:T(8,128)(2,1)S(1)}, bf16[3,256,768]{2,1,0:T(8,128)(2,1)S(1)}, u32[]{:S(2)}, u32[]{:S(2)}) %collective-permute-start.38) | collective-permute-done | bytes 1179680 | tf_op jit(solution)/shard_map/ppermute | solution.py:112
  276.7 15.4 %local_expert.3 = (bf16[2,128,768]{2,1,0:T(8,128)(2,1)}, bf16[2,128,768]{2,1,0:T(8,128)(2,1)}, bf16[2,128,768]{2,1,0:T(8,128)(2,1)}, bf16[2,128,768]{2,1,0:T(8,128)(2,1)}) custom-call(bf16[2,512,768]{2,1,0:T(8,128)(2,1)} %get-tuple-element.219.x_ref.refs_0_, bf16[2,512,768]{2,1,0:T(8,128)(2,1)} %get-tuple-element.220.s_ref.refs_1_, ...), custom_call_target="tpu_custom_call" | custom-call | flops 9663676416 | bytes 12582912 | tf_op jit(solution)/shard_map/local_expert/pallas_call | solution.py:603
  292.0 9.8 %collective-permute-done.39 = bf16[3,256,768]{2,1,0:T(8,128)(2,1)S(1)} collective-permute-done((bf16[3,256,768]{2,1,0:T(8,128)(2,1)S(1)}, bf16[3,256,768]{2,1,0:T(8,128)(2,1)S(1)}, u32[]{:S(2)}, u32[]{:S(2)}) %collective-permute-start.39) | collective-permute-done | bytes 1179680 | tf_op jit(solution)/shard_map/ppermute | solution.py:112
  310.8 10.0 %collective-permute-done.42.refs_4_ = bf16[2,128,768]{2,1,0:T(8,128)(2,1)} collective-permute-done((bf16[2,128,768]{2,1,0:T(8,128)(2,1)}, bf16[2,128,768]{2,1,0:T(8,128)(2,1)}, u32[]{:S(2)}, u32[]{:S(2)}) %collective-permute-start.42) | collective-permute-done | bytes 393248 | tf_op jit(solution)/shard_map/ppermute | solution.py:112
  337.7 7.7 %collective-permute-done.45.refs_7_ = bf16[2,128,768]{2,1,0:T(8,128)(2,1)} collective-permute-done((bf16[2,128,768]{2,1,0:T(8,128)(2,1)}, bf16[2,128,768]{2,1,0:T(8,128)(2,1)}, u32[]{:S(2)}, u32[]{:S(2)}) %collective-permute-start.45) | collective-permute-done | bytes 393248 | tf_op jit(solution)/shard_map/ppermute | solution.py:112
  345.4 21.4 %combine.1 = (f32[512,768]{1,0:T(8,128)}, f32[512,768]{1,0:T(8,128)}, bf16[512,768]{1,0:T(8,128)(2,1)}, bf16[512,768]{1,0:T(8,128)(2,1)}, f32[512,128]{1,0:T(8,128)}, /*index=5*/f32[40,768]{1,0:T(8,128)}) custom-call(s32[6]{0:T(128)} %pad_add_fusion.scal.refs_0_, bf16[2,128,768]{2,1,0:T(8,128)(2,1)} %get-tuple-element.221.refs_10_.refs_0_, ...), custom_call_target="tpu_custom_call" | custom-call | flops 3019898880 | bytes 15477760 | tf_op jit(solution)/shard_map/combine/pallas_call | solution.py:96
  372.2 24.7 %attention_backward.1 = (bf16[512,768]{1,0:T(8,128)(2,1)}, bf16[2,256,768]{2,1,0:T(8,128)(2,1)}, bf16[2,256,768]{2,1,0:T(8,128)(2,1)}, bf16[2,256,768]{2,1,0:T(8...) custom-call(s32[6]{0:T(128)} %pad_add_fusion.scal.refs_0_, ...), custom_call_target="tpu_custom_call" | custom-call | flops 20132659200 | bytes 15728640 | tf_op jit(solution)/shard_map/attention_backward/pallas_call | solution.py:368
  413.6 17.8 %collective-permute-done.63.piece = bf16[3,256,768]{2,1,0:T(8,128)(2,1)S(1)} collective-permute-done((bf16[3,256,768]{2,1,0:T(8,128)(2,1)}, bf16[3,256,768]{2,1,0:T(8,128)(2,1)S(1)}, u32[]{:S(2)}, u32[]{:S(2)}) %collective-permute-start.63) | collective-permute-done | bytes 1179680 | tf_op jit(solution)/shard_map/ppermute | solution.py:119
  436.9 8.0 %finish.1 = (bf16[512,2304]{1,0:T(8,128)(2,1)}, f32[512,768]{1,0:T(8,128)}, f32[8,768]{1,0:T(8,128)}) custom-call(s32[6]{0:T(128)} %pad_add_fusion.scal.refs_0_, bf16[512,768]{1,0:T(8,128)(2,1)} %get-tuple-element.260.dq, f32[2,256,768]{2,1,0:T(8,128)} %get-tuple-element.261.own, bf16[2,256,768]{2,1,0:T(8,128)(2,1)} %collective-permute-done.52.received, ...), custom_call_target="tpu_custom_call" | custom-call | flops 1811939328 | bytes 15363072 | tf_op jit(solution)/shard_map/finish/pallas_call | solution.py:96
  455.6 7.0 %collective-permute-done.65.piece = bf16[3,256,768]{2,1,0:T(8,128)(2,1)} collective-permute-done((bf16[3,256,768]{2,1,0:T(8,128)(2,1)S(1)}, bf16[3,256,768]{2,1,0:T(8,128)(2,1)}, u32[]{:S(2)}, u32[]{:S(2)}) %collective-permute-start.65) | collective-permute-done | bytes 1179680 | tf_op jit(solution)/shard_map/ppermute | solution.py:119
  474.9 17.4 %collective-permute-done.69.piece = bf16[3,256,768]{2,1,0:T(8,128)(2,1)} collective-permute-done((bf16[3,256,768]{2,1,0:T(8,128)(2,1)}, bf16[3,256,768]{2,1,0:T(8,128)(2,1)}, u32[]{:S(2)}, u32[]{:S(2)}) %collective-permute-start.69) | collective-permute-done | bytes 1179680 | tf_op jit(solution)/shard_map/ppermute | solution.py:119
  495.5 24.7 %collective-permute-done.56 = f32[48,768]{1,0:T(8,128)S(1)} collective-permute-done((f32[48,768]{1,0:T(8,128)S(1)}, f32[48,768]{1,0:T(8,128)S(1)}, u32[]{:S(2)}, u32[]{:S(2)}) %collective-permute-start.56) | collective-permute-done | bytes 147488 | tf_op jit(solution)/shard_map/ppermute | solution.py:820
  555.7 13.5 %collective-permute-done.72.piece = bf16[3,256,768]{2,1,0:T(8,128)(2,1)} collective-permute-done((bf16[3,256,768]{2,1,0:T(8,128)(2,1)S(1)}, bf16[3,256,768]{2,1,0:T(8,128)(2,1)}, u32[]{:S(2)}, u32[]{:S(2)}) %collective-permute-start.72) | collective-permute-done | bytes 1179680 | tf_op jit(solution)/shard_map/ppermute | solution.py:119
  572.0 55.6 %all-reduce.2.cloned.1.call-done = bf16[192,3072]{1,0:T(8,128)(2,1)} async-done(((bf16[192,3072]{1,0:T(8,128)(2,1)}), bf16[192,3072]{1,0:T(8,128)(2,1)}) %all-reduce.2.cloned.1.call-update) | async-done | bytes 1179664 | tf_op jit(solution)/shard_map/psum | solution.py:1177
  (309 shorter events, 247.7 us)
Async XLA Ops:
  7.2 620.4 %all-reduce.2.cloned.1.call-start = ((), (), s32[]{:S(2)}) async-start(), calls=%async_computation | async-start | bytes 2359296 | tf_op jit(solution)/shard_map/psum | solution.py:1177
  7.2 31.4 %collective-permute-start.4 = (bf16[192,2304]{1,0:T(8,128)(2,1)}, bf16[192,2304]{1,0:T(8,128)(2,1)S(1)}, u32[]{:S(2)}, u32[]{:S(2)}) collective-permute-start(bf16[192,2304]{1,0:T(8,128)(2,1)} %rest_3_.1), channel_id=1, source_target_pairs={{0,2},{1,3},{2,0},{3,1},{4,6},{5,7},{6,4},{7,5},{8,10},{9,11},{10,... | collective-permute-start | bytes 2654216 | tf_op jit(solution)/shard_map/ppermute | solution.py:112
  65.7 49.7 %collective-permute-start.19 = (bf16[1,3,256,768]{3,2,1,0:T(8,128)(2,1)}, bf16[1,3,256,768]{3,2,1,0:T(8,128)(2,1)S(1)}, u32[]{:S(2)}, u32[]{:S(2)}) collective-permute-start(bf16[1,3,256,768]{3,2,1,0:T(8,128)(2,1)} %get-tuple-element.218.refs_10_.refs_7_.refs_4_), channel_id=1, source_target_pairs={{0,2},{1,3},{2,0},{3,1},{4,6},{5,7},{6,4},{7,5},{8,10},{9,11},{10,... | collective-permute-start | bytes 3538952 | tf_op jit(solution)/shard_map/ppermute | solution.py:112
  67.2 48.2 %collective-permute-start.20 = (bf16[1,3,256,768]{3,2,1,0:T(8,128)(2,1)}, bf16[1,3,256,768]{3,2,1,0:T(8,128)(2,1)S(1)}, u32[]{:S(2)}, u32[]{:S(2)}) collective-permute-start(bf16[1,3,256,768]{3,2,1,0:T(8,128)(2,1)} %get-tuple-element.218.refs_10_.refs_7_.refs_4_), channel_id=1, source_target_pairs={{0,1},{1,0},{2,3},{3,2},{4,5},{5,4},{6,7},{7,6},{8,9},{9,8},{10,11... | collective-permute-start | bytes 3538952 | tf_op jit(solution)/shard_map/ppermute | solution.py:112
  112.1 29.5 %collective-permute-start.27 = (bf16[528,768]{1,0:T(8,128)(2,1)}, bf16[528,768]{1,0:T(8,128)(2,1)}, u32[]{:S(2)}, u32[]{:S(2)}) collective-permute-start(bf16[528,768]{1,0:T(8,128)(2,1)} %collective-permute-done.26.refs_2_.refs_6_), channel_id=1, source_target_pairs={{0,8},{8,16},{16,24},{24,28},{28,20},{20,12},{12,4},{4,0},{1,9},{9... | collective-permute-start | bytes 2433032 | tf_op jit(solution)/shard_map/ppermute | solution.py:119
  115.4 34.0 %collective-permute-start.22 = (bf16[528,768]{1,0:T(8,128)(2,1)}, bf16[528,768]{1,0:T(8,128)(2,1)}, u32[]{:S(2)}, u32[]{:S(2)}) collective-permute-start(bf16[528,768]{1,0:T(8,128)(2,1)} %get-tuple-element.217.refs_1_.refs_0_.refs_10_), channel_id=1, source_target_pairs={{0,8},{8,16},{16,24},{24,28},{28,20},{20,12},{12,4},{4,0},{1,9},{9... | collective-permute-start | bytes 2433032 | tf_op jit(solution)/shard_map/ppermute | solution.py:119
  141.7 54.6 %collective-permute-start.32 = (bf16[1,3,256,768]{3,2,1,0:T(8,128)(2,1)}, bf16[1,3,256,768]{3,2,1,0:T(8,128)(2,1)S(1)}, u32[]{:S(2)}, u32[]{:S(2)}) collective-permute-start(bf16[1,3,256,768]{3,2,1,0:T(8,128)(2,1)} %pack_weights.3.refs_9_.refs_11_.refs_6_), channel_id=1, source_target_pairs={{0,2},{1,3},{2,0},{3,1},{4,6},{5,7},{6,4},{7,5},{8,10},{9,11},{10,... | collective-permute-start | bytes 3538952 | tf_op jit(solution)/shard_map/ppermute | solution.py:112
  143.2 30.4 %collective-permute-start.17 = (bf16[528,768]{1,0:T(8,128)(2,1)}, bf16[528,768]{1,0:T(8,128)(2,1)S(1)}, u32[]{:S(2)}, u32[]{:S(2)}) collective-permute-start(bf16[528,768]{1,0:T(8,128)(2,1)} %copy-done.14), channel_id=1, source_target_pairs={{0,1},{1,0},{2,3},{3,2},{4,5},{5,4},{6,7},{7,6},{8,9},{9,8},{10,11... | collective-permute-start | bytes 2433032 | tf_op jit(solution)/shard_map/ppermute | solution.py:112
  161.7 60.5 %collective-permute-start.34 = (bf16[1,3,256,768]{3,2,1,0:T(8,128)(2,1)S(1)}, bf16[1,3,256,768]{3,2,1,0:T(8,128)(2,1)S(1)}, u32[]{:S(2)}, u32[]{:S(2)}) collective-permute-start(bf16[1,3,256,768]{3,2,1,0:T(8,128)(2,1)S(1)} %copy-done.4), channel_id=1, source_target_pairs={{0,1},{1,0},{2,3},{3,2},{4,5},{5,4},{6,7},{7,6},{8,9},{9,8},{10,11... | collective-permute-start | bytes 3538952 | tf_op jit(solution)/shard_map/ppermute | solution.py:112
  276.1 31.9 %collective-permute-start.46 = (bf16[3,256,768]{2,1,0:T(8,128)(2,1)S(1)}, bf16[3,256,768]{2,1,0:T(8,128)(2,1)}, u32[]{:S(2)}, u32[]{:S(2)}) collective-permute-start(bf16[3,256,768]{2,1,0:T(8,128)(2,1)S(1)} %add_convert_fusion.2.refs_6_.piece), channel_id=1, source_target_pairs={{0,8},{8,16},{16,24},{24,28},{28,20},{20,12},{12,4},{4,0},{1,9},{9... | collective-permute-start | bytes 3538952 | tf_op jit(solution)/shard_map/ppermute | solution.py:119
  303.6 63.3 %collective-permute-start.49 = (bf16[3,256,768]{2,1,0:T(8,128)(2,1)S(1)}, bf16[3,256,768]{2,1,0:T(8,128)(2,1)S(1)}, u32[]{:S(2)}, u32[]{:S(2)}) collective-permute-start(bf16[3,256,768]{2,1,0:T(8,128)(2,1)S(1)} %add_convert_fusion.piece), channel_id=1, source_target_pairs={{0,4},{8,0},{16,8},{24,16},{28,24},{20,28},{12,20},{4,12},{1,5},{9... | collective-permute-start | bytes 3538952 | tf_op jit(solution)/shard_map/ppermute | solution.py:119
  308.0 62.1 %collective-permute-start.47 = (bf16[3,256,768]{2,1,0:T(8,128)(2,1)}, bf16[3,256,768]{2,1,0:T(8,128)(2,1)S(1)}, u32[]{:S(2)}, u32[]{:S(2)}) collective-permute-start(bf16[3,256,768]{2,1,0:T(8,128)(2,1)} %collective-permute-done.46.piece), channel_id=1, source_target_pairs={{0,8},{8,16},{16,24},{24,28},{28,20},{20,12},{12,4},{4,0},{1,9},{9... | collective-permute-start | bytes 3538952 | tf_op jit(solution)/shard_map/ppermute | solution.py:119
  370.1 32.6 %collective-permute-start.50 = (bf16[3,256,768]{2,1,0:T(8,128)(2,1)S(1)}, bf16[3,256,768]{2,1,0:T(8,128)(2,1)}, u32[]{:S(2)}, u32[]{:S(2)}) collective-permute-start(bf16[3,256,768]{2,1,0:T(8,128)(2,1)S(1)} %collective-permute-done.47.piece), channel_id=1, source_target_pairs={{0,8},{8,16},{16,24},{24,28},{28,20},{20,12},{12,4},{4,0},{1,9},{9... | collective-permute-start | bytes 3538952 | tf_op jit(solution)/shard_map/ppermute | solution.py:119
  370.5 29.2 %collective-permute-start.51 = (bf16[3,256,768]{2,1,0:T(8,128)(2,1)S(1)}, bf16[3,256,768]{2,1,0:T(8,128)(2,1)}, u32[]{:S(2)}, u32[]{:S(2)}) collective-permute-start(bf16[3,256,768]{2,1,0:T(8,128)(2,1)S(1)} %collective-permute-done.49.piece), channel_id=1, source_target_pairs={{0,4},{8,0},{16,8},{24,16},{28,24},{20,28},{12,20},{4,12},{1,5},{9... | collective-permute-start | bytes 3538952 | tf_op jit(solution)/shard_map/ppermute | solution.py:119
  404.3 30.3 %collective-permute-start.62 = (bf16[3,256,768]{2,1,0:T(8,128)(2,1)}, bf16[3,256,768]{2,1,0:T(8,128)(2,1)S(1)}, u32[]{:S(2)}, u32[]{:S(2)}) collective-permute-start(bf16[3,256,768]{2,1,0:T(8,128)(2,1)} %collective-permute-done.50.piece), channel_id=1, source_target_pairs={{0,8},{8,16},{16,24},{24,28},{28,20},{20,12},{12,4},{4,0},{1,9},{9... | collective-permute-start | bytes 3538952 | tf_op jit(solution)/shard_map/ppermute | solution.py:119
  404.8 32.0 %collective-permute-start.52 = (bf16[2,256,768]{2,1,0:T(8,128)(2,1)}, bf16[2,256,768]{2,1,0:T(8,128)(2,1)}, u32[]{:S(2)}, u32[]{:S(2)}) collective-permute-start(bf16[2,256,768]{2,1,0:T(8,128)(2,1)} %get-tuple-element.301), channel_id=1, source_target_pairs={{0,1},{1,0},{2,3},{3,2},{4,5},{5,4},{6,7},{7,6},{8,9},{9,8},{10,11... | collective-permute-start | bytes 2359304 | tf_op jit(solution)/shard_map/ppermute | solution.py:112
  404.8 32.0 %collective-permute-start.53 = (bf16[2,256,768]{2,1,0:T(8,128)(2,1)}, bf16[2,256,768]{2,1,0:T(8,128)(2,1)}, u32[]{:S(2)}, u32[]{:S(2)}) collective-permute-start(bf16[2,256,768]{2,1,0:T(8,128)(2,1)} %get-tuple-element.303), channel_id=1, source_target_pairs={{0,1},{1,0},{2,3},{3,2},{4,5},{5,4},{6,7},{7,6},{8,9},{9,8},{10,11... | collective-permute-start | bytes 2359304 | tf_op jit(solution)/shard_map/ppermute | solution.py:112
  406.4 30.5 %collective-permute-start.55 = (bf16[2,256,768]{2,1,0:T(8,128)(2,1)}, bf16[2,256,768]{2,1,0:T(8,128)(2,1)}, u32[]{:S(2)}, u32[]{:S(2)}) collective-permute-start(bf16[2,256,768]{2,1,0:T(8,128)(2,1)} %add_convert_fusion.6), channel_id=1, source_target_pairs={{0,2},{1,3},{2,0},{3,1},{4,6},{5,7},{6,4},{7,5},{8,10},{9,11},{10,... | collective-permute-start | bytes 2359304 | tf_op jit(solution)/shard_map/ppermute | solution.py:112
  434.6 31.0 %collective-permute-start.64 = (bf16[3,256,768]{2,1,0:T(8,128)(2,1)S(1)}, bf16[3,256,768]{2,1,0:T(8,128)(2,1)}, u32[]{:S(2)}, u32[]{:S(2)}) collective-permute-start(bf16[3,256,768]{2,1,0:T(8,128)(2,1)S(1)} %collective-permute-done.62.piece), channel_id=1, source_target_pairs={{0,8},{8,16},{16,24},{24,28},{28,20},{20,12},{12,4},{4,0},{1,9},{9... | collective-permute-start | bytes 3538952 | tf_op jit(solution)/shard_map/ppermute | solution.py:119
  467.2 65.6 %collective-permute-start.68 = (bf16[3,256,768]{2,1,0:T(8,128)(2,1)}, bf16[3,256,768]{2,1,0:T(8,128)(2,1)S(1)}, u32[]{:S(2)}, u32[]{:S(2)}) collective-permute-start(bf16[3,256,768]{2,1,0:T(8,128)(2,1)} %collective-permute-done.64.piece), channel_id=1, source_target_pairs={{0,8},{8,16},{16,24},{24,28},{28,20},{20,12},{12,4},{4,0},{1,9},{9... | collective-permute-start | bytes 3538952 | tf_op jit(solution)/shard_map/ppermute | solution.py:119
  470.4 62.4 %collective-permute-start.67 = (bf16[192,3072]{1,0:T(8,128)(2,1)}, bf16[192,3072]{1,0:T(8,128)(2,1)}, u32[]{:S(2)}, u32[]{:S(2)}) collective-permute-start(bf16[192,3072]{1,0:T(8,128)(2,1)} %fusion.10), channel_id=1, source_target_pairs={{0,2},{1,3},{2,0},{3,1},{4,6},{5,7},{6,4},{7,5},{8,10},{9,11},{10,... | collective-permute-start | bytes 3538952 | tf_op jit(solution)/shard_map/ppermute | solution.py:112
  492.3 48.6 %collective-permute-start.70 = (bf16[3,256,768]{2,1,0:T(8,128)(2,1)}, bf16[3,256,768]{2,1,0:T(8,128)(2,1)}, u32[]{:S(2)}, u32[]{:S(2)}) collective-permute-start(bf16[3,256,768]{2,1,0:T(8,128)(2,1)} %collective-permute-done.69.piece), channel_id=1, source_target_pairs={{0,4},{8,0},{16,8},{24,16},{28,24},{20,28},{12,20},{4,12},{1,5},{9... | collective-permute-start | bytes 3538952 | tf_op jit(solution)/shard_map/ppermute | solution.py:119
  532.9 36.3 %collective-permute-start.72 = (bf16[3,256,768]{2,1,0:T(8,128)(2,1)S(1)}, bf16[3,256,768]{2,1,0:T(8,128)(2,1)}, u32[]{:S(2)}, u32[]{:S(2)}) collective-permute-start(bf16[3,256,768]{2,1,0:T(8,128)(2,1)S(1)} %collective-permute-done.68.piece), channel_id=1, source_target_pairs={{0,8},{8,16},{16,24},{24,28},{28,20},{20,12},{12,4},{4,0},{1,9},{9... | collective-permute-start | bytes 3538952 | tf_op jit(solution)/shard_map/ppermute | solution.py:119
  540.8 90.2 %collective-permute-start.71 = (bf16[3,256,768]{2,1,0:T(8,128)(2,1)}, bf16[3,256,768]{2,1,0:T(8,128)(2,1)S(1)}, u32[]{:S(2)}, u32[]{:S(2)}) collective-permute-start(bf16[3,256,768]{2,1,0:T(8,128)(2,1)} %collective-permute-done.70.piece), channel_id=1, source_target_pairs={{0,4},{8,0},{16,8},{24,16},{28,24},{20,28},{12,20},{4,12},{1,5},{9... | collective-permute-start | bytes 3538952 | tf_op jit(solution)/shard_map/ppermute | solution.py:119
  (104 other events, 1495.0 us)
Sparse Core Ops, SparseCore 0:
  538.0 89.4 all-reduce.1

commit v3 on v2

--- a/solution.py
+++ b/solution.py
@@ -40,7 +40,7 @@
 W_FRONT = 1
 W_RING = 0
 W_LOCAL = 1
-W_SLICE = 0
+W_SLICE = 1
 W_BACK = 1
 
 
@@ -1178,6 +1178,11 @@
     else:
         dense = sum_replicas(held[0])
     small = jnp.concatenate([small, small_two], axis=0)
+    if W_DENSE and spread:
+        advance_to(*range(len(rings[0]), count))
+        small, rings[0][6], rings[1][6] = lax.optimization_barrier(
+            (small, rings[0][6], rings[1][6])
+        )
     small = lax.psum(small, ("rep", "grp")) if SC_SMALL else sum_everywhere(small)
 
     if spread:

time: 653 us -> 619 us (0.948)
  waiting for transfers between devices: 262 us -> 229 us
    psum x1, waiting for transfers between devices: 55.6 us -> 30.9 us  [body(): dense = lax.psum(held[0].astype(BF16), 'rep').astype(F32)]
    ppermute x5, waiting for transfers between devices: 34.6 us -> 18.7 us  [sum_everywhere(): value = value + lax.ppermute(value, axis, pairs)]
    ppermute x28, waiting for transfers between devices: 88.3 us -> 99.7 us  [ring_permute(): return lax.ppermute(value, 'rep', pairs)]
    unnamed x115 -> x124, local copies, waits for them, and re-layouts: 17.1 us -> 17.9 us
  transfers between devices with their start and end apart: 74 -> 74, of which waited for: 29 -> 28; matrix products, arithmetic and copies ran while one was open for 6% -> 6% of each run, Pallas kernels for 36% -> 38%
where the time goes in v3:
time: 619 us; the launch traced here: 611 us
  Pallas kernels  254 us (41%)
  waiting for transfers between devices  229 us (37%)
  starting transfers between devices  64.9 us (10%)
  local copies, waits for them, and re-layouts  24.9 us (4%)
  other arithmetic  17.4 us (3%)
  between operations  15.1 us (2%)
    ppermute x28, waiting for transfers between devices, ring_permute(): return lax.ppermute(value, 'rep', pairs)  99.7 us
    ppermute x40, waiting for transfers between devices, xor_permute(): return lax.ppermute(value, 'grp', pairs)  79.4 us
    pallas_call x5, Pallas kernels, whole_call(): pl.pallas_call(without(kernel, 1 + len(arrays), len(waits)), out_shape=tu...  58 us
    pallas_call x16, Pallas kernels, place_slice(): pl.pallas_call(partial(place_kernel, len(held)), out_shape=(shape_of((D,...  48.1 us
    pallas_call x2, Pallas kernels, weight_slices(): pl.pallas_call(without(partial(slice_kernel, many), 3 + many, len(waits))...  35.6 us
    ppermute x28, starting transfers between devices, ring_permute(): return lax.ppermute(value, 'rep', pairs)  35.5 us
    psum x1, waiting for transfers between devices, body(): dense = lax.psum(held[0].astype(BF16), 'rep').astype(F32)  30.9 us
    pallas_call x2, Pallas kernels, local_expert(): pl.pallas_call(without(partial(expert_kernel, group, offsets), 5, len(wai...  30.8 us
  transfers between devices with their start and end apart: 74, of which 28 were waited for; matrix products, arithmetic and copies ran while one was open for 6% of the time, Pallas kernels for 38%

profile of v3, /device:TPU:0, one launch (start us, length us, event | category | flops | bytes accessed | tf_op | source)
XLA Modules:
  0.0 610.6 jit_solution(7395925235226850562)
XLA Ops:
  25.2 13.4 %collective-permute-done.1.rest_1_ = bf16[256,768]{1,0:T(8,128)(2,1)} collective-permute-done((bf16[256,768]{1,0:T(8,128)(2,1)}, bf16[256,768]{1,0:T(8,128)(2,1)}, u32[]{:S(2)}, u32[]{:S(2)}) %collective-permute-start.1) | collective-permute-done | bytes 393248 | tf_op jit(solution)/shard_map/ppermute | solution.py:112
  50.4 12.2 %projections.1 = (bf16[512,768]{1,0:T(8,128)(2,1)}, bf16[1024,768]{1,0:T(8,128)(2,1)}, bf16[1024,768]{1,0:T(8,128)(2,1)}, bf16[512,768]{1,0:T(8,128)(2,1)}, bf16...) custom-call(s32[6]{0:T(128)} %pad_add_fusion.scal.refs_0_, ...), custom_call_target="tpu_custom_call" | custom-call | flops 4227858432 | bytes 20302848 | tf_op jit(solution)/shard_map/projections/pallas_call | solution.py:96
  72.7 18.6 %attention_forward.1 = (f32[512,768]{1,0:T(8,128)}, f32[512,768]{1,0:T(8,128)}) custom-call(s32[6]{0:T(128)} %pad_add_fusion.scal.refs_0_, bf16[512,768]{1,0:T(8,128)(2,1)} %get-tuple-element.206.refs_1_.q_ref, bf16[1024,768]{1,0:T(8,128)(2,1)} %get-tuple-element.207.refs_2_.kp_ref, bf16[1024,768]{1,0:T(8,128)(2,1)} %get-tuple-element.208.refs_3_.vp_ref, ...), custom_call_target="tpu_custom_call" | custom-call | flops 8053063680 | bytes 7864320 | tf_op jit(solution)/shard_map/attention_forward/pallas_call | solution.py:281
  94.5 10.0 %routing.1 = (bf16[768,768]{1,0:T(8,128)(2,1)}, f32[512,768]{1,0:T(8,128)}, f32[512,768]{1,0:T(8,128)}, bf16[528,768]{1,0:T(8,128)(2,1)}, f32[512,128]{1,0:T(8,128)}, /*index=5*/bf16[512,768]{1,0:T(8,128)(2,1)}) custom-call(s32[6]{0:T(128)} %pad_add_fusion.scal.refs_0_, bf16[512,768]{1,0:T(8,128)(2,1)} %bitcast.49, ...), custom_call_target="tpu_custom_call" | custom-call | flops 603979776 | bytes 10472448 | tf_op jit(solution)/shard_map/routing/pallas_call | solution.py:96
  117.3 15.0 %collective-permute-done.15.refs_4_.refs_2_ = bf16[528,768]{1,0:T(8,128)(2,1)S(1)} collective-permute-done((bf16[528,768]{1,0:T(8,128)(2,1)}, bf16[528,768]{1,0:T(8,128)(2,1)S(1)}, u32[]{:S(2)}, u32[]{:S(2)}) %collective-permute-start.15) | collective-permute-done | bytes 811040 | tf_op jit(solution)/shard_map/ppermute | solution.py:112
  154.1 7.6 %column_rows.5 = (bf16[8,8,128,768]{3,2,1,0:T(8,128)(2,1)}, bf16[8,8,128,768]{3,2,1,0:T(8,128)(2,1)}) custom-call(bf16[528,768]{1,0:T(8,128)(2,1)} %collective-permute-done.22.refs_0_, bf16[528,768]{1,0:T(8,128)(2,1)} %collective-permute-done.28.refs_1_, ...), custom_call_target="tpu_custom_call", output_to_operand_aliasing={{0}: (4, {}), {1}: (5, {})} | custom-call | flops 12884901888 | bytes 38141952 | tf_op jit(solution)/shard_map/column_rows/pallas_call | solution.py:530
  180.9 15.4 %local_expert.2 = (bf16[2,128,768]{2,1,0:T(8,128)(2,1)}, bf16[2,128,768]{2,1,0:T(8,128)(2,1)}, bf16[2,128,768]{2,1,0:T(8,128)(2,1)}, bf16[2,128,768]{2,1,0:T(8,128)(2,1)}) custom-call(bf16[2,512,768]{2,1,0:T(8,128)(2,1)} %get-tuple-element.220.x_ref.refs_0_, bf16[2,512,768]{2,1,0:T(8,128)(2,1)} %get-tuple-element.221.s_ref.refs_1_, ...), custom_call_target="tpu_custom_call" | custom-call | flops 9663676416 | bytes 12582912 | tf_op jit(solution)/shard_map/local_expert/pallas_call | solution.py:603
  197.4 12.5 %column_rows.6 = (bf16[8,8,128,768]{3,2,1,0:T(8,128)(2,1)}, bf16[8,8,128,768]{3,2,1,0:T(8,128)(2,1)}) custom-call(bf16[528,768]{1,0:T(8,128)(2,1)} %copy-done.45, bf16[528,768]{1,0:T(8,128)(2,1)} %collective-permute-done.29.refs_1_, bf16[528,768]{1,0:T(8,128)(2,1)} %copy-done.46, ...), custom_call_target="tpu_custom_call", output_to_operand_aliasing={{0}: (8, {}), {1}: (9, {})} | custom-call | flops 25769803776 | bytes 76283904 | tf_op jit(solution)/shard_map/column_rows/pallas_call | solution.py:530
  223.7 17.7 %weight_slices.2 = (bf16[3,256,768]{2,1,0:T(8,128)(2,1)}, bf16[3,256,768]{2,1,0:T(8,128)(2,1)}, bf16[3,256,768]{2,1,0:T(8,128)(2,1)}, bf16[3,256,768]{2,1,0:T(8,128)(2,1)}) custom-call(s32[4]{0:T(128)} %pad_add_fusion.1.refs_0_, bf16[8,8,128,768]{3,2,1,0:T(8,128)(2,1)} %get-tuple-element.229.refs_1_, bf16[8,8,128,768]{3,2,1,0:T(8,128)(2,1)} %get-tuple-element.230.refs_2_, ...), custom_call_target="tpu_custom_call" | custom-call | flops 9663676416 | bytes 22020096 | tf_op jit(solution)/shard_map/weight_slices/pallas_call | solution.py:663
  253.9 7.4 %collective-permute-done.39.refs_11_.refs_6_ = bf16[2,128,768]{2,1,0:T(8,128)(2,1)S(1)} collective-permute-done((bf16[2,128,768]{2,1,0:T(8,128)(2,1)S(1)}, bf16[2,128,768]{2,1,0:T(8,128)(2,1)S(1)}, u32[]{:S(2)}, u32[]{:S(2)}) %collective-permute-start.39) | collective-permute-done | bytes 393248 | tf_op jit(solution)/shard_map/ppermute | solution.py:112
  262.1 17.9 %weight_slices.3 = (bf16[3,256,768]{2,1,0:T(8,128)(2,1)}, bf16[3,256,768]{2,1,0:T(8,128)(2,1)}, bf16[3,256,768]{2,1,0:T(8,128)(2,1)}, bf16[3,256,768]{2,1,0:T(8,128)(2,1)}) custom-call(s32[4]{0:T(128)} %pad_add_fusion.2.refs_0_, bf16[8,8,128,768]{3,2,1,0:T(8,128)(2,1)} %get-tuple-element.229.refs_1_, bf16[8,8,128,768]{3,2,1,0:T(8,128)(2,1)} %get-tuple-element.230.refs_2_, ...), custom_call_target="tpu_custom_call" | custom-call | flops 9663676416 | bytes 22020096 | tf_op jit(solution)/shard_map/weight_slices/pallas_call | solution.py:663
  289.3 15.5 %local_expert.3 = (bf16[2,128,768]{2,1,0:T(8,128)(2,1)}, bf16[2,128,768]{2,1,0:T(8,128)(2,1)}, bf16[2,128,768]{2,1,0:T(8,128)(2,1)}, bf16[2,128,768]{2,1,0:T(8,128)(2,1)}) custom-call(bf16[2,512,768]{2,1,0:T(8,128)(2,1)} %get-tuple-element.220.x_ref.refs_0_, bf16[2,512,768]{2,1,0:T(8,128)(2,1)} %get-tuple-element.221.s_ref.refs_1_, ...), custom_call_target="tpu_custom_call" | custom-call | flops 9663676416 | bytes 12582912 | tf_op jit(solution)/shard_map/local_expert/pallas_call | solution.py:603
  304.8 9.6 %collective-permute-done.42 = bf16[3,256,768]{2,1,0:T(8,128)(2,1)S(1)} collective-permute-done((bf16[3,256,768]{2,1,0:T(8,128)(2,1)S(1)}, bf16[3,256,768]{2,1,0:T(8,128)(2,1)S(1)}, u32[]{:S(2)}, u32[]{:S(2)}) %collective-permute-start.42) | collective-permute-done | bytes 1179680 | tf_op jit(solution)/shard_map/ppermute | solution.py:112
  325.9 7.5 %collective-permute-done.44.refs_5_ = bf16[2,128,768]{2,1,0:T(8,128)(2,1)} collective-permute-done((bf16[2,128,768]{2,1,0:T(8,128)(2,1)}, bf16[2,128,768]{2,1,0:T(8,128)(2,1)}, u32[]{:S(2)}, u32[]{:S(2)}) %collective-permute-start.44) | collective-permute-done | bytes 393248 | tf_op jit(solution)/shard_map/ppermute | solution.py:112
  333.4 7.7 %collective-permute-done.45.refs_7_ = bf16[2,128,768]{2,1,0:T(8,128)(2,1)} collective-permute-done((bf16[2,128,768]{2,1,0:T(8,128)(2,1)}, bf16[2,128,768]{2,1,0:T(8,128)(2,1)}, u32[]{:S(2)}, u32[]{:S(2)}) %collective-permute-start.45) | collective-permute-done | bytes 393248 | tf_op jit(solution)/shard_map/ppermute | solution.py:112
  341.1 21.4 %combine.1 = (f32[512,768]{1,0:T(8,128)}, f32[512,768]{1,0:T(8,128)}, bf16[512,768]{1,0:T(8,128)(2,1)}, bf16[512,768]{1,0:T(8,128)(2,1)}, f32[512,128]{1,0:T(8,128)}, /*index=5*/f32[40,768]{1,0:T(8,128)}) custom-call(s32[6]{0:T(128)} %pad_add_fusion.scal.refs_0_, bf16[2,128,768]{2,1,0:T(8,128)(2,1)} %get-tuple-element.222.refs_10_.refs_0_, ...), custom_call_target="tpu_custom_call" | custom-call | flops 3019898880 | bytes 15477760 | tf_op jit(solution)/shard_map/combine/pallas_call | solution.py:96
  367.9 24.7 %attention_backward.1 = (bf16[512,768]{1,0:T(8,128)(2,1)}, bf16[2,256,768]{2,1,0:T(8,128)(2,1)}, bf16[2,256,768]{2,1,0:T(8,128)(2,1)}, bf16[2,256,768]{2,1,0:T(8...) custom-call(s32[6]{0:T(128)} %pad_add_fusion.scal.refs_0_, ...), custom_call_target="tpu_custom_call" | custom-call | flops 20132659200 | bytes 15728640 | tf_op jit(solution)/shard_map/attention_backward/pallas_call | solution.py:368
  409.3 17.8 %collective-permute-done.60.piece = bf16[3,256,768]{2,1,0:T(8,128)(2,1)S(1)} collective-permute-done((bf16[3,256,768]{2,1,0:T(8,128)(2,1)}, bf16[3,256,768]{2,1,0:T(8,128)(2,1)S(1)}, u32[]{:S(2)}, u32[]{:S(2)}) %collective-permute-start.60) | collective-permute-done | bytes 1179680 | tf_op jit(solution)/shard_map/ppermute | solution.py:119
  432.6 8.0 %finish.1 = (bf16[512,2304]{1,0:T(8,128)(2,1)}, f32[512,768]{1,0:T(8,128)}, f32[8,768]{1,0:T(8,128)}) custom-call(s32[6]{0:T(128)} %pad_add_fusion.scal.refs_0_, bf16[512,768]{1,0:T(8,128)(2,1)} %get-tuple-element.261.dq, f32[2,256,768]{2,1,0:T(8,128)} %get-tuple-element.262.own, bf16[2,256,768]{2,1,0:T(8,128)(2,1)} %collective-permute-done.52.received, ...), custom_call_target="tpu_custom_call" | custom-call | flops 1811939328 | bytes 15363072 | tf_op jit(solution)/shard_map/finish/pallas_call | solution.py:96
  451.3 7.2 %collective-permute-done.62.piece = bf16[3,256,768]{2,1,0:T(8,128)(2,1)} collective-permute-done((bf16[3,256,768]{2,1,0:T(8,128)(2,1)S(1)}, bf16[3,256,768]{2,1,0:T(8,128)(2,1)}, u32[]{:S(2)}, u32[]{:S(2)}) %collective-permute-start.62) | collective-permute-done | bytes 1179680 | tf_op jit(solution)/shard_map/ppermute | solution.py:119
  470.7 17.5 %collective-permute-done.64.piece = bf16[3,256,768]{2,1,0:T(8,128)(2,1)} collective-permute-done((bf16[3,256,768]{2,1,0:T(8,128)(2,1)}, bf16[3,256,768]{2,1,0:T(8,128)(2,1)}, u32[]{:S(2)}, u32[]{:S(2)}) %collective-permute-start.64) | collective-permute-done | bytes 1179680 | tf_op jit(solution)/shard_map/ppermute | solution.py:119
  501.5 25.0 %collective-permute-done.65.piece = bf16[3,256,768]{2,1,0:T(8,128)(2,1)} collective-permute-done((bf16[3,256,768]{2,1,0:T(8,128)(2,1)}, bf16[3,256,768]{2,1,0:T(8,128)(2,1)}, u32[]{:S(2)}, u32[]{:S(2)}) %collective-permute-start.65) | collective-permute-done | bytes 1179680 | tf_op jit(solution)/shard_map/ppermute | solution.py:119
  542.8 7.4 %collective-permute-done.68 = f32[48,768]{1,0:T(8,128)S(1)} collective-permute-done((f32[48,768]{1,0:T(8,128)S(1)}, f32[48,768]{1,0:T(8,128)S(1)}, u32[]{:S(2)}, u32[]{:S(2)}) %collective-permute-start.68) | collective-permute-done | bytes 147488 | tf_op jit(solution)/shard_map/ppermute | solution.py:820
  559.7 30.9 %all-reduce.2.cloned.1.call-done = bf16[192,3072]{1,0:T(8,128)(2,1)} async-done(((bf16[192,3072]{1,0:T(8,128)(2,1)}), bf16[192,3072]{1,0:T(8,128)(2,1)}) %all-reduce.2.cloned.1.call-update) | async-done | bytes 1179664 | tf_op jit(solution)/shard_map/psum | solution.py:1177
  (318 shorter events, 247.6 us)
Async XLA Ops:
  7.2 583.4 %all-reduce.2.cloned.1.call-start = ((), (), s32[]{:S(2)}) async-start(), calls=%async_computation | async-start | bytes 2359296 | tf_op jit(solution)/shard_map/psum | solution.py:1177
  7.2 31.4 %collective-permute-start.4 = (bf16[192,2304]{1,0:T(8,128)(2,1)}, bf16[192,2304]{1,0:T(8,128)(2,1)S(1)}, u32[]{:S(2)}, u32[]{:S(2)}) collective-permute-start(bf16[192,2304]{1,0:T(8,128)(2,1)} %rest_3_.1), channel_id=1, source_target_pairs={{0,2},{1,3},{2,0},{3,1},{4,6},{5,7},{6,4},{7,5},{8,10},{9,11},{10,... | collective-permute-start | bytes 2654216 | tf_op jit(solution)/shard_map/ppermute | solution.py:112
  65.7 49.7 %collective-permute-start.19 = (bf16[1,3,256,768]{3,2,1,0:T(8,128)(2,1)}, bf16[1,3,256,768]{3,2,1,0:T(8,128)(2,1)S(1)}, u32[]{:S(2)}, u32[]{:S(2)}) collective-permute-start(bf16[1,3,256,768]{3,2,1,0:T(8,128)(2,1)} %get-tuple-element.219.refs_10_.refs_7_.refs_4_), channel_id=1, source_target_pairs={{0,2},{1,3},{2,0},{3,1},{4,6},{5,7},{6,4},{7,5},{8,10},{9,11},{10,... | collective-permute-start | bytes 3538952 | tf_op jit(solution)/shard_map/ppermute | solution.py:112
  67.2 48.2 %collective-permute-start.20 = (bf16[1,3,256,768]{3,2,1,0:T(8,128)(2,1)}, bf16[1,3,256,768]{3,2,1,0:T(8,128)(2,1)S(1)}, u32[]{:S(2)}, u32[]{:S(2)}) collective-permute-start(bf16[1,3,256,768]{3,2,1,0:T(8,128)(2,1)} %get-tuple-element.219.refs_10_.refs_7_.refs_4_), channel_id=1, source_target_pairs={{0,1},{1,0},{2,3},{3,2},{4,5},{5,4},{6,7},{7,6},{8,9},{9,8},{10,11... | collective-permute-start | bytes 3538952 | tf_op jit(solution)/shard_map/ppermute | solution.py:112
  115.4 33.9 %collective-permute-start.22 = (bf16[528,768]{1,0:T(8,128)(2,1)}, bf16[528,768]{1,0:T(8,128)(2,1)}, u32[]{:S(2)}, u32[]{:S(2)}) collective-permute-start(bf16[528,768]{1,0:T(8,128)(2,1)} %get-tuple-element.218.refs_1_.refs_0_.refs_10_), channel_id=1, source_target_pairs={{0,8},{8,16},{16,24},{24,28},{28,20},{20,12},{12,4},{4,0},{1,9},{9... | collective-permute-start | bytes 2433032 | tf_op jit(solution)/shard_map/ppermute | solution.py:119
  141.7 54.6 %collective-permute-start.32 = (bf16[1,3,256,768]{3,2,1,0:T(8,128)(2,1)}, bf16[1,3,256,768]{3,2,1,0:T(8,128)(2,1)S(1)}, u32[]{:S(2)}, u32[]{:S(2)}) collective-permute-start(bf16[1,3,256,768]{3,2,1,0:T(8,128)(2,1)} %pack_weights.3.refs_9_.refs_11_.refs_6_), channel_id=1, source_target_pairs={{0,2},{1,3},{2,0},{3,1},{4,6},{5,7},{6,4},{7,5},{8,10},{9,11},{10,... | collective-permute-start | bytes 3538952 | tf_op jit(solution)/shard_map/ppermute | solution.py:112
  143.3 30.4 %collective-permute-start.17 = (bf16[528,768]{1,0:T(8,128)(2,1)}, bf16[528,768]{1,0:T(8,128)(2,1)S(1)}, u32[]{:S(2)}, u32[]{:S(2)}) collective-permute-start(bf16[528,768]{1,0:T(8,128)(2,1)} %copy-done.14), channel_id=1, source_target_pairs={{0,1},{1,0},{2,3},{3,2},{4,5},{5,4},{6,7},{7,6},{8,9},{9,8},{10,11... | collective-permute-start | bytes 2433032 | tf_op jit(solution)/shard_map/ppermute | solution.py:112
  161.7 60.5 %collective-permute-start.34 = (bf16[1,3,256,768]{3,2,1,0:T(8,128)(2,1)S(1)}, bf16[1,3,256,768]{3,2,1,0:T(8,128)(2,1)S(1)}, u32[]{:S(2)}, u32[]{:S(2)}) collective-permute-start(bf16[1,3,256,768]{3,2,1,0:T(8,128)(2,1)S(1)} %copy-done.4), channel_id=1, source_target_pairs={{0,1},{1,0},{2,3},{3,2},{4,5},{5,4},{6,7},{7,6},{8,9},{9,8},{10,11... | collective-permute-start | bytes 3538952 | tf_op jit(solution)/shard_map/ppermute | solution.py:112
  244.1 36.7 %collective-permute-start.35 = (bf16[3,256,768]{2,1,0:T(8,128)(2,1)}, bf16[3,256,768]{2,1,0:T(8,128)(2,1)S(1)}, u32[]{:S(2)}, u32[]{:S(2)}) collective-permute-start(bf16[3,256,768]{2,1,0:T(8,128)(2,1)} %get-tuple-element.232), channel_id=1, source_target_pairs={{0,1},{1,0},{2,3},{3,2},{4,5},{5,4},{6,7},{7,6},{8,9},{9,8},{10,11... | collective-permute-start | bytes 3538952 | tf_op jit(solution)/shard_map/ppermute | solution.py:112
  246.6 40.1 %collective-permute-start.41 = (bf16[3,256,768]{2,1,0:T(8,128)(2,1)S(1)}, bf16[3,256,768]{2,1,0:T(8,128)(2,1)S(1)}, u32[]{:S(2)}, u32[]{:S(2)}) collective-permute-start(bf16[3,256,768]{2,1,0:T(8,128)(2,1)S(1)} %add_convert_fusion.4.refs_8_), channel_id=1, source_target_pairs={{0,2},{1,3},{2,0},{3,1},{4,6},{5,7},{6,4},{7,5},{8,10},{9,11},{10,... | collective-permute-start | bytes 3538952 | tf_op jit(solution)/shard_map/ppermute | solution.py:112
  288.8 31.8 %collective-permute-start.46 = (bf16[3,256,768]{2,1,0:T(8,128)(2,1)S(1)}, bf16[3,256,768]{2,1,0:T(8,128)(2,1)}, u32[]{:S(2)}, u32[]{:S(2)}) collective-permute-start(bf16[3,256,768]{2,1,0:T(8,128)(2,1)S(1)} %add_convert_fusion.2.refs_6_.piece), channel_id=1, source_target_pairs={{0,8},{8,16},{16,24},{24,28},{28,20},{20,12},{12,4},{4,0},{1,9},{9... | collective-permute-start | bytes 3538952 | tf_op jit(solution)/shard_map/ppermute | solution.py:119
  316.1 46.4 %collective-permute-start.49 = (bf16[3,256,768]{2,1,0:T(8,128)(2,1)S(1)}, bf16[3,256,768]{2,1,0:T(8,128)(2,1)S(1)}, u32[]{:S(2)}, u32[]{:S(2)}) collective-permute-start(bf16[3,256,768]{2,1,0:T(8,128)(2,1)S(1)} %add_convert_fusion.piece), channel_id=1, source_target_pairs={{0,4},{8,0},{16,8},{24,16},{28,24},{20,28},{12,20},{4,12},{1,5},{9... | collective-permute-start | bytes 3538952 | tf_op jit(solution)/shard_map/ppermute | solution.py:119
  320.6 45.2 %collective-permute-start.47 = (bf16[3,256,768]{2,1,0:T(8,128)(2,1)}, bf16[3,256,768]{2,1,0:T(8,128)(2,1)S(1)}, u32[]{:S(2)}, u32[]{:S(2)}) collective-permute-start(bf16[3,256,768]{2,1,0:T(8,128)(2,1)} %collective-permute-done.46.piece), channel_id=1, source_target_pairs={{0,8},{8,16},{16,24},{24,28},{28,20},{20,12},{12,4},{4,0},{1,9},{9... | collective-permute-start | bytes 3538952 | tf_op jit(solution)/shard_map/ppermute | solution.py:119
  365.8 32.6 %collective-permute-start.50 = (bf16[3,256,768]{2,1,0:T(8,128)(2,1)S(1)}, bf16[3,256,768]{2,1,0:T(8,128)(2,1)}, u32[]{:S(2)}, u32[]{:S(2)}) collective-permute-start(bf16[3,256,768]{2,1,0:T(8,128)(2,1)S(1)} %collective-permute-done.47.piece), channel_id=1, source_target_pairs={{0,8},{8,16},{16,24},{24,28},{28,20},{20,12},{12,4},{4,0},{1,9},{9... | collective-permute-start | bytes 3538952 | tf_op jit(solution)/shard_map/ppermute | solution.py:119
  400.1 30.2 %collective-permute-start.59 = (bf16[3,256,768]{2,1,0:T(8,128)(2,1)}, bf16[3,256,768]{2,1,0:T(8,128)(2,1)S(1)}, u32[]{:S(2)}, u32[]{:S(2)}) collective-permute-start(bf16[3,256,768]{2,1,0:T(8,128)(2,1)} %collective-permute-done.50.piece), channel_id=1, source_target_pairs={{0,8},{8,16},{16,24},{24,28},{28,20},{20,12},{12,4},{4,0},{1,9},{9... | collective-permute-start | bytes 3538952 | tf_op jit(solution)/shard_map/ppermute | solution.py:119
  400.6 32.0 %collective-permute-start.52 = (bf16[2,256,768]{2,1,0:T(8,128)(2,1)}, bf16[2,256,768]{2,1,0:T(8,128)(2,1)}, u32[]{:S(2)}, u32[]{:S(2)}) collective-permute-start(bf16[2,256,768]{2,1,0:T(8,128)(2,1)} %get-tuple-element.302), channel_id=1, source_target_pairs={{0,1},{1,0},{2,3},{3,2},{4,5},{5,4},{6,7},{7,6},{8,9},{9,8},{10,11... | collective-permute-start | bytes 2359304 | tf_op jit(solution)/shard_map/ppermute | solution.py:112
  400.6 32.0 %collective-permute-start.53 = (bf16[2,256,768]{2,1,0:T(8,128)(2,1)}, bf16[2,256,768]{2,1,0:T(8,128)(2,1)}, u32[]{:S(2)}, u32[]{:S(2)}) collective-permute-start(bf16[2,256,768]{2,1,0:T(8,128)(2,1)} %get-tuple-element.304), channel_id=1, source_target_pairs={{0,1},{1,0},{2,3},{3,2},{4,5},{5,4},{6,7},{7,6},{8,9},{9,8},{10,11... | collective-permute-start | bytes 2359304 | tf_op jit(solution)/shard_map/ppermute | solution.py:112
  402.1 30.5 %collective-permute-start.55 = (bf16[2,256,768]{2,1,0:T(8,128)(2,1)}, bf16[2,256,768]{2,1,0:T(8,128)(2,1)}, u32[]{:S(2)}, u32[]{:S(2)}) collective-permute-start(bf16[2,256,768]{2,1,0:T(8,128)(2,1)} %add_convert_fusion.6), channel_id=1, source_target_pairs={{0,2},{1,3},{2,0},{3,1},{4,6},{5,7},{6,4},{7,5},{8,10},{9,11},{10,... | collective-permute-start | bytes 2359304 | tf_op jit(solution)/shard_map/ppermute | solution.py:112
  430.3 31.2 %collective-permute-start.61 = (bf16[3,256,768]{2,1,0:T(8,128)(2,1)S(1)}, bf16[3,256,768]{2,1,0:T(8,128)(2,1)}, u32[]{:S(2)}, u32[]{:S(2)}) collective-permute-start(bf16[3,256,768]{2,1,0:T(8,128)(2,1)S(1)} %collective-permute-done.59.piece), channel_id=1, source_target_pairs={{0,8},{8,16},{16,24},{24,28},{28,20},{20,12},{12,4},{4,0},{1,9},{9... | collective-permute-start | bytes 3538952 | tf_op jit(solution)/shard_map/ppermute | solution.py:119
  462.9 29.6 %collective-permute-start.63 = (bf16[3,256,768]{2,1,0:T(8,128)(2,1)}, bf16[3,256,768]{2,1,0:T(8,128)(2,1)S(1)}, u32[]{:S(2)}, u32[]{:S(2)}) collective-permute-start(bf16[3,256,768]{2,1,0:T(8,128)(2,1)} %collective-permute-done.61.piece), channel_id=1, source_target_pairs={{0,8},{8,16},{16,24},{24,28},{28,20},{20,12},{12,4},{4,0},{1,9},{9... | collective-permute-start | bytes 3538952 | tf_op jit(solution)/shard_map/ppermute | solution.py:119
  488.2 38.4 %collective-permute-start.65 = (bf16[3,256,768]{2,1,0:T(8,128)(2,1)}, bf16[3,256,768]{2,1,0:T(8,128)(2,1)}, u32[]{:S(2)}, u32[]{:S(2)}) collective-permute-start(bf16[3,256,768]{2,1,0:T(8,128)(2,1)} %collective-permute-done.64.piece), channel_id=1, source_target_pairs={{0,4},{8,0},{16,8},{24,16},{28,24},{20,28},{12,20},{4,12},{1,5},{9... | collective-permute-start | bytes 3538952 | tf_op jit(solution)/shard_map/ppermute | solution.py:119
  492.6 64.3 %collective-permute-start.72 = (bf16[3,256,768]{2,1,0:T(8,128)(2,1)S(1)}, bf16[3,256,768]{2,1,0:T(8,128)(2,1)}, u32[]{:S(2)}, u32[]{:S(2)}) collective-permute-start(bf16[3,256,768]{2,1,0:T(8,128)(2,1)S(1)} %collective-permute-done.63.piece), channel_id=1, source_target_pairs={{0,8},{8,16},{16,24},{24,28},{28,20},{20,12},{12,4},{4,0},{1,9},{9... | collective-permute-start | bytes 3538952 | tf_op jit(solution)/shard_map/ppermute | solution.py:119
  540.8 56.4 %collective-permute-start.71 = (bf16[3,256,768]{2,1,0:T(8,128)(2,1)}, bf16[3,256,768]{2,1,0:T(8,128)(2,1)S(1)}, u32[]{:S(2)}, u32[]{:S(2)}) collective-permute-start(bf16[3,256,768]{2,1,0:T(8,128)(2,1)} %collective-permute-done.65.piece), channel_id=1, source_target_pairs={{0,4},{8,0},{16,8},{24,16},{28,24},{20,28},{12,20},{4,12},{1,5},{9... | collective-permute-start | bytes 3538952 | tf_op jit(solution)/shard_map/ppermute | solution.py:119
  551.7 42.4 %collective-permute-start.70 = (f32[48,768]{1,0:T(8,128)S(1)}, f32[48,768]{1,0:T(8,128)S(1)}, u32[]{:S(2)}, u32[]{:S(2)}) collective-permute-start(f32[48,768]{1,0:T(8,128)S(1)} %add.282), channel_id=1, source_target_pairs={{0,2},{1,3},{2,0},{3,1},{4,6},{5,7},{6,4},{7,5},{8,10},{9,11},{10,... | collective-permute-start | bytes 442376 | tf_op jit(solution)/shard_map/ppermute | solution.py:820
  (109 other events, 1574.0 us)
Sparse Core Ops, SparseCore 0:
  497.8 92.7 all-reduce.1

commit v4 on v3

--- a/solution.py
+++ b/solution.py
@@ -708,26 +708,29 @@
     (base, cot, blk, info_ref, slots, routes, res_ref, gain, vectors, mixers_t, resid_t, prev, w_out) = refs[
         group * per : group * per + 13
     ]
-    layer_out, grad_out, mix_out, mixed_out, prev_out, small_out = refs[group * per + 13 :]
+    layer_out, grad_out, mix_out, mixed_out, prev_out, small_out = refs[
+        group * per + 13 : group * per + 19
+    ]
+    out_rows, back_rows, pick0, pick1 = refs[group * per + 19 :]
     info = info_ref[...]
     first, second = routes[:, 0:1], routes[:, 1:2]
     lane = lax.broadcasted_iota(jnp.int32, (1, LANES), 1)
     slot_lane = lane.astype(F32)
     taken = slots[...]
-    out0 = out1 = back = None
     for offset in range(group):
         for member in range(per):
             expert = (scal[offset] * per + member) // share
             column = jnp.sum(jnp.where(lane == expert, taken, 0.0), axis=1, keepdims=True)
-            chooser = column == slot_lane
-            piece = pieces[offset * per + member]
-            pick0 = jnp.where(chooser & (first == expert), 1.0, 0.0).astype(BF16)
-            pick1 = jnp.where(chooser & (second == expert), 1.0, 0.0).astype(BF16)
-            add0, add1 = mm(pick0, piece[0]), mm(pick1, piece[0])
-            add2 = mm(pick0 + pick1, piece[1])
-            out0 = add0 if out0 is None else out0 + add0
-            out1 = add1 if out1 is None else out1 + add1
-            back = add2 if back is None else back + add2
+            at = offset * per + member
+            span = slice(at * CAP, (at + 1) * CAP)
+            out_rows[span, :] = pieces[at][0]
+            back_rows[span, :] = pieces[at][1]
+            column0 = jnp.where(first == expert, column, -1.0)
+            column1 = jnp.where(second == expert, column, -1.0)
+            pick0[:, span] = jnp.where(column0 == slot_lane, 1.0, 0.0).astype(BF16)
+            pick1[:, span] = jnp.where(column1 == slot_lane, 1.0, 0.0).astype(BF16)
+    out0, out1 = mm(pick0[...], out_rows[...]), mm(pick1[...], out_rows[...])
+    back = mm(pick0[...] + pick1[...], back_rows[...])
     get = lambda at: info[:, at : at + 1]
     gate0, gate1, hidden_part, both = get(12), get(13), get(14), get(21)
     layer_out[...] = base[...] + gate0 * out0 + gate1 * out1
@@ -1117,6 +1120,12 @@
             shape_of((SMALL_ROWS, D), F32),
         ],
         6 * TOK_DEV * group * per * CAP * D + 2 * TOK_DEV * D * D,
+        scratch=[
+            pltpu.VMEM((group * per * CAP, D), BF16),
+            pltpu.VMEM((group * per * CAP, D), BF16),
+            pltpu.VMEM((TOK_DEV, group * per * CAP), BF16),
+            pltpu.VMEM((TOK_DEV, group * per * CAP), BF16),
+        ],
         waits=arrived(1, 0) if W_RING else (),
     )
 

time: 619 us -> 613 us (level)
  transfers between devices with their start and end apart: 74 -> 74, of which waited for: 28 -> 28; matrix products, arithmetic and copies ran while one was open for 6% -> 6% of each run, Pallas kernels for 38% -> 37%
where the time goes in v4:
time: 613 us; the launch traced here: 604 us
  Pallas kernels  248 us (40%)
  waiting for transfers between devices  228 us (37%)
  starting transfers between devices  64.8 us (11%)
  local copies, waits for them, and re-layouts  24.8 us (4%)
  other arithmetic  17.4 us (3%)
  between operations  14.9 us (2%)
    ppermute x28, waiting for transfers between devices, ring_permute(): return lax.ppermute(value, 'rep', pairs)  99.6 us
    ppermute x40, waiting for transfers between devices, xor_permute(): return lax.ppermute(value, 'grp', pairs)  79.3 us
    pallas_call x5, Pallas kernels, whole_call(): pl.pallas_call(without(kernel, 1 + len(arrays), len(waits)), out_shape=tu...  52.2 us
    pallas_call x16, Pallas kernels, place_slice(): pl.pallas_call(partial(place_kernel, len(held)), out_shape=(shape_of((D,...  48.1 us
    pallas_call x2, Pallas kernels, weight_slices(): pl.pallas_call(without(partial(slice_kernel, many), 3 + many, len(waits))...  35.6 us
    ppermute x28, starting transfers between devices, ring_permute(): return lax.ppermute(value, 'rep', pairs)  35.5 us
    psum x1, waiting for transfers between devices, body(): dense = lax.psum(held[0].astype(BF16), 'rep').astype(F32)  31.3 us
    pallas_call x2, Pallas kernels, local_expert(): pl.pallas_call(without(partial(expert_kernel, group, offsets), 5, len(wai...  31.2 us
  transfers between devices with their start and end apart: 74, of which 28 were waited for; matrix products, arithmetic and copies ran while one was open for 6% of the time, Pallas kernels for 37%

profile of v4, /device:TPU:0, one launch (start us, length us, event | category | flops | bytes accessed | tf_op | source)
XLA Modules:
  0.0 604.5 jit_solution(15240610977578466882)
XLA Ops:
  25.2 13.4 %collective-permute-done.1.rest_1_ = bf16[256,768]{1,0:T(8,128)(2,1)} collective-permute-done((bf16[256,768]{1,0:T(8,128)(2,1)}, bf16[256,768]{1,0:T(8,128)(2,1)}, u32[]{:S(2)}, u32[]{:S(2)}) %collective-permute-start.1) | collective-permute-done | bytes 393248 | tf_op jit(solution)/shard_map/ppermute | solution.py:112
  50.4 12.2 %projections.1 = (bf16[512,768]{1,0:T(8,128)(2,1)}, bf16[1024,768]{1,0:T(8,128)(2,1)}, bf16[1024,768]{1,0:T(8,128)(2,1)}, bf16[512,768]{1,0:T(8,128)(2,1)}, bf16...) custom-call(s32[6]{0:T(128)} %pad_add_fusion.scal.refs_0_, ...), custom_call_target="tpu_custom_call" | custom-call | flops 4227858432 | bytes 20302848 | tf_op jit(solution)/shard_map/projections/pallas_call | solution.py:96
  72.7 18.6 %attention_forward.1 = (f32[512,768]{1,0:T(8,128)}, f32[512,768]{1,0:T(8,128)}) custom-call(s32[6]{0:T(128)} %pad_add_fusion.scal.refs_0_, bf16[512,768]{1,0:T(8,128)(2,1)} %get-tuple-element.206.refs_1_.q_ref, bf16[1024,768]{1,0:T(8,128)(2,1)} %get-tuple-element.207.refs_2_.kp_ref, bf16[1024,768]{1,0:T(8,128)(2,1)} %get-tuple-element.208.refs_3_.vp_ref, ...), custom_call_target="tpu_custom_call" | custom-call | flops 8053063680 | bytes 7864320 | tf_op jit(solution)/shard_map/attention_forward/pallas_call | solution.py:281
  94.5 10.0 %routing.1 = (bf16[768,768]{1,0:T(8,128)(2,1)}, f32[512,768]{1,0:T(8,128)}, f32[512,768]{1,0:T(8,128)}, bf16[528,768]{1,0:T(8,128)(2,1)}, f32[512,128]{1,0:T(8,128)}, /*index=5*/bf16[512,768]{1,0:T(8,128)(2,1)}) custom-call(s32[6]{0:T(128)} %pad_add_fusion.scal.refs_0_, bf16[512,768]{1,0:T(8,128)(2,1)} %bitcast.49, ...), custom_call_target="tpu_custom_call" | custom-call | flops 603979776 | bytes 10472448 | tf_op jit(solution)/shard_map/routing/pallas_call | solution.py:96
  117.3 15.0 %collective-permute-done.15.refs_4_.refs_2_ = bf16[528,768]{1,0:T(8,128)(2,1)S(1)} collective-permute-done((bf16[528,768]{1,0:T(8,128)(2,1)}, bf16[528,768]{1,0:T(8,128)(2,1)S(1)}, u32[]{:S(2)}, u32[]{:S(2)}) %collective-permute-start.15) | collective-permute-done | bytes 811040 | tf_op jit(solution)/shard_map/ppermute | solution.py:112
  154.1 7.6 %column_rows.5 = (bf16[8,8,128,768]{3,2,1,0:T(8,128)(2,1)}, bf16[8,8,128,768]{3,2,1,0:T(8,128)(2,1)}) custom-call(bf16[528,768]{1,0:T(8,128)(2,1)} %collective-permute-done.22.refs_0_, bf16[528,768]{1,0:T(8,128)(2,1)} %collective-permute-done.28.refs_1_, ...), custom_call_target="tpu_custom_call", output_to_operand_aliasing={{0}: (4, {}), {1}: (5, {})} | custom-call | flops 12884901888 | bytes 38141952 | tf_op jit(solution)/shard_map/column_rows/pallas_call | solution.py:530
  180.7 15.4 %local_expert.2 = (bf16[2,128,768]{2,1,0:T(8,128)(2,1)}, bf16[2,128,768]{2,1,0:T(8,128)(2,1)}, bf16[2,128,768]{2,1,0:T(8,128)(2,1)}, bf16[2,128,768]{2,1,0:T(8,128)(2,1)}) custom-call(bf16[2,512,768]{2,1,0:T(8,128)(2,1)} %get-tuple-element.220.x_ref.refs_0_, bf16[2,512,768]{2,1,0:T(8,128)(2,1)} %get-tuple-element.221.s_ref.refs_1_, ...), custom_call_target="tpu_custom_call" | custom-call | flops 9663676416 | bytes 12582912 | tf_op jit(solution)/shard_map/local_expert/pallas_call | solution.py:603
  197.2 12.5 %column_rows.6 = (bf16[8,8,128,768]{3,2,1,0:T(8,128)(2,1)}, bf16[8,8,128,768]{3,2,1,0:T(8,128)(2,1)}) custom-call(bf16[528,768]{1,0:T(8,128)(2,1)} %copy-done.45, bf16[528,768]{1,0:T(8,128)(2,1)} %collective-permute-done.29.refs_1_, bf16[528,768]{1,0:T(8,128)(2,1)} %copy-done.46, ...), custom_call_target="tpu_custom_call", output_to_operand_aliasing={{0}: (8, {}), {1}: (9, {})} | custom-call | flops 25769803776 | bytes 76283904 | tf_op jit(solution)/shard_map/column_rows/pallas_call | solution.py:530
  223.5 17.9 %weight_slices.2 = (bf16[3,256,768]{2,1,0:T(8,128)(2,1)}, bf16[3,256,768]{2,1,0:T(8,128)(2,1)}, bf16[3,256,768]{2,1,0:T(8,128)(2,1)}, bf16[3,256,768]{2,1,0:T(8,128)(2,1)}) custom-call(s32[4]{0:T(128)} %pad_add_fusion.1.refs_0_, bf16[8,8,128,768]{3,2,1,0:T(8,128)(2,1)} %get-tuple-element.229.refs_1_, bf16[8,8,128,768]{3,2,1,0:T(8,128)(2,1)} %get-tuple-element.230.refs_2_, ...), custom_call_target="tpu_custom_call" | custom-call | flops 9663676416 | bytes 22020096 | tf_op jit(solution)/shard_map/weight_slices/pallas_call | solution.py:663
  253.9 7.4 %collective-permute-done.39.refs_11_.refs_6_ = bf16[2,128,768]{2,1,0:T(8,128)(2,1)S(1)} collective-permute-done((bf16[2,128,768]{2,1,0:T(8,128)(2,1)S(1)}, bf16[2,128,768]{2,1,0:T(8,128)(2,1)S(1)}, u32[]{:S(2)}, u32[]{:S(2)}) %collective-permute-start.39) | collective-permute-done | bytes 393248 | tf_op jit(solution)/shard_map/ppermute | solution.py:112
  262.1 17.7 %weight_slices.3 = (bf16[3,256,768]{2,1,0:T(8,128)(2,1)}, bf16[3,256,768]{2,1,0:T(8,128)(2,1)}, bf16[3,256,768]{2,1,0:T(8,128)(2,1)}, bf16[3,256,768]{2,1,0:T(8,128)(2,1)}) custom-call(s32[4]{0:T(128)} %pad_add_fusion.2.refs_0_, bf16[8,8,128,768]{3,2,1,0:T(8,128)(2,1)} %get-tuple-element.229.refs_1_, bf16[8,8,128,768]{3,2,1,0:T(8,128)(2,1)} %get-tuple-element.230.refs_2_, ...), custom_call_target="tpu_custom_call" | custom-call | flops 9663676416 | bytes 22020096 | tf_op jit(solution)/shard_map/weight_slices/pallas_call | solution.py:663
  289.3 15.9 %local_expert.3 = (bf16[2,128,768]{2,1,0:T(8,128)(2,1)}, bf16[2,128,768]{2,1,0:T(8,128)(2,1)}, bf16[2,128,768]{2,1,0:T(8,128)(2,1)}, bf16[2,128,768]{2,1,0:T(8,128)(2,1)}) custom-call(bf16[2,512,768]{2,1,0:T(8,128)(2,1)} %get-tuple-element.220.x_ref.refs_0_, bf16[2,512,768]{2,1,0:T(8,128)(2,1)} %get-tuple-element.221.s_ref.refs_1_, ...), custom_call_target="tpu_custom_call" | custom-call | flops 9663676416 | bytes 12582912 | tf_op jit(solution)/shard_map/local_expert/pallas_call | solution.py:603
  305.2 9.2 %collective-permute-done.42 = bf16[3,256,768]{2,1,0:T(8,128)(2,1)S(1)} collective-permute-done((bf16[3,256,768]{2,1,0:T(8,128)(2,1)S(1)}, bf16[3,256,768]{2,1,0:T(8,128)(2,1)S(1)}, u32[]{:S(2)}, u32[]{:S(2)}) %collective-permute-start.42) | collective-permute-done | bytes 1179680 | tf_op jit(solution)/shard_map/ppermute | solution.py:112
  325.8 7.5 %collective-permute-done.44.refs_5_ = bf16[2,128,768]{2,1,0:T(8,128)(2,1)} collective-permute-done((bf16[2,128,768]{2,1,0:T(8,128)(2,1)}, bf16[2,128,768]{2,1,0:T(8,128)(2,1)}, u32[]{:S(2)}, u32[]{:S(2)}) %collective-permute-start.44) | collective-permute-done | bytes 393248 | tf_op jit(solution)/shard_map/ppermute | solution.py:112
  333.3 7.7 %collective-permute-done.45.refs_7_ = bf16[2,128,768]{2,1,0:T(8,128)(2,1)} collective-permute-done((bf16[2,128,768]{2,1,0:T(8,128)(2,1)}, bf16[2,128,768]{2,1,0:T(8,128)(2,1)}, u32[]{:S(2)}, u32[]{:S(2)}) %collective-permute-start.45) | collective-permute-done | bytes 393248 | tf_op jit(solution)/shard_map/ppermute | solution.py:112
  341.0 15.6 %combine.1 = (f32[512,768]{1,0:T(8,128)}, f32[512,768]{1,0:T(8,128)}, bf16[512,768]{1,0:T(8,128)(2,1)}, bf16[512,768]{1,0:T(8,128)(2,1)}, f32[512,128]{1,0:T(8,128)}, /*index=5*/f32[40,768]{1,0:T(8,128)}) custom-call(s32[6]{0:T(128)} %pad_add_fusion.scal.refs_0_, bf16[2,128,768]{2,1,0:T(8,128)(2,1)} %get-tuple-element.222.refs_10_.refs_0_, ...), custom_call_target="tpu_custom_call" | custom-call | flops 3019898880 | bytes 15477760 | tf_op jit(solution)/shard_map/combine/pallas_call | solution.py:96
  362.0 24.7 %attention_backward.1 = (bf16[512,768]{1,0:T(8,128)(2,1)}, bf16[2,256,768]{2,1,0:T(8,128)(2,1)}, bf16[2,256,768]{2,1,0:T(8,128)(2,1)}, bf16[2,256,768]{2,1,0:T(8...) custom-call(s32[6]{0:T(128)} %pad_add_fusion.scal.refs_0_, ...), custom_call_target="tpu_custom_call" | custom-call | flops 20132659200 | bytes 15728640 | tf_op jit(solution)/shard_map/attention_backward/pallas_call | solution.py:368
  403.5 17.8 %collective-permute-done.60.piece = bf16[3,256,768]{2,1,0:T(8,128)(2,1)S(1)} collective-permute-done((bf16[3,256,768]{2,1,0:T(8,128)(2,1)}, bf16[3,256,768]{2,1,0:T(8,128)(2,1)S(1)}, u32[]{:S(2)}, u32[]{:S(2)}) %collective-permute-start.60) | collective-permute-done | bytes 1179680 | tf_op jit(solution)/shard_map/ppermute | solution.py:119
  426.6 8.0 %finish.1 = (bf16[512,2304]{1,0:T(8,128)(2,1)}, f32[512,768]{1,0:T(8,128)}, f32[8,768]{1,0:T(8,128)}) custom-call(s32[6]{0:T(128)} %pad_add_fusion.scal.refs_0_, bf16[512,768]{1,0:T(8,128)(2,1)} %get-tuple-element.261.dq, f32[2,256,768]{2,1,0:T(8,128)} %get-tuple-element.262.own, bf16[2,256,768]{2,1,0:T(8,128)(2,1)} %collective-permute-done.52.received, ...), custom_call_target="tpu_custom_call" | custom-call | flops 1811939328 | bytes 15363072 | tf_op jit(solution)/shard_map/finish/pallas_call | solution.py:96
  445.3 7.2 %collective-permute-done.62.piece = bf16[3,256,768]{2,1,0:T(8,128)(2,1)} collective-permute-done((bf16[3,256,768]{2,1,0:T(8,128)(2,1)S(1)}, bf16[3,256,768]{2,1,0:T(8,128)(2,1)}, u32[]{:S(2)}, u32[]{:S(2)}) %collective-permute-start.62) | collective-permute-done | bytes 1179680 | tf_op jit(solution)/shard_map/ppermute | solution.py:119
  464.8 17.3 %collective-permute-done.64.piece = bf16[3,256,768]{2,1,0:T(8,128)(2,1)} collective-permute-done((bf16[3,256,768]{2,1,0:T(8,128)(2,1)}, bf16[3,256,768]{2,1,0:T(8,128)(2,1)}, u32[]{:S(2)}, u32[]{:S(2)}) %collective-permute-start.64) | collective-permute-done | bytes 1179680 | tf_op jit(solution)/shard_map/ppermute | solution.py:119
  495.5 25.0 %collective-permute-done.65.piece = bf16[3,256,768]{2,1,0:T(8,128)(2,1)} collective-permute-done((bf16[3,256,768]{2,1,0:T(8,128)(2,1)}, bf16[3,256,768]{2,1,0:T(8,128)(2,1)}, u32[]{:S(2)}, u32[]{:S(2)}) %collective-permute-start.65) | collective-permute-done | bytes 1179680 | tf_op jit(solution)/shard_map/ppermute | solution.py:119
  536.8 7.1 %collective-permute-done.68 = f32[48,768]{1,0:T(8,128)S(1)} collective-permute-done((f32[48,768]{1,0:T(8,128)S(1)}, f32[48,768]{1,0:T(8,128)S(1)}, u32[]{:S(2)}, u32[]{:S(2)}) %collective-permute-start.68) | collective-permute-done | bytes 147488 | tf_op jit(solution)/shard_map/ppermute | solution.py:823
  553.4 31.3 %all-reduce.2.cloned.1.call-done = bf16[192,3072]{1,0:T(8,128)(2,1)} async-done(((bf16[192,3072]{1,0:T(8,128)(2,1)}), bf16[192,3072]{1,0:T(8,128)(2,1)}) %all-reduce.2.cloned.1.call-update) | async-done | bytes 1179664 | tf_op jit(solution)/shard_map/psum | solution.py:1186
  (318 shorter events, 247.5 us)
Async XLA Ops:
  7.2 577.5 %all-reduce.2.cloned.1.call-start = ((), (), s32[]{:S(2)}) async-start(), calls=%async_computation | async-start | bytes 2359296 | tf_op jit(solution)/shard_map/psum | solution.py:1186
  7.2 31.4 %collective-permute-start.4 = (bf16[192,2304]{1,0:T(8,128)(2,1)}, bf16[192,2304]{1,0:T(8,128)(2,1)S(1)}, u32[]{:S(2)}, u32[]{:S(2)}) collective-permute-start(bf16[192,2304]{1,0:T(8,128)(2,1)} %rest_3_.1), channel_id=1, source_target_pairs={{0,2},{1,3},{2,0},{3,1},{4,6},{5,7},{6,4},{7,5},{8,10},{9,11},{10,... | collective-permute-start | bytes 2654216 | tf_op jit(solution)/shard_map/ppermute | solution.py:112
  65.7 49.7 %collective-permute-start.19 = (bf16[1,3,256,768]{3,2,1,0:T(8,128)(2,1)}, bf16[1,3,256,768]{3,2,1,0:T(8,128)(2,1)S(1)}, u32[]{:S(2)}, u32[]{:S(2)}) collective-permute-start(bf16[1,3,256,768]{3,2,1,0:T(8,128)(2,1)} %get-tuple-element.219.refs_10_.refs_7_.refs_4_), channel_id=1, source_target_pairs={{0,2},{1,3},{2,0},{3,1},{4,6},{5,7},{6,4},{7,5},{8,10},{9,11},{10,... | collective-permute-start | bytes 3538952 | tf_op jit(solution)/shard_map/ppermute | solution.py:112
  67.2 48.2 %collective-permute-start.20 = (bf16[1,3,256,768]{3,2,1,0:T(8,128)(2,1)}, bf16[1,3,256,768]{3,2,1,0:T(8,128)(2,1)S(1)}, u32[]{:S(2)}, u32[]{:S(2)}) collective-permute-start(bf16[1,3,256,768]{3,2,1,0:T(8,128)(2,1)} %get-tuple-element.219.refs_10_.refs_7_.refs_4_), channel_id=1, source_target_pairs={{0,1},{1,0},{2,3},{3,2},{4,5},{5,4},{6,7},{7,6},{8,9},{9,8},{10,11... | collective-permute-start | bytes 3538952 | tf_op jit(solution)/shard_map/ppermute | solution.py:112
  115.4 33.9 %collective-permute-start.22 = (bf16[528,768]{1,0:T(8,128)(2,1)}, bf16[528,768]{1,0:T(8,128)(2,1)}, u32[]{:S(2)}, u32[]{:S(2)}) collective-permute-start(bf16[528,768]{1,0:T(8,128)(2,1)} %get-tuple-element.218.refs_1_.refs_0_.refs_10_), channel_id=1, source_target_pairs={{0,8},{8,16},{16,24},{24,28},{28,20},{20,12},{12,4},{4,0},{1,9},{9... | collective-permute-start | bytes 2433032 | tf_op jit(solution)/shard_map/ppermute | solution.py:119
  141.7 54.4 %collective-permute-start.32 = (bf16[1,3,256,768]{3,2,1,0:T(8,128)(2,1)}, bf16[1,3,256,768]{3,2,1,0:T(8,128)(2,1)S(1)}, u32[]{:S(2)}, u32[]{:S(2)}) collective-permute-start(bf16[1,3,256,768]{3,2,1,0:T(8,128)(2,1)} %pack_weights.3.refs_9_.refs_11_.refs_6_), channel_id=1, source_target_pairs={{0,2},{1,3},{2,0},{3,1},{4,6},{5,7},{6,4},{7,5},{8,10},{9,11},{10,... | collective-permute-start | bytes 3538952 | tf_op jit(solution)/shard_map/ppermute | solution.py:112
  143.3 30.2 %collective-permute-start.17 = (bf16[528,768]{1,0:T(8,128)(2,1)}, bf16[528,768]{1,0:T(8,128)(2,1)S(1)}, u32[]{:S(2)}, u32[]{:S(2)}) collective-permute-start(bf16[528,768]{1,0:T(8,128)(2,1)} %copy-done.14), channel_id=1, source_target_pairs={{0,1},{1,0},{2,3},{3,2},{4,5},{5,4},{6,7},{7,6},{8,9},{9,8},{10,11... | collective-permute-start | bytes 2433032 | tf_op jit(solution)/shard_map/ppermute | solution.py:112
  161.7 60.3 %collective-permute-start.34 = (bf16[1,3,256,768]{3,2,1,0:T(8,128)(2,1)S(1)}, bf16[1,3,256,768]{3,2,1,0:T(8,128)(2,1)S(1)}, u32[]{:S(2)}, u32[]{:S(2)}) collective-permute-start(bf16[1,3,256,768]{3,2,1,0:T(8,128)(2,1)S(1)} %copy-done.4), channel_id=1, source_target_pairs={{0,1},{1,0},{2,3},{3,2},{4,5},{5,4},{6,7},{7,6},{8,9},{9,8},{10,11... | collective-permute-start | bytes 3538952 | tf_op jit(solution)/shard_map/ppermute | solution.py:112
  244.1 36.5 %collective-permute-start.35 = (bf16[3,256,768]{2,1,0:T(8,128)(2,1)}, bf16[3,256,768]{2,1,0:T(8,128)(2,1)S(1)}, u32[]{:S(2)}, u32[]{:S(2)}) collective-permute-start(bf16[3,256,768]{2,1,0:T(8,128)(2,1)} %get-tuple-element.232), channel_id=1, source_target_pairs={{0,1},{1,0},{2,3},{3,2},{4,5},{5,4},{6,7},{7,6},{8,9},{9,8},{10,11... | collective-permute-start | bytes 3538952 | tf_op jit(solution)/shard_map/ppermute | solution.py:112
  246.6 40.1 %collective-permute-start.41 = (bf16[3,256,768]{2,1,0:T(8,128)(2,1)S(1)}, bf16[3,256,768]{2,1,0:T(8,128)(2,1)S(1)}, u32[]{:S(2)}, u32[]{:S(2)}) collective-permute-start(bf16[3,256,768]{2,1,0:T(8,128)(2,1)S(1)} %add_convert_fusion.4.refs_8_), channel_id=1, source_target_pairs={{0,2},{1,3},{2,0},{3,1},{4,6},{5,7},{6,4},{7,5},{8,10},{9,11},{10,... | collective-permute-start | bytes 3538952 | tf_op jit(solution)/shard_map/ppermute | solution.py:112
  288.8 31.8 %collective-permute-start.46 = (bf16[3,256,768]{2,1,0:T(8,128)(2,1)S(1)}, bf16[3,256,768]{2,1,0:T(8,128)(2,1)}, u32[]{:S(2)}, u32[]{:S(2)}) collective-permute-start(bf16[3,256,768]{2,1,0:T(8,128)(2,1)S(1)} %add_convert_fusion.2.refs_6_.piece), channel_id=1, source_target_pairs={{0,8},{8,16},{16,24},{24,28},{28,20},{20,12},{12,4},{4,0},{1,9},{9... | collective-permute-start | bytes 3538952 | tf_op jit(solution)/shard_map/ppermute | solution.py:119
  316.2 40.4 %collective-permute-start.49 = (bf16[3,256,768]{2,1,0:T(8,128)(2,1)S(1)}, bf16[3,256,768]{2,1,0:T(8,128)(2,1)S(1)}, u32[]{:S(2)}, u32[]{:S(2)}) collective-permute-start(bf16[3,256,768]{2,1,0:T(8,128)(2,1)S(1)} %add_convert_fusion.piece), channel_id=1, source_target_pairs={{0,4},{8,0},{16,8},{24,16},{28,24},{20,28},{12,20},{4,12},{1,5},{9... | collective-permute-start | bytes 3538952 | tf_op jit(solution)/shard_map/ppermute | solution.py:119
  320.7 39.2 %collective-permute-start.47 = (bf16[3,256,768]{2,1,0:T(8,128)(2,1)}, bf16[3,256,768]{2,1,0:T(8,128)(2,1)S(1)}, u32[]{:S(2)}, u32[]{:S(2)}) collective-permute-start(bf16[3,256,768]{2,1,0:T(8,128)(2,1)} %collective-permute-done.46.piece), channel_id=1, source_target_pairs={{0,8},{8,16},{16,24},{24,28},{28,20},{20,12},{12,4},{4,0},{1,9},{9... | collective-permute-start | bytes 3538952 | tf_op jit(solution)/shard_map/ppermute | solution.py:119
  359.9 32.7 %collective-permute-start.50 = (bf16[3,256,768]{2,1,0:T(8,128)(2,1)S(1)}, bf16[3,256,768]{2,1,0:T(8,128)(2,1)}, u32[]{:S(2)}, u32[]{:S(2)}) collective-permute-start(bf16[3,256,768]{2,1,0:T(8,128)(2,1)S(1)} %collective-permute-done.47.piece), channel_id=1, source_target_pairs={{0,8},{8,16},{16,24},{24,28},{28,20},{20,12},{12,4},{4,0},{1,9},{9... | collective-permute-start | bytes 3538952 | tf_op jit(solution)/shard_map/ppermute | solution.py:119
  394.3 30.2 %collective-permute-start.59 = (bf16[3,256,768]{2,1,0:T(8,128)(2,1)}, bf16[3,256,768]{2,1,0:T(8,128)(2,1)S(1)}, u32[]{:S(2)}, u32[]{:S(2)}) collective-permute-start(bf16[3,256,768]{2,1,0:T(8,128)(2,1)} %collective-permute-done.50.piece), channel_id=1, source_target_pairs={{0,8},{8,16},{16,24},{24,28},{28,20},{20,12},{12,4},{4,0},{1,9},{9... | collective-permute-start | bytes 3538952 | tf_op jit(solution)/shard_map/ppermute | solution.py:119
  394.7 31.8 %collective-permute-start.52 = (bf16[2,256,768]{2,1,0:T(8,128)(2,1)}, bf16[2,256,768]{2,1,0:T(8,128)(2,1)}, u32[]{:S(2)}, u32[]{:S(2)}) collective-permute-start(bf16[2,256,768]{2,1,0:T(8,128)(2,1)} %get-tuple-element.302), channel_id=1, source_target_pairs={{0,1},{1,0},{2,3},{3,2},{4,5},{5,4},{6,7},{7,6},{8,9},{9,8},{10,11... | collective-permute-start | bytes 2359304 | tf_op jit(solution)/shard_map/ppermute | solution.py:112
  394.7 31.8 %collective-permute-start.53 = (bf16[2,256,768]{2,1,0:T(8,128)(2,1)}, bf16[2,256,768]{2,1,0:T(8,128)(2,1)}, u32[]{:S(2)}, u32[]{:S(2)}) collective-permute-start(bf16[2,256,768]{2,1,0:T(8,128)(2,1)} %get-tuple-element.304), channel_id=1, source_target_pairs={{0,1},{1,0},{2,3},{3,2},{4,5},{5,4},{6,7},{7,6},{8,9},{9,8},{10,11... | collective-permute-start | bytes 2359304 | tf_op jit(solution)/shard_map/ppermute | solution.py:112
  396.3 30.2 %collective-permute-start.55 = (bf16[2,256,768]{2,1,0:T(8,128)(2,1)}, bf16[2,256,768]{2,1,0:T(8,128)(2,1)}, u32[]{:S(2)}, u32[]{:S(2)}) collective-permute-start(bf16[2,256,768]{2,1,0:T(8,128)(2,1)} %add_convert_fusion.6), channel_id=1, source_target_pairs={{0,2},{1,3},{2,0},{3,1},{4,6},{5,7},{6,4},{7,5},{8,10},{9,11},{10,... | collective-permute-start | bytes 2359304 | tf_op jit(solution)/shard_map/ppermute | solution.py:112
  424.5 31.0 %collective-permute-start.61 = (bf16[3,256,768]{2,1,0:T(8,128)(2,1)S(1)}, bf16[3,256,768]{2,1,0:T(8,128)(2,1)}, u32[]{:S(2)}, u32[]{:S(2)}) collective-permute-start(bf16[3,256,768]{2,1,0:T(8,128)(2,1)S(1)} %collective-permute-done.59.piece), channel_id=1, source_target_pairs={{0,8},{8,16},{16,24},{24,28},{28,20},{20,12},{12,4},{4,0},{1,9},{9... | collective-permute-start | bytes 3538952 | tf_op jit(solution)/shard_map/ppermute | solution.py:119
  456.9 29.6 %collective-permute-start.63 = (bf16[3,256,768]{2,1,0:T(8,128)(2,1)}, bf16[3,256,768]{2,1,0:T(8,128)(2,1)S(1)}, u32[]{:S(2)}, u32[]{:S(2)}) collective-permute-start(bf16[3,256,768]{2,1,0:T(8,128)(2,1)} %collective-permute-done.61.piece), channel_id=1, source_target_pairs={{0,8},{8,16},{16,24},{24,28},{28,20},{20,12},{12,4},{4,0},{1,9},{9... | collective-permute-start | bytes 3538952 | tf_op jit(solution)/shard_map/ppermute | solution.py:119
  482.1 38.4 %collective-permute-start.65 = (bf16[3,256,768]{2,1,0:T(8,128)(2,1)}, bf16[3,256,768]{2,1,0:T(8,128)(2,1)}, u32[]{:S(2)}, u32[]{:S(2)}) collective-permute-start(bf16[3,256,768]{2,1,0:T(8,128)(2,1)} %collective-permute-done.64.piece), channel_id=1, source_target_pairs={{0,4},{8,0},{16,8},{24,16},{28,24},{20,28},{12,20},{4,12},{1,5},{9... | collective-permute-start | bytes 3538952 | tf_op jit(solution)/shard_map/ppermute | solution.py:119
  486.6 64.0 %collective-permute-start.72 = (bf16[3,256,768]{2,1,0:T(8,128)(2,1)S(1)}, bf16[3,256,768]{2,1,0:T(8,128)(2,1)}, u32[]{:S(2)}, u32[]{:S(2)}) collective-permute-start(bf16[3,256,768]{2,1,0:T(8,128)(2,1)S(1)} %collective-permute-done.63.piece), channel_id=1, source_target_pairs={{0,8},{8,16},{16,24},{24,28},{28,20},{20,12},{12,4},{4,0},{1,9},{9... | collective-permute-start | bytes 3538952 | tf_op jit(solution)/shard_map/ppermute | solution.py:119
  534.7 56.6 %collective-permute-start.71 = (bf16[3,256,768]{2,1,0:T(8,128)(2,1)}, bf16[3,256,768]{2,1,0:T(8,128)(2,1)S(1)}, u32[]{:S(2)}, u32[]{:S(2)}) collective-permute-start(bf16[3,256,768]{2,1,0:T(8,128)(2,1)} %collective-permute-done.65.piece), channel_id=1, source_target_pairs={{0,4},{8,0},{16,8},{24,16},{28,24},{20,28},{12,20},{4,12},{1,5},{9... | collective-permute-start | bytes 3538952 | tf_op jit(solution)/shard_map/ppermute | solution.py:119
  545.4 42.7 %collective-permute-start.70 = (f32[48,768]{1,0:T(8,128)S(1)}, f32[48,768]{1,0:T(8,128)S(1)}, u32[]{:S(2)}, u32[]{:S(2)}) collective-permute-start(f32[48,768]{1,0:T(8,128)S(1)} %add.282), channel_id=1, source_target_pairs={{0,2},{1,3},{2,0},{3,1},{4,6},{5,7},{6,4},{7,5},{8,10},{9,11},{10,... | collective-permute-start | bytes 442376 | tf_op jit(solution)/shard_map/ppermute | solution.py:823
  (109 other events, 1573.7 us)
Sparse Core Ops, SparseCore 0:
  491.7 92.8 all-reduce.1
